TPU v7x, 32 devices: a whole 2x2x4 slice. The times are simulated.
32 devices in a mesh: dev: 32 (over z, y, x, core).
Axes of the slice: x: 2, y: 2, z: 4, core: 2. Of those that a mesh axis runs over, the one named last changes fastest.
Arguments:
- field_in: float32 [32, 8, 128, 128], P(None, None, 'dev'), may hold values from -6 to 6
- source: float32 [32, 8, 128, 128], P(None, None, 'dev'), may hold values from -12 to 12
- cell_factor: float32 [8, 128, 128], P(None, 'dev'), may hold values from 0.5 to 2
- layer_material: int32 [8], replicated, may hold values from 0 to 3
- material_scale: float32 [4], replicated, may hold values from 0.25 to 4
- panel_cell: int32 [32768], P('dev'), may hold values from 0 to 16383
- panel_pos: float32 [3, 32768], replicated, may hold values from 0 to 1
- panel_area: float32 [32768], replicated, may hold values from 0.5 to 2
- flux_in: float32 [32, 32768], P(None, 'dev'), may hold values from -6 to 6
- pair_list: int32 [128, 2], P('dev'), may hold values from -1 to 15, as said below
Outputs:
- field_out: float32 [32, 8, 128, 128], P(None, None, 'dev')
- flux_out: float32 [32, 32768], P(None, 'dev')
Inputs may be any that keep to these rules, and one draw needn't show every extreme that they name: `pair_list`: each row is a tile pair (i, j) with i >= j, or (-1, -1) for an empty slot. No pair is listed twice. In each device's 4 rows the pairs come first, then the empty slots; at least a quarter of every device's slots are filled, and some device has all 4 filled.
All inputs are finite; a program needn't handle non-finite values.
Results may differ from a plain program's by a relative error of at most 0.0038.
Values may be sent and summed in bfloat16 or wider, within the bound.
No kernel may reach another device: no remote copies, remote signals or barrier semaphores. Data moves between devices by JAX's collectives and lax.ppermute only.
A program may use at most 192 MiB of HBM per device.

v0:
```python
import math

import jax
import jax.numpy as jnp
from jax import lax
from jax.sharding import PartitionSpec as P

TILE = 2048
PAN_DEV = 1024


softening = 0.0004
relax_rate = 0.8
update_rate = 0.5
kernel_gain = 0.25


def padded_2(array, sides, width):
    for axis, dim in sides:
        size, length = (lax.axis_size(axis), array.shape[dim])
        up = [(i, (i + 1) % size) for i in range(size - 1)]
        down = [(j, i) for i, j in up]
        last = lax.slice_in_dim(array, length - width, length, axis=dim)
        first = lax.slice_in_dim(array, 0, width, axis=dim)
        before = lax.ppermute(last, axis, up)
        after = lax.ppermute(first, axis, down)
        array = jnp.concatenate([before, array, after], axis=dim)
    return array


def coefficient(cell_factor, layer_material, material_scale):
    matched = (
        layer_material[:, None] == jnp.arange(material_scale.shape[0], dtype=jnp.int32)[None, :]
    )
    layer_scale = jnp.sum(jnp.where(matched, material_scale[None, :], 0.0), axis=1)
    return layer_scale[:, None, None] * cell_factor


def relax_rows(widened, source, conduct):
    centre = widened[:, :, 1:-1, :]
    padded = jnp.pad(centre, ((0, 0), (1, 1), (0, 0), (1, 1)))
    beside = (
        padded[:, 2:, :, 1:-1]
        + padded[:, :-2, :, 1:-1]
        + (widened[:, :, 2:, :] + widened[:, :, :-2, :])
        + (padded[:, 1:-1, :, 2:] + padded[:, 1:-1, :, :-2])
    )
    applied = conduct * (6.0 * centre - beside) + centre
    return centre + relax_rate * (source - applied) / (6.0 * conduct + 1.0)


def kernel_tile(row_pos, row_area, col_pos, col_area):
    delta_x = row_pos[0][:, None] - col_pos[0][None, :]
    delta_y = row_pos[1][:, None] - col_pos[1][None, :]
    delta_z = row_pos[2][:, None] - col_pos[2][None, :]
    distance = delta_x * delta_x + delta_y * delta_y + delta_z * delta_z
    weight = row_area[:, None] * col_area[None, :]
    return (weight * lax.rsqrt(distance + softening) * (kernel_gain / math.sqrt(TILE))).astype(
        jnp.bfloat16
    )


def body(
    field_in,
    source,
    cell_factor,
    layer_material,
    material_scale,
    panel_cell,
    panel_pos,
    panel_area,
    flux_in,
    pair_list,
):
    conduct = coefficient(cell_factor, layer_material, material_scale)
    load_count = field_in.shape[0]
    field_now = field_in
    for repeat in range(2):
        widened = padded_2(field_now, (("dev", 2),), 1)
        field_now = relax_rows(widened, source, conduct)
    surface_top = field_now[:, -1].astype(jnp.bfloat16)
    gathered = lax.all_gather(surface_top, "dev", axis=1, tiled=True)
    flattened = gathered.reshape(gathered.shape[0], -1)
    traces = jnp.take(flattened, panel_cell, axis=1)
    flux_half = lax.all_gather(flux_in.astype(jnp.bfloat16), "dev", axis=1, tiled=True)
    table_all = lax.all_gather(pair_list, "dev", axis=0, tiled=True)
    row_start = lax.axis_index("dev") * PAN_DEV
    own_tile = row_start // TILE
    num_tiles = flux_half.shape[1] // TILE
    tile_ids = jnp.arange(num_tiles, dtype=jnp.int32)
    upper_all = table_all[:, 0:1]
    lower_all = table_all[:, 1:2]
    linked = (upper_all == own_tile) & (lower_all == tile_ids[None, :]) | (
        lower_all == own_tile
    ) & (upper_all == tile_ids[None, :])
    active = jnp.any(linked, axis=0)
    anchor = jnp.int32(0)
    own_pos = lax.dynamic_slice(panel_pos, (anchor, row_start), (3, PAN_DEV))
    own_area = lax.dynamic_slice(panel_area, (row_start,), (PAN_DEV,))
    group_width = 4 * TILE

    def visit_group(group_index, totals):
        col_start = (group_index * group_width).astype(jnp.int32)
        live_tiles = lax.dynamic_slice(active, (group_index * 4,), (4,))

        def work(totals):
            kernel_block = kernel_tile(
                lax.dynamic_slice(panel_pos, (anchor, col_start), (3, group_width)),
                lax.dynamic_slice(panel_area, (col_start,), (group_width,)),
                own_pos,
                own_area,
            )
            gate_cols = jnp.repeat(live_tiles, TILE)
            group_flux = jnp.where(
                gate_cols[None, :],
                lax.dynamic_slice(flux_half, (anchor, col_start), (load_count, group_width)),
                jnp.zeros((), jnp.bfloat16),
            )
            return totals + jnp.dot(group_flux, kernel_block, preferred_element_type=jnp.float32)

        return lax.cond(jnp.any(live_tiles), work, lambda kept: kept, totals)

    potential = lax.fori_loop(
        0, num_tiles // 4, visit_group, jnp.zeros((load_count, PAN_DEV), jnp.float32)
    )
    flux_out = flux_in + update_rate * (traces.astype(jnp.float32) - potential)
    return (field_now, flux_out)


def solution(mesh):
    in_specs = (
        P(None, None, "dev", None),
        P(None, None, "dev", None),
        P(None, "dev", None),
        P(),
        P(),
        P("dev"),
        P(),
        P(),
        P(None, "dev"),
        P("dev", None),
    )
    out_specs = (P(None, None, "dev", None), P(None, "dev"))
    return jax.shard_map(body, mesh=mesh, in_specs=in_specs, out_specs=out_specs, check_vma=False)
```

profile of v0, /device:TPU:3, one launch (start us, length us, event | category | flops | bytes accessed | tf_op | source)
XLA Modules:
  0.0 234.8 jit_solution(6422417332679456347)
XLA Ops:
  7.3 1.4 copy.49
  8.7 2.6 %collective-permute-start = (f32[32,8,1,128]{3,0,1,2:T(8,128)S(1)}, f32[32,8,1,128]{3,0,1,2:T(8,128)S(1)}, u32[]{:S(2)}, u32[]{:S(2)}) collective-permute-start(f32[32,8,1,128]{3,0,1,2:T(8,128)S(1)} %get-tuple-element.228), channel_id=1, source_target_pairs={{1,0},{2,1},{3,2},{4,3},{5,4},{6,5},{7,6},{8,7},{9,8},{10,9},{11,1... | collective-permute-start | bytes 393224 | tf_op jit(solution)/shard_map/ppermute | solution.py:26
  11.3 3.9 %collective-permute-start.1 = (f32[32,8,1,128]{3,0,1,2:T(8,128)S(1)}, f32[32,8,1,128]{3,0,1,2:T(8,128)S(1)}, u32[]{:S(2)}, u32[]{:S(2)}) collective-permute-start(f32[32,8,1,128]{3,0,1,2:T(8,128)S(1)} %get-tuple-element.229), channel_id=1, source_target_pairs={{0,1},{1,2},{2,3},{3,4},{4,5},{5,6},{6,7},{7,8},{8,9},{9,10},{10,1... | collective-permute-start | bytes 393224 | tf_op jit(solution)/shard_map/ppermute | solution.py:25
  17.1 1.6 fusion.19
  18.8 3.7 %collective-permute-start.2 = (f32[32,8,1,128]{3,0,1,2:T(8,128)S(1)}, f32[32,8,1,128]{3,0,1,2:T(8,128)S(1)}, u32[]{:S(2)}, u32[]{:S(2)}) collective-permute-start(f32[32,8,1,128]{3,0,1,2:T(8,128)S(1)} %get-tuple-element.226), channel_id=1, source_target_pairs={{1,0},{2,1},{3,2},{4,3},{5,4},{6,5},{7,6},{8,7},{9,8},{10,9},{11,1... | collective-permute-start | bytes 393224 | tf_op jit(solution)/shard_map/ppermute | solution.py:26
  22.5 3.4 %collective-permute-start.3 = (f32[32,8,1,128]{3,0,1,2:T(8,128)S(1)}, f32[32,8,1,128]{3,0,1,2:T(8,128)S(1)}, u32[]{:S(2)}, u32[]{:S(2)}) collective-permute-start(f32[32,8,1,128]{3,0,1,2:T(8,128)S(1)} %get-tuple-element.227), channel_id=1, source_target_pairs={{0,1},{1,2},{2,3},{3,4},{4,5},{5,6},{6,7},{7,8},{8,9},{9,10},{10,1... | collective-permute-start | bytes 393224 | tf_op jit(solution)/shard_map/ppermute | solution.py:25
  30.9 39.4 %all-gather.1 = s32[32,4,2]{1,2,0:T(2,128)S(1)} all-gather(s32[1,4,2]{1,2,0:T(2,128)S(1)} %bitcast.35), channel_id=1, replica_groups=mesh['dev'=32] {'dev'}, dimensions={0}, use_global_device_ids=true | all-gather | bytes 1056 | tf_op jit(solution)/shard_map/all_gather | solution.py:86
  73.7 13.1 %all-gather.7.cloned.1.call-done = bf16[32,1,128,128]{3,0,1,2:T(8,128)(2,1)} async-done(((bf16[32,1,4,128]{3,0,1,2:T(8,128)(2,1)}), bf16[32,1,128,128]{3,0,1,2:T(8,128)(2,1)}) %all-gather.7.cloned.1.call-update) | async-done | bytes 1048592 | tf_op jit(solution)/shard_map/all_gather | solution.py:82
  86.8 4.6 %copy.51 = bf16[32,1,128,128]{0,3,2,1:T(8,128)(2,1)} copy(bf16[32,1,128,128]{3,0,1,2:T(8,128)(2,1)} %all-gather.7.cloned.1.call-done) | data formatting | bytes 2097152 | tf_op jit(solution)/shard_map/all_gather | solution.py:82
  91.4 5.6 %gather_fusion = bf16[1024,32]{1,0:T(8,128)(2,1)S(1)} fusion(bf16[32,16384]{0,1:T(8,128)(2,1)} %bitcast.27, s32[1024]{0:T(1024)S(1)} %fusion.40), kind=kCustom, calls=%fused_computation | custom fusion | bytes 135168 | tf_op jit(solution)/shard_map/jit(_take)/gather | solution.py:84
  97.0 48.4 %all-gather.5.cloned.1.call-done = bf16[32,32768]{1,0:T(8,128)(2,1)} async-done(((bf16[32,1024]{1,0:T(8,128)(2,1)}), bf16[32,32768]{1,0:T(8,128)(2,1)}) %all-gather.5.cloned.1.call-update) | async-done | bytes 2097168 | tf_op jit(solution)/shard_map/all_gather | solution.py:85
  145.5 81.1 %while.16 = (s32[]{:T(128)}, f32[32,1024]{1,0:T(8,128)S(1)}, pred[16]{0:T(512)(128)(4,1)S(1)}, bf16[32,32768]{1,0:T(8,128)(2,1)}, f32[32768]{0:T(1024)}, /*index...) while((s32[]{:T(128)}, f32[32,1024]{1,0:T(8,128)S(1)}, ...), condition=%wide.region_6.7_spmd, body=%wide.region_2.6_spmd.sunk | while | flops 646217728 | bytes 1253723 | solution.py:123
  147.1 18.8 %conditional.2 = (f32[32,1024]{1,0:T(8,128)S(1)}) conditional(s32[]{:T(128)} %convert_element_type.34, f32[32,1024]{1,0:T(8,128)S(1)} %get-tuple-element.300, (pred[4]{0:T(512)(128)(4,1)S(1)}, s32[]{:T(128)}, bf16[32,32768]{1,0:T(8,128)(2,1)}, f32[32768]{0:T(1024)}, f32[1024]{0:T(1024)S(1)}, /*index=5*/f32[3,32768]{1,0:T(4,128)}, ...), branch_computations={%region_4.4_spmd, %region_5.5_spmd} | conditional | flops 646217728 | bytes 1253478 | solution.py:121
  147.1 1.3 constant_dynamic-slice_fusion
  149.2 16.7 %fusion.1 = f32[32,1024]{1,0:T(8,128)S(1)} fusion(f32[32,1024]{1,0:T(8,128)S(1)} %get-tuple-element.171, f32[1024]{0:T(1024)S(1)} %bitcast.33, f32[8192]{0:T(1024)S(1)} %bitcast.30, f32[1024]{0:T(1024)S(1)} %bitcast.34, f32[8192]{0:T(1024)S(1)} %bitcast.29, f32[1024]{0:T(1024)S(1)} %bitcast.32, f32[8192]{0:T(1024)S(1)} %bitcast.28, ...), kind=kOutput, calls=%fused_computation.3 | convolution fusion | flops 646217728 | bytes 942084 | tf_op jit(solution)/shard_map/while/body/eval_jaxpr/cond/branch_1_fun/dot_general | solution.py:119
  167.3 18.8 %conditional.2 = (f32[32,1024]{1,0:T(8,128)S(1)}) conditional(s32[]{:T(128)} %convert_element_type.34, f32[32,1024]{1,0:T(8,128)S(1)} %get-tuple-element.300, (pred[4]{0:T(512)(128)(4,1)S(1)}, s32[]{:T(128)}, bf16[32,32768]{1,0:T(8,128)(2,1)}, f32[32768]{0:T(1024)}, f32[1024]{0:T(1024)S(1)}, /*index=5*/f32[3,32768]{1,0:T(4,128)}, ...), branch_computations={%region_4.4_spmd, %region_5.5_spmd} | conditional | flops 646217728 | bytes 1253478 | solution.py:121
  167.3 1.3 constant_dynamic-slice_fusion
  169.4 16.7 %fusion.1 = f32[32,1024]{1,0:T(8,128)S(1)} fusion(f32[32,1024]{1,0:T(8,128)S(1)} %get-tuple-element.171, f32[1024]{0:T(1024)S(1)} %bitcast.33, f32[8192]{0:T(1024)S(1)} %bitcast.30, f32[1024]{0:T(1024)S(1)} %bitcast.34, f32[8192]{0:T(1024)S(1)} %bitcast.29, f32[1024]{0:T(1024)S(1)} %bitcast.32, f32[8192]{0:T(1024)S(1)} %bitcast.28, ...), kind=kOutput, calls=%fused_computation.3 | convolution fusion | flops 646217728 | bytes 942084 | tf_op jit(solution)/shard_map/while/body/eval_jaxpr/cond/branch_1_fun/dot_general | solution.py:119
  187.5 18.9 %conditional.2 = (f32[32,1024]{1,0:T(8,128)S(1)}) conditional(s32[]{:T(128)} %convert_element_type.34, f32[32,1024]{1,0:T(8,128)S(1)} %get-tuple-element.300, (pred[4]{0:T(512)(128)(4,1)S(1)}, s32[]{:T(128)}, bf16[32,32768]{1,0:T(8,128)(2,1)}, f32[32768]{0:T(1024)}, f32[1024]{0:T(1024)S(1)}, /*index=5*/f32[3,32768]{1,0:T(4,128)}, ...), branch_computations={%region_4.4_spmd, %region_5.5_spmd} | conditional | flops 646217728 | bytes 1253478 | solution.py:121
  187.5 1.3 constant_dynamic-slice_fusion
  189.7 16.7 %fusion.1 = f32[32,1024]{1,0:T(8,128)S(1)} fusion(f32[32,1024]{1,0:T(8,128)S(1)} %get-tuple-element.171, f32[1024]{0:T(1024)S(1)} %bitcast.33, f32[8192]{0:T(1024)S(1)} %bitcast.30, f32[1024]{0:T(1024)S(1)} %bitcast.34, f32[8192]{0:T(1024)S(1)} %bitcast.29, f32[1024]{0:T(1024)S(1)} %bitcast.32, f32[8192]{0:T(1024)S(1)} %bitcast.28, ...), kind=kOutput, calls=%fused_computation.3 | convolution fusion | flops 646217728 | bytes 942084 | tf_op jit(solution)/shard_map/while/body/eval_jaxpr/cond/branch_1_fun/dot_general | solution.py:119
  207.8 18.8 %conditional.2 = (f32[32,1024]{1,0:T(8,128)S(1)}) conditional(s32[]{:T(128)} %convert_element_type.34, f32[32,1024]{1,0:T(8,128)S(1)} %get-tuple-element.300, (pred[4]{0:T(512)(128)(4,1)S(1)}, s32[]{:T(128)}, bf16[32,32768]{1,0:T(8,128)(2,1)}, f32[32768]{0:T(1024)}, f32[1024]{0:T(1024)S(1)}, /*index=5*/f32[3,32768]{1,0:T(4,128)}, ...), branch_computations={%region_4.4_spmd, %region_5.5_spmd} | conditional | flops 646217728 | bytes 1253478 | solution.py:121
  207.8 1.3 constant_dynamic-slice_fusion
  209.9 16.7 %fusion.1 = f32[32,1024]{1,0:T(8,128)S(1)} fusion(f32[32,1024]{1,0:T(8,128)S(1)} %get-tuple-element.171, f32[1024]{0:T(1024)S(1)} %bitcast.33, f32[8192]{0:T(1024)S(1)} %bitcast.30, f32[1024]{0:T(1024)S(1)} %bitcast.34, f32[8192]{0:T(1024)S(1)} %bitcast.29, f32[1024]{0:T(1024)S(1)} %bitcast.32, f32[8192]{0:T(1024)S(1)} %bitcast.28, ...), kind=kOutput, calls=%fused_computation.3 | convolution fusion | flops 646217728 | bytes 942084 | tf_op jit(solution)/shard_map/while/body/eval_jaxpr/cond/branch_1_fun/dot_general | solution.py:119
  (64 shorter events, 17.9 us)
Async XLA Ops:
  7.2 20.7 %copy-start = (f32[32,8,4,128]{3,2,1,0:T(4,128)S(1)}, f32[32,8,4,128]{3,2,1,0:T(4,128)}, u32[]{:S(2)}) copy-start(f32[32,8,4,128]{3,2,1,0:T(4,128)} %param.15) | copy-start | bytes 1572868
  7.2 22.0 %copy-start.2 = (f32[32,1024]{1,0:T(8,128)S(1)}, f32[32,1024]{1,0:T(8,128)}, u32[]{:S(2)}) copy-start(f32[32,1024]{1,0:T(8,128)} %param.22) | copy-start | bytes 393220
  7.2 23.8 %copy-start.5 = (s32[4,2]{0,1:T(2,128)S(1)}, s32[4,2]{0,1:T(2,128)}, u32[]{:S(2)}) copy-start(s32[4,2]{0,1:T(2,128)} %param.23) | copy-start | bytes 100
  7.2 64.8 %copy-start.3 = (s32[1024]{0:T(1024)S(1)}, s32[1024]{0:T(1024)}, u32[]{:S(2)}) copy-start(s32[1024]{0:T(1024)} %param.19) | copy-start | bytes 12292
  7.2 79.6 %all-gather.7.cloned.1.call-start = ((), (), s32[]{:S(2)}) async-start(), calls=%async_computation.1 | async-start | bytes 1081344 | tf_op jit(solution)/shard_map/all_gather | solution.py:82
  8.7 8.0 %collective-permute-start = (f32[32,8,1,128]{3,0,1,2:T(8,128)S(1)}, f32[32,8,1,128]{3,0,1,2:T(8,128)S(1)}, u32[]{:S(2)}, u32[]{:S(2)}) collective-permute-start(f32[32,8,1,128]{3,0,1,2:T(8,128)S(1)} %get-tuple-element.228), channel_id=1, source_target_pairs={{1,0},{2,1},{3,2},{4,3},{5,4},{6,5},{7,6},{8,7},{9,8},{10,9},{11,1... | collective-permute-start | bytes 393224 | tf_op jit(solution)/shard_map/ppermute | solution.py:26
  11.3 5.8 %collective-permute-start.1 = (f32[32,8,1,128]{3,0,1,2:T(8,128)S(1)}, f32[32,8,1,128]{3,0,1,2:T(8,128)S(1)}, u32[]{:S(2)}, u32[]{:S(2)}) collective-permute-start(f32[32,8,1,128]{3,0,1,2:T(8,128)S(1)} %get-tuple-element.229), channel_id=1, source_target_pairs={{0,1},{1,2},{2,3},{3,4},{4,5},{5,6},{6,7},{7,8},{8,9},{9,10},{10,1... | collective-permute-start | bytes 393224 | tf_op jit(solution)/shard_map/ppermute | solution.py:25
  18.8 7.9 %collective-permute-start.2 = (f32[32,8,1,128]{3,0,1,2:T(8,128)S(1)}, f32[32,8,1,128]{3,0,1,2:T(8,128)S(1)}, u32[]{:S(2)}, u32[]{:S(2)}) collective-permute-start(f32[32,8,1,128]{3,0,1,2:T(8,128)S(1)} %get-tuple-element.226), channel_id=1, source_target_pairs={{1,0},{2,1},{3,2},{4,3},{5,4},{6,5},{7,6},{8,7},{9,8},{10,9},{11,1... | collective-permute-start | bytes 393224 | tf_op jit(solution)/shard_map/ppermute | solution.py:26
  22.5 5.4 %collective-permute-start.3 = (f32[32,8,1,128]{3,0,1,2:T(8,128)S(1)}, f32[32,8,1,128]{3,0,1,2:T(8,128)S(1)}, u32[]{:S(2)}, u32[]{:S(2)}) collective-permute-start(f32[32,8,1,128]{3,0,1,2:T(8,128)S(1)} %get-tuple-element.227), channel_id=1, source_target_pairs={{0,1},{1,2},{2,3},{3,4},{4,5},{5,6},{6,7},{7,8},{8,9},{9,10},{10,1... | collective-permute-start | bytes 393224 | tf_op jit(solution)/shard_map/ppermute | solution.py:25
  29.2 116.3 %all-gather.5.cloned.1.call-start = ((), (), s32[]{:S(2)}) async-start(), calls=%async_computation | async-start | bytes 2162688 | tf_op jit(solution)/shard_map/all_gather | solution.py:85
  145.5 81.4 %copy-start.1 = (f32[32,1024]{0,1:T(8,128)S(1)}, f32[32,1024]{0,1:T(8,128)}, u32[]{:S(2)}) copy-start(f32[32,1024]{0,1:T(8,128)} %copy.54) | copy-start | bytes 393220
  145.5 81.4 %copy-start.4 = (pred[1024]{0:T(1024)(128)(4,1)S(1)}, pred[1024]{0:T(1024)(128)(4,1)}, u32[]{:S(2)}) copy-start(pred[1024]{0:T(1024)(128)(4,1)} %compare_and_fusion) | copy-start | bytes 3076
Sparse Core Ops, SparseCore 0:
  29.3 57.4 all-gather.6
  90.3 55.1 all-gather.4
where the time goes:
time: 237 us; the launch traced here: 235 us
  matrix products  66.8 us (28%)
  waiting for transfers between devices  63.9 us (27%)
  blocking collectives  39.4 us (17%)
  local copies, waits for them, and re-layouts  25.5 us (11%)
  between operations  14.3 us (6%)
  starting transfers between devices  13.7 us (6%)
  other arithmetic  8.25 us (3%)
  loops' own time  3.03 us (1%)
    dot_general x4, matrix products, work(): jnp.dot(group_flux, kernel_block, preferred_element_type=jnp.float32)  66.8 us
    all_gather x1, waiting for transfers between devices, body(): lax.all_gather(flux_in.astype(jnp.bfloat16), 'dev', axis=1, tiled=True)  48.4 us
    all_gather x1, blocking collectives, body(): table_all = lax.all_gather(pair_list, 'dev', axis=0, tiled=True)  39.4 us
    all_gather x1, waiting for transfers between devices, body(): gathered = lax.all_gather(surface_top, 'dev', axis=1, tiled=True)  13.1 us
    ppermute x2, starting transfers between devices, padded_2(): before = lax.ppermute(last, axis, up)  7.31 us
    ppermute x2, starting transfers between devices, padded_2(): after = lax.ppermute(first, axis, down)  6.32 us
    gather x1, local copies, waits for them, and re-layouts, body(): traces = jnp.take(flattened, panel_cell, axis=1)  5.6 us
    slice x8, local copies, waits for them, and re-layouts, kernel_tile(): delta_x = row_pos[0][:, None] - col_pos[0][None, :]  5.11 us
  transfers between devices with their start and end apart: 6, of which 5 were waited for; matrix products, arithmetic and copies ran while one was open for 7% of the time, Pallas kernels for 0%

commit v1 on v0

v1 whole, which is shorter than its diff:
```python
import math

import jax
import jax.numpy as jnp
from jax import lax
from jax.experimental import pallas as pl
from jax.experimental.pallas import tpu as pltpu
from jax.sharding import PartitionSpec as P

TILE = 2048

softening = 0.0004
relax_rate = 0.8
update_rate = 0.5
kernel_gain = 0.25

FEATURES = 32
PAIR_ROWS = 16
VMEM_LIMIT = 52 << 20

F32 = jnp.float32
BF16 = jnp.bfloat16


def vmem():
    return pl.BlockSpec(memory_space=pltpu.VMEM)


def smem():
    return pl.BlockSpec(memory_space=pltpu.SMEM)


def call(body, outs, ins, name, scratch=(), cost=None):
    return pl.pallas_call(
        body,
        out_shape=outs,
        in_specs=ins,
        out_specs=[vmem() for _ in outs],
        scratch_shapes=list(scratch),
        name=name,
        cost_estimate=cost,
        compiler_params=pltpu.CompilerParams(vmem_limit_bytes=VMEM_LIMIT),
    )


def halo_kernel(field, source, factor, up, down, *, rows, layers, width):
    lines = field.shape[0] // width

    def line(ref, x, count):
        return ref[pl.ds(x, count, stride=width), :].astype(BF16)

    for out, near, far, edge in (
        (up, width - 2, width - 1, width - 1),
        (down, 0, 1, 0),
    ):
        out[0:lines, :] = line(field, near, lines)
        out[lines : 2 * lines, :] = line(field, far, lines)
        out[2 * lines : 3 * lines, :] = line(source, edge, lines)
        tail = factor[pl.ds(edge, layers, stride=width), :]
        out[3 * lines : rows, :] = jnp.concatenate([tail, tail], axis=0).astype(BF16)


def relax_kernel(material, scale, field, source, factor, above, below, out, top, *, layers, width):
    lines = field.shape[0] // width
    loads = lines // layers
    ny = field.shape[1]
    depth = lax.broadcasted_iota(jnp.int32, (layers, ny), 0)
    lane = lax.broadcasted_iota(jnp.int32, (1, layers, ny), 2)
    level = lax.broadcasted_iota(jnp.int32, (1, layers, ny), 1)
    layer_scale = jnp.zeros((layers, ny), F32)
    for k in range(layers):
        layer_scale = jnp.where(depth == k, scale[material[k]], layer_scale)

    def cube(value):
        return value.reshape(loads, layers, ny)

    def own(ref, x):
        return cube(ref[pl.ds(x, lines, stride=width), :])

    def sent(ref, part):
        return cube(ref[part * lines : (part + 1) * lines, :].astype(F32))

    def sent_factor(ref):
        return ref[3 * lines : 3 * lines + 2 * layers, :].astype(F32)[0:layers]

    fields = {-2: sent(above, 0), -1: sent(above, 1), width: sent(below, 0), width + 1: sent(below, 1)}
    sources = {-1: sent(above, 2), width: sent(below, 2)}
    factors = {-1: sent_factor(above), width: sent_factor(below)}
    for x in range(width):
        fields[x] = own(field, x)
        sources[x] = own(source, x)
        factors[x] = factor[pl.ds(x, layers, stride=width), :]
    conducts = {x: (layer_scale * value)[None] for x, value in factors.items()}
    gains = {x: relax_rate / (6.0 * value + 1.0) for x, value in conducts.items()}

    def sweep(values, x):
        centre = values[x]
        over = jnp.where(level == layers - 1, 0.0, pltpu.roll(centre, layers - 1, 1))
        under = jnp.where(level == 0, 0.0, pltpu.roll(centre, 1, 1))
        right = jnp.where(lane == ny - 1, 0.0, pltpu.roll(centre, ny - 1, 2))
        left = jnp.where(lane == 0, 0.0, pltpu.roll(centre, 1, 2))
        beside = over + under + (values[x + 1] + values[x - 1]) + (right + left)
        applied = conducts[x] * (6.0 * centre - beside) + centre
        return centre + (sources[x] - applied) * gains[x]

    first = {x: sweep(fields, x) for x in range(-1, width + 1)}
    for x in range(width):
        out[pl.ds(x, lines, stride=width), :] = sweep(first, x).reshape(lines, ny)
    for x in range(width):
        rows = pl.ds((layers - 1) * width + x, loads, stride=layers * width)
        top[x * loads : (x + 1) * loads, :] = out[rows, :].astype(BF16)


def pieces(value):
    high = value.astype(BF16).astype(F32)
    rest = value - high
    middle = rest.astype(BF16).astype(F32)
    return high, middle, (rest - middle).astype(BF16).astype(F32)


def row_side(value):
    high, middle, low = pieces(value)
    return [high, high, middle, middle, high, low]


def col_side(value):
    high, middle, low = pieces(value)
    return [high, middle, high, middle, low, high]


def feature_kernel(pos, area, rows_out, cols_out, *, pan, blocks):
    me = lax.axis_index("dev")
    core = lax.rem(me, 2)

    def pick(ref, k, device):
        return ref[k : k + 1, pl.ds(pl.multiple_of(device * pan, pan), pan)]

    def gather(devices):
        lines = [jnp.concatenate([pick(pos, k, d) for d in devices], axis=0) - 0.5 for k in range(3)]
        return lines, jnp.concatenate([pick(area, 0, d) for d in devices], axis=0)

    (x, y, z), weight = gather([2 * g + core for g in range(blocks)])
    scale = 1.0 / (weight * weight)
    terms = [(x * x + y * y + z * z + softening) * scale, scale, x * scale, y * scale, z * scale]
    flat = [piece for term in terms for piece in row_side(term)]
    lanes = rows_out.shape[1]
    for j in range(pan // lanes):
        for f in range(FEATURES):
            start = (j * FEATURES + f) * blocks
            value = flat[f][:, j * lanes : (j + 1) * lanes] if f < len(flat) else jnp.zeros((blocks, lanes), F32)
            rows_out[start : start + blocks, :] = value

    constant = TILE / (kernel_gain * kernel_gain)
    for half, device in enumerate((me, me + 1 - 2 * core)):
        (x, y, z), weight = gather([device])
        scale = constant / (weight * weight)
        terms = [scale, (x * x + y * y + z * z) * scale, -2.0 * x * scale, -2.0 * y * scale, -2.0 * z * scale]
        flat = [piece for term in terms for piece in col_side(term)]
        flat += [jnp.zeros_like(x)] * (FEATURES - len(flat))
        cols_out[:, half * pan : (half + 1) * pan] = jnp.concatenate(flat, axis=0).astype(BF16)


def message_kernel(flux, pairs, partner, out, scratch, *, slots):
    loads, pan = flux.shape
    lanes = out.shape[1]
    for j in range(pan // lanes):
        out[j * loads : (j + 1) * loads, :] = flux[:, j * lanes : (j + 1) * lanes].astype(BF16)
    scratch[...] = jnp.full(scratch.shape, -2.0, F32)
    scratch[0:2, 0:slots] = pairs[...].astype(F32)
    scratch[2:4, 0:slots] = partner[...].astype(F32)
    out[pan // lanes * loads :, :] = scratch[...].astype(BF16)


def add_block(rows, cols, message, start, block, blocks, store, *, loads, pan, wide):
    lanes = message.shape[1]
    parts = [message[pl.ds(start + j * loads, loads), :] for j in range(pan // lanes)]
    flux = jnp.concatenate(parts, axis=1)
    strip = FEATURES * blocks
    parts = [rows[pl.ds(j * strip + block, FEATURES, stride=blocks), :] for j in range(pan // lanes)]
    features = jnp.concatenate(parts, axis=1).astype(BF16)
    for c in range(cols.shape[1] // wide):
        span = slice(c * wide, (c + 1) * wide)
        squared = lax.dot_general(
            features, cols[:, span], (((0,), (0,)), ((), ())), preferred_element_type=F32
        )
        kernel = lax.rsqrt(squared.astype(BF16))
        store(span, jnp.dot(flux, kernel, preferred_element_type=F32))


def near_kernel(rows, cols, *refs, masks, blocks, loads, pan):
    messages, out = refs[:-1], refs[-1]
    me = lax.axis_index("dev")
    for i, (message, mask) in enumerate(zip(messages, masks)):

        def store(span, value, i=i):
            out[i, :, span] = value

        block = lax.shift_right_logical(me ^ mask, 1)
        add_block(rows, cols, message, 0, block, blocks, store, loads=loads, pan=pan, wide=512)


def far_kernel(rows, cols, near, *refs, near_masks, stacks, blocks, loads, pan, size):
    count = len(near_masks)
    firsts, arrived, out = refs[:count], refs[count:-1], refs[-1]
    me = lax.axis_index("dev")
    own = lax.shift_right_logical(me, 1)
    info = size - PAIR_ROWS
    tables = [ref[info:size, :] for ref in firsts]
    for ref, masks in zip(arrived, stacks):
        tables += [ref[i * size + info : (i + 1) * size, :] for i in range(len(masks))]
    first = jnp.concatenate(tables, axis=0).astype(F32)
    total = first.shape[0]
    second = pltpu.roll(first, total - 1, 0)
    index = lax.broadcasted_iota(jnp.int32, first.shape, 0)
    paired = (index % PAIR_ROWS == 0) | (index % PAIR_ROWS == 2)
    mine = own.astype(F32)
    linked = paired & ((first == mine) | (second == mine))
    other = jnp.where(first == mine, second, first).astype(jnp.int32)
    words = []
    for w in range((blocks + 15) // 16):
        inside = linked & (other >= 16 * w) & (other < 16 * (w + 1))
        bit = jnp.left_shift(1, jnp.clip(other - 16 * w, 0, 15)).astype(F32)
        words.append(jnp.sum(jnp.where(inside, bit, 0.0)).astype(jnp.int32))

    def active(block):
        word = words[0]
        for w in range(1, len(words)):
            word = jnp.where(lax.shift_right_logical(block, 4) == w, words[w], word)
        return (lax.shift_right_logical(word, block & 15) & 1) != 0

    gate = [active(lax.shift_right_logical(me ^ mask, 1)).astype(F32) for mask in near_masks]
    out[...] = sum(near[i] * gate[i] for i in range(count))

    def store(span, value):
        out[:, span] += value

    for ref, masks in zip(arrived, stacks):

        @pl.loop(0, len(masks))
        def _(i, ref=ref, masks=masks):
            mask = jnp.int32(masks[0])
            for k in range(1, len(masks)):
                mask = jnp.where(i == k, masks[k], mask)
            block = lax.shift_right_logical(me ^ mask, 1)

            @pl.when(active(block))
            def _():
                start = pl.multiple_of(i * size, 16)
                add_block(rows, cols, ref, start, block, blocks, store, loads=loads, pan=pan, wide=512)


def trace_kernel(potential, cells, partner, *refs, groups, loads, width, pan, ny):
    arrived, outs, table = refs[: len(groups)], refs[len(groups) : -1], refs[-1]
    me = lax.axis_index("dev")
    base = 0
    owners = []
    for ref, masks in zip(arrived, groups):
        count = len(masks) * width * loads
        table[pl.ds(base, count), :] = ref[...].astype(F32)
        base += count
        owners += [me ^ mask for mask in masks]
    lanes = cells.shape[1]
    for half, (cell_ref, out) in enumerate(zip((cells, partner), outs)):
        for pb in range(pan // lanes):
            cell = jnp.broadcast_to(cell_ref[pb : pb + 1, :], (loads, lanes))
            line = lax.div(cell, ny)
            lane = cell - line * ny
            acc = jnp.zeros((loads, lanes), F32)
            for b, owner in enumerate(owners):
                for x in range(width):
                    start = (b * width + x) * loads
                    seen = jnp.take_along_axis(table[start : start + loads, :], lane, axis=1)
                    acc = jnp.where(line == owner * width + x, seen, acc)
            here = half * pan + pb * lanes
            out[:, pb * lanes : (pb + 1) * lanes] = update_rate * (acc - potential[:, here : here + lanes])


def groups_of(size):
    bits = [1 << b for b in range(1, size.bit_length() - 1)]
    low = len(bits) % 2
    split = [bits[i : i + 2] for i in range(low, len(bits), 2)]
    split = ([bits[:low]] if low else []) + split
    phases = []
    for pair in reversed(split):
        phases.append([pair[0]] if len(pair) == 1 else [pair[0], pair[1], pair[0] | pair[1]])
    return phases


def swap(array, mask, size):
    return lax.ppermute(array, "dev", [(i, i ^ mask) for i in range(size)])


def spread(array, phases, size):
    parts = [(array, [0])]
    for masks in phases:
        stack = parts[0][0] if len(parts) == 1 else jnp.concatenate([a for a, _ in parts], axis=0)
        held = [m for _, group in parts for m in group]
        parts = [*parts, *((swap(stack, mask, size), [mask ^ m for m in held]) for mask in masks)]
    return parts


def body(
    field_in,
    source,
    cell_factor,
    layer_material,
    material_scale,
    panel_cell,
    panel_pos,
    panel_area,
    flux_in,
    pair_list,
):
    size = lax.axis_size("dev")
    loads, layers, width, ny = field_in.shape
    pan = flux_in.shape[1]
    slots = pair_list.shape[0]
    blocks = size // 2
    lanes = 128
    lines = loads * layers
    phases = groups_of(size)

    cells = panel_cell.reshape(pan // lanes, lanes)
    pairs = pair_list.T
    partner_cells = swap(cells, 1, size)
    partner_pairs = swap(pairs, 1, size)

    field = field_in.reshape(lines * width, ny)
    load = source.reshape(lines * width, ny)
    factor = cell_factor.reshape(layers * width, ny)
    halo_rows = 3 * lines + 2 * layers
    halo = jax.ShapeDtypeStruct((halo_rows, ny), BF16)
    up, down = call(
        lambda *refs: halo_kernel(*refs, rows=halo_rows, layers=layers, width=width),
        [halo, halo],
        [vmem()] * 3,
        "halo",
    )(field, load, factor)
    above = lax.ppermute(up, "dev", [(i, i + 1) for i in range(size - 1)])
    below = lax.ppermute(down, "dev", [(i + 1, i) for i in range(size - 1)])

    rows, cols = call(
        lambda *refs: feature_kernel(*refs, pan=pan, blocks=blocks),
        [
            jax.ShapeDtypeStruct((pan // lanes * FEATURES * blocks, lanes), F32),
            jax.ShapeDtypeStruct((FEATURES, 2 * pan), BF16),
        ],
        [vmem()] * 2,
        "features",
    )(panel_pos, panel_area.reshape(1, -1))

    message_rows = pan // lanes * loads + PAIR_ROWS
    (message,) = call(
        lambda *refs: message_kernel(*refs, slots=slots),
        [jax.ShapeDtypeStruct((message_rows, lanes), BF16)],
        [vmem()] * 3,
        "message",
        scratch=[pltpu.VMEM((PAIR_ROWS, lanes), F32)],
    )(flux_in, pairs, partner_pairs)
    flux_parts = spread(message, phases, size)
    near_count = 1 + len(phases[0])
    near_parts, far_parts = flux_parts[:near_count], flux_parts[near_count:]

    field_out, top = call(
        lambda *refs: relax_kernel(*refs, layers=layers, width=width),
        [
            jax.ShapeDtypeStruct((lines * width, ny), F32),
            jax.ShapeDtypeStruct((width * loads, ny), BF16),
        ],
        [smem()] * 2 + [vmem()] * 5,
        "relax",
    )(layer_material, material_scale, field, load, factor, above, below)
    top_parts = spread(top, phases, size)

    near_masks = [masks[0] for _, masks in near_parts]
    (near,) = call(
        lambda *refs: near_kernel(*refs, masks=near_masks, blocks=blocks, loads=loads, pan=pan),
        [jax.ShapeDtypeStruct((near_count, loads, 2 * pan), F32)],
        [vmem()] * (2 + near_count),
        "near",
    )(rows, cols, *[a for a, _ in near_parts])
    (potential,) = call(
        lambda *refs: far_kernel(
            *refs,
            near_masks=near_masks,
            stacks=[masks for _, masks in far_parts],
            blocks=blocks,
            loads=loads,
            pan=pan,
            size=message_rows,
        ),
        [jax.ShapeDtypeStruct((loads, 2 * pan), F32)],
        [vmem()] * (3 + near_count + len(far_parts)),
        "far",
    )(rows, cols, near, *[a for a, _ in near_parts], *[a for a, _ in far_parts])

    half = jax.ShapeDtypeStruct((loads, pan), F32)
    kept, given = call(
        lambda *refs: trace_kernel(
            *refs,
            groups=[masks for _, masks in top_parts],
            loads=loads,
            width=width,
            pan=pan,
            ny=ny,
        ),
        [half, half],
        [vmem()] * (3 + len(top_parts)),
        "traces",
        scratch=[pltpu.VMEM((blocks * width * loads, ny), F32)],
    )(potential, cells, partner_cells, *[a for a, _ in top_parts])
    flux_out = flux_in + kept + swap(given, 1, size)
    return (field_out.reshape(field_in.shape), flux_out)


def solution(mesh):
    in_specs = (
        P(None, None, "dev", None),
        P(None, None, "dev", None),
        P(None, "dev", None),
        P(),
        P(),
        P("dev"),
        P(),
        P(),
        P(None, "dev"),
        P("dev", None),
    )
    out_specs = (P(None, None, "dev", None), P(None, "dev"))
    return jax.shard_map(body, mesh=mesh, in_specs=in_specs, out_specs=out_specs, check_vma=False)
```

time: 237 us -> 80.8 us (0.34); the launches traced: 235 us -> 81.7 us
  matrix products: 66.8 us -> 0 us
  waiting for transfers between devices: 63.9 us -> 9.43 us
  Pallas kernels: 0 us -> 41.2 us
  blocking collectives: 39.4 us -> 0 us
  local copies, waits for them, and re-layouts: 25.5 us -> 6.73 us
  between operations: 14.3 us -> 0.77 us
  starting transfers between devices: 13.7 us -> 22.9 us
  other arithmetic: 8.25 us -> 0.7 us
  loops' own time: 3.03 us -> 0 us
    dot_general x4 -> x0, matrix products: 66.8 us -> none  [work(): jnp.dot(group_flux, kernel_block, preferred_element_type=jnp.float32)]
    all_gather x2 -> x0, waiting for transfers between devices: 61.5 us -> none  [the longest x1 48.4 us: body(): lax.all_gather(flux_in.astype(jnp.bfloat16), 'dev', axis=1, tiled=True)]
    pallas_call x0 -> x7, Pallas kernels: none -> 41.2 us  [the longest x1 24.8 us: body(): call(lambda *refs: far_kernel(*refs, near_masks=near_masks, stacks=[masks...]
    all_gather x1 -> x0, blocking collectives: 39.4 us -> none  [body(): table_all = lax.all_gather(pair_list, 'dev', axis=0, tiled=True)]
    ppermute x4 -> x17, starting transfers between devices: 13.6 us -> 22.9 us  [the longest x15 16.7 us: swap(): return lax.ppermute(array, 'dev', [(i, i ^ mask) for i in range(size)])]
    ppermute x4 -> x17, waiting for transfers between devices: 2.28 us -> 9.43 us  [the longest x1 5.47 us: body(): below = lax.ppermute(down, 'dev', [(i + 1, i) for i in range(size - 1)])]
    slice x11 -> x0, local copies, waits for them, and re-layouts: 5.77 us -> none  [the longest x8 5.11 us: kernel_tile(): delta_x = row_pos[0][:, None] - col_pos[0][None, :]]
    gather x1 -> x0, local copies, waits for them, and re-layouts: 5.6 us -> none  [body(): traces = jnp.take(flattened, panel_cell, axis=1)]
  transfers between devices with their start and end apart: 6 -> 17, of which waited for: 5 -> 4; matrix products, arithmetic and copies ran while one was open for 7% -> 0% of each run, Pallas kernels for 0% -> 48%
where the time goes in v1:
time: 80.8 us; the launch traced here: 81.7 us
  Pallas kernels  41.2 us (51%)
  starting transfers between devices  22.9 us (28%)
  waiting for transfers between devices  9.43 us (12%)
  local copies, waits for them, and re-layouts  6.73 us (8%)
    pallas_call x1, Pallas kernels, body(): call(lambda *refs: far_kernel(*refs, near_masks=near_masks, stacks=[masks...  24.8 us
    ppermute x15, starting transfers between devices, swap(): return lax.ppermute(array, 'dev', [(i, i ^ mask) for i in range(size)])  16.7 us
    pallas_call x1, Pallas kernels, body(): call(lambda *refs: near_kernel(*refs, masks=near_masks, blocks=blocks, lo...  10 us
    unnamed x27, local copies, waits for them, and re-layouts  6.72 us
    ppermute x1, waiting for transfers between devices, body(): below = lax.ppermute(down, 'dev', [(i + 1, i) for i in range(size - 1)])  5.47 us
    ppermute x1, starting transfers between devices, body(): above = lax.ppermute(up, 'dev', [(i, i + 1) for i in range(size - 1)])  4.26 us
    ppermute x15, waiting for transfers between devices, swap(): return lax.ppermute(array, 'dev', [(i, i ^ mask) for i in range(size)])  3.96 us
    pallas_call x1, Pallas kernels, body(): call(lambda *refs: relax_kernel(*refs, layers=layers, width=width), [jax....  2.34 us
  transfers between devices with their start and end apart: 17, of which 4 were waited for; matrix products, arithmetic and copies ran while one was open for 0% of the time, Pallas kernels for 48%

profile of v1, /device:TPU:3, one launch (start us, length us, event | category | flops | bytes accessed | tf_op | source)
XLA Modules:
  0.0 81.7 jit_solution(5713446995171183647)
XLA Ops:
  0.6 0.7 collective-permute-start.2
  1.4 1.0 %collective-permute-done.2.refs_2_ = s32[2,4]{1,0:T(2,128)S(1)} collective-permute-done((s32[2,4]{1,0:T(2,128)}, s32[2,4]{1,0:T(2,128)S(1)}, u32[]{:S(2)}, u32[]{:S(2)}) %collective-permute-start.2) | collective-permute-done | bytes 64 | tf_op jit(solution)/shard_map/ppermute | solution.py:290
  2.4 0.9 %copy-done.4 = f32[32,1024]{1,0:T(8,128)S(1)} copy-done((f32[32,1024]{1,0:T(8,128)S(1)}, f32[32,1024]{1,0:T(8,128)}, u32[]{:S(2)}) %copy-start.4) | copy-done | bytes 131096
  4.0 1.4 %collective-permute-start.3 = (bf16[272,128]{1,0:T(8,128)(2,1)S(1)}, bf16[272,128]{1,0:T(8,128)(2,1)S(1)}, u32[]{:S(2)}, u32[]{:S(2)}) collective-permute-start(bf16[272,128]{1,0:T(8,128)(2,1)S(1)} %message.1.refs_2_.refs_3_), channel_id=1, source_target_pairs={{0,8},{1,9},{2,10},{3,11},{4,12},{5,13},{6,14},{7,15},{8,0},{9,1},... | collective-permute-start | bytes 208904 | tf_op jit(solution)/shard_map/ppermute | solution.py:290
  5.4 2.3 %collective-permute-start.4 = (bf16[272,128]{1,0:T(8,128)(2,1)S(1)}, bf16[272,128]{1,0:T(8,128)(2,1)S(1)}, u32[]{:S(2)}, u32[]{:S(2)}) collective-permute-start(bf16[272,128]{1,0:T(8,128)(2,1)S(1)} %message.1.refs_2_.refs_3_), channel_id=1, source_target_pairs={{0,16},{1,17},{2,18},{3,19},{4,20},{5,21},{6,22},{7,23},{8,24},{9,... | collective-permute-start | bytes 208904 | tf_op jit(solution)/shard_map/ppermute | solution.py:290
  7.7 1.0 %copy-done.1 = f32[32,8,4,128]{3,2,1,0:T(4,128)S(1)} copy-done((f32[32,8,4,128]{3,2,1,0:T(4,128)S(1)}, f32[32,8,4,128]{3,2,1,0:T(4,128)}, u32[]{:S(2)}) %copy-start.1) | copy-done | bytes 524312
  8.7 1.0 %copy-done.2 = f32[32,8,4,128]{3,2,1,0:T(4,128)S(1)} copy-done((f32[32,8,4,128]{3,2,1,0:T(4,128)S(1)}, f32[32,8,4,128]{3,2,1,0:T(4,128)}, u32[]{:S(2)}) %copy-start.2) | copy-done | bytes 524312
  10.5 4.3 %collective-permute-start = (bf16[784,128]{1,0:T(8,128)(2,1)S(1)}, bf16[784,128]{1,0:T(8,128)(2,1)S(1)}, u32[]{:S(2)}, u32[]{:S(2)}) collective-permute-start(bf16[784,128]{1,0:T(8,128)(2,1)S(1)} %get-tuple-element.10), channel_id=1, source_target_pairs={{0,1},{1,2},{2,3},{3,4},{4,5},{5,6},{6,7},{7,8},{8,9},{9,10},{10,1... | collective-permute-start | bytes 602120 | tf_op jit(solution)/shard_map/ppermute | solution.py:339
  14.8 1.9 %collective-permute-start.1 = (bf16[784,128]{1,0:T(8,128)(2,1)S(1)}, bf16[784,128]{1,0:T(8,128)(2,1)S(1)}, u32[]{:S(2)}, u32[]{:S(2)}) collective-permute-start(bf16[784,128]{1,0:T(8,128)(2,1)S(1)} %get-tuple-element.11), channel_id=1, source_target_pairs={{1,0},{2,1},{3,2},{4,3},{5,4},{6,5},{7,6},{8,7},{9,8},{10,9},{11,1... | collective-permute-start | bytes 602120 | tf_op jit(solution)/shard_map/ppermute | solution.py:340
  17.1 1.2 %collective-permute-start.7 = (bf16[1088,128]{1,0:T(8,128)(2,1)S(1)}, bf16[1088,128]{1,0:T(8,128)(2,1)S(1)}, u32[]{:S(2)}, u32[]{:S(2)}) collective-permute-start(bf16[1088,128]{1,0:T(8,128)(2,1)S(1)} %pad_maximum_fusion), channel_id=1, source_target_pairs={{0,4},{1,5},{2,6},{3,7},{4,0},{5,1},{6,2},{7,3},{8,12},{9,13},{10,... | collective-permute-start | bytes 835592 | tf_op jit(solution)/shard_map/ppermute | solution.py:290
  18.4 1.2 %collective-permute-start.8 = (bf16[1088,128]{1,0:T(8,128)(2,1)S(1)}, bf16[1088,128]{1,0:T(8,128)(2,1)S(1)}, u32[]{:S(2)}, u32[]{:S(2)}) collective-permute-start(bf16[1088,128]{1,0:T(8,128)(2,1)S(1)} %pad_maximum_fusion), channel_id=1, source_target_pairs={{0,6},{1,7},{2,4},{3,5},{4,2},{5,3},{6,0},{7,1},{8,14},{9,15},{10,... | collective-permute-start | bytes 835592 | tf_op jit(solution)/shard_map/ppermute | solution.py:290
  19.5 5.5 %collective-permute-done.1.refs_6_ = bf16[784,128]{1,0:T(8,128)(2,1)S(1)} collective-permute-done((bf16[784,128]{1,0:T(8,128)(2,1)S(1)}, bf16[784,128]{1,0:T(8,128)(2,1)S(1)}, u32[]{:S(2)}, u32[]{:S(2)}) %collective-permute-start.1) | collective-permute-done | bytes 200736 | tf_op jit(solution)/shard_map/ppermute | solution.py:340
  26.3 2.3 %relax.1 = (f32[1024,128]{1,0:T(8,128)}, bf16[128,128]{1,0:T(8,128)(2,1)S(1)}) custom-call(s32[8]{0:T(128)S(1)} %copy-done.10, f32[4]{0:T(128)S(1)} %copy-done.11, f32[1024,128]{1,0:T(8,128)S(1)} %bitcast.8, f32[1024,128]{1,0:T(8,128)S(1)} %bitcast.10, f32[32,128]{1,0:T(8,128)S(1)} %bitcast.13, bf16[784,128]{1,0:T(8,128)(2,1)S(1)} %collective-permute-done.refs_5_, ...), custom_call_target="tpu_custom_call" | custom-call | tf_op jit(solution)/shard_map/relax/pallas_call | solution.py:364
  28.9 3.3 %collective-permute-start.11 = (bf16[128,128]{1,0:T(8,128)(2,1)S(1)}, bf16[128,128]{1,0:T(8,128)(2,1)S(1)}, u32[]{:S(2)}, u32[]{:S(2)}) collective-permute-start(bf16[128,128]{1,0:T(8,128)(2,1)S(1)} %get-tuple-element.15.refs_3_), channel_id=1, source_target_pairs={{0,16},{1,17},{2,18},{3,19},{4,20},{5,21},{6,22},{7,23},{8,24},{9,... | collective-permute-start | bytes 98312 | tf_op jit(solution)/shard_map/ppermute | solution.py:290
  32.3 2.8 %collective-permute-start.12 = (bf16[128,128]{1,0:T(8,128)(2,1)S(1)}, bf16[128,128]{1,0:T(8,128)(2,1)S(1)}, u32[]{:S(2)}, u32[]{:S(2)}) collective-permute-start(bf16[128,128]{1,0:T(8,128)(2,1)S(1)} %get-tuple-element.15.refs_3_), channel_id=1, source_target_pairs={{0,24},{1,25},{2,26},{3,27},{4,28},{5,29},{6,30},{7,31},{8,16},{9,... | collective-permute-start | bytes 98312 | tf_op jit(solution)/shard_map/ppermute | solution.py:290
  35.1 1.8 %collective-permute-done.12.refs_6_ = bf16[128,128]{1,0:T(8,128)(2,1)S(1)} collective-permute-done((bf16[128,128]{1,0:T(8,128)(2,1)S(1)}, bf16[128,128]{1,0:T(8,128)(2,1)S(1)}, u32[]{:S(2)}, u32[]{:S(2)}) %collective-permute-start.12) | collective-permute-done | bytes 32800 | tf_op jit(solution)/shard_map/ppermute | solution.py:290
  36.8 0.8 collective-permute-start.14
  37.6 1.9 %collective-permute-start.15 = (bf16[512,128]{1,0:T(8,128)(2,1)S(1)}, bf16[512,128]{1,0:T(8,128)(2,1)S(1)}, u32[]{:S(2)}, u32[]{:S(2)}) collective-permute-start(bf16[512,128]{1,0:T(8,128)(2,1)S(1)} %constant_dynamic-update-slice_fusion), channel_id=1, source_target_pairs={{0,6},{1,7},{2,4},{3,5},{4,2},{5,3},{6,0},{7,1},{8,14},{9,15},{10,... | collective-permute-start | bytes 393224 | tf_op jit(solution)/shard_map/ppermute | solution.py:290
  39.8 1.7 %features.1 = (f32[4096,128]{1,0:T(8,128)}, bf16[32,2048]{1,0:T(8,128)(2,1)S(1)}) custom-call(f32[3,32768]{1,0:T(4,128)S(1)} %copy-done.3, f32[1,32768]{1,0:T(1,128)S(1)} %bitcast.11), custom_call_target="tpu_custom_call" | custom-call | tf_op jit(solution)/shard_map/features/pallas_call | solution.py:342
  41.5 10.0 %near.1.refs_2_ = f32[4,32,2048]{2,1,0:T(8,128)S(1)} custom-call(f32[4096,128]{1,0:T(8,128)} %get-tuple-element.13.refs_0_, bf16[32,2048]{1,0:T(8,128)(2,1)S(1)} %get-tuple-element.14.refs_1_, bf16[272,128]{1,0:T(8,128)(2,1)S(1)} %message.1.refs_2_.refs_3_, bf16[272,128]{1,0:T(8,128)(2,1)S(1)} %collective-permute-done.3.refs_3_.refs_4_, ...), custom_call_target="tpu_custom_call" | custom-call | tf_op jit(solution)/shard_map/near/pallas_call | solution.py:376
  51.5 1.0 %copy-done = f32[4,32,2048]{2,1,0:T(8,128)} copy-done((f32[4,32,2048]{2,1,0:T(8,128)}, f32[4,32,2048]{2,1,0:T(8,128)S(1)}, u32[]{:S(2)}) %copy-start) | copy-done | bytes 1048600
  52.5 24.8 %far.1.refs_0_ = f32[32,2048]{1,0:T(8,128)S(1)} custom-call(f32[4096,128]{1,0:T(8,128)} %get-tuple-element.13.refs_0_, bf16[32,2048]{1,0:T(8,128)(2,1)S(1)} %get-tuple-element.14.refs_1_, f32[4,32,2048]{2,1,0:T(8,128)} %copy-done, bf16[272,128]{1,0:T(8,128)(2,1)S(1)} %message.1.refs_2_.refs_3_, bf16[272,128]{1,0:T(8,128)(2,1)S(1)} %collective-permute-done.3.refs_3_.refs_4_, ...), custom_call_target="tpu_custom_call" | custom-call | tf_op jit(solution)/shard_map/far/pallas_call | solution.py:382
  77.3 2.3 %traces.1 = (f32[32,1024]{1,0:T(8,128)S(1)}, f32[32,1024]{1,0:T(8,128)S(1)}) custom-call(f32[32,2048]{1,0:T(8,128)S(1)} %far.1.refs_0_, s32[8,128]{1,0:T(8,128)S(1)} %bitcast.15, s32[8,128]{1,0:T(8,128)S(1)} %collective-permute-done.9.refs_2_, bf16[128,128]{1,0:T(8,128)(2,1)S(1)} %get-tuple-element.15.refs_3_, ...), custom_call_target="tpu_custom_call" | custom-call | tf_op jit(solution)/shard_map/traces/pallas_call | solution.py:398
  79.9 1.1 %collective-permute-done.16 = f32[32,1024]{1,0:T(8,128)S(1)} collective-permute-done((f32[32,1024]{1,0:T(8,128)S(1)}, f32[32,1024]{1,0:T(8,128)S(1)}, u32[]{:S(2)}, u32[]{:S(2)}) %collective-permute-start.16) | collective-permute-done | bytes 131104 | tf_op jit(solution)/shard_map/ppermute | solution.py:290
  (47 shorter events, 4.8 us)
Async XLA Ops:
  0.6 1.8 %collective-permute-start.2 = (s32[2,4]{1,0:T(2,128)}, s32[2,4]{1,0:T(2,128)S(1)}, u32[]{:S(2)}, u32[]{:S(2)}) collective-permute-start(s32[2,4]{1,0:T(2,128)} %bitcast.16), channel_id=1, source_target_pairs={{0,1},{1,0},{2,3},{3,2},{4,5},{5,4},{6,7},{7,6},{8,9},{9,8},{10,11... | collective-permute-start | bytes 104 | tf_op jit(solution)/shard_map/ppermute | solution.py:290
  4.0 35.5 %copy-start.8 = (s32[1024]{0:T(1024)S(1)}, s32[1024]{0:T(1024)}, u32[]{:S(2)}) copy-start(s32[1024]{0:T(1024)} %param.15) | copy-start | bytes 12292
  4.0 35.8 %copy-start.6 = (f32[32768]{0:T(1024)S(1)}, f32[32768]{0:T(1024)}, u32[]{:S(2)}) copy-start(f32[32768]{0:T(1024)} %param.17) | copy-start | bytes 393220
  4.0 12.7 %collective-permute-start.3 = (bf16[272,128]{1,0:T(8,128)(2,1)S(1)}, bf16[272,128]{1,0:T(8,128)(2,1)S(1)}, u32[]{:S(2)}, u32[]{:S(2)}) collective-permute-start(bf16[272,128]{1,0:T(8,128)(2,1)S(1)} %message.1.refs_2_.refs_3_), channel_id=1, source_target_pairs={{0,8},{1,9},{2,10},{3,11},{4,12},{5,13},{6,14},{7,15},{8,0},{9,1},... | collective-permute-start | bytes 208904 | tf_op jit(solution)/shard_map/ppermute | solution.py:290
  5.4 11.4 %collective-permute-start.4 = (bf16[272,128]{1,0:T(8,128)(2,1)S(1)}, bf16[272,128]{1,0:T(8,128)(2,1)S(1)}, u32[]{:S(2)}, u32[]{:S(2)}) collective-permute-start(bf16[272,128]{1,0:T(8,128)(2,1)S(1)} %message.1.refs_2_.refs_3_), channel_id=1, source_target_pairs={{0,16},{1,17},{2,18},{3,19},{4,20},{5,21},{6,22},{7,23},{8,24},{9,... | collective-permute-start | bytes 208904 | tf_op jit(solution)/shard_map/ppermute | solution.py:290
  7.7 9.1 %collective-permute-start.5 = (bf16[272,128]{1,0:T(8,128)(2,1)S(1)}, bf16[272,128]{1,0:T(8,128)(2,1)S(1)}, u32[]{:S(2)}, u32[]{:S(2)}) collective-permute-start(bf16[272,128]{1,0:T(8,128)(2,1)S(1)} %message.1.refs_2_.refs_3_), channel_id=1, source_target_pairs={{0,24},{1,25},{2,26},{3,27},{4,28},{5,29},{6,30},{7,31},{8,16},{9,... | collective-permute-start | bytes 208904 | tf_op jit(solution)/shard_map/ppermute | solution.py:290
  7.7 1.0 %copy-start.1 = (f32[32,8,4,128]{3,2,1,0:T(4,128)S(1)}, f32[32,8,4,128]{3,2,1,0:T(4,128)}, u32[]{:S(2)}) copy-start(f32[32,8,4,128]{3,2,1,0:T(4,128)} %param.10) | copy-start | bytes 1572868
  8.7 1.0 %copy-start.2 = (f32[32,8,4,128]{3,2,1,0:T(4,128)S(1)}, f32[32,8,4,128]{3,2,1,0:T(4,128)}, u32[]{:S(2)}) copy-start(f32[32,8,4,128]{3,2,1,0:T(4,128)} %param.11) | copy-start | bytes 1572868
  10.5 29.3 %copy-start.3 = (f32[3,32768]{1,0:T(4,128)S(1)}, f32[3,32768]{1,0:T(4,128)}, u32[]{:S(2)}) copy-start(f32[3,32768]{1,0:T(4,128)} %refs_0_.4) | copy-start | bytes 1179652
  10.5 9.0 %collective-permute-start = (bf16[784,128]{1,0:T(8,128)(2,1)S(1)}, bf16[784,128]{1,0:T(8,128)(2,1)S(1)}, u32[]{:S(2)}, u32[]{:S(2)}) collective-permute-start(bf16[784,128]{1,0:T(8,128)(2,1)S(1)} %get-tuple-element.10), channel_id=1, source_target_pairs={{0,1},{1,2},{2,3},{3,4},{4,5},{5,6},{6,7},{7,8},{8,9},{9,10},{10,1... | collective-permute-start | bytes 602120 | tf_op jit(solution)/shard_map/ppermute | solution.py:339
  14.8 10.2 %collective-permute-start.1 = (bf16[784,128]{1,0:T(8,128)(2,1)S(1)}, bf16[784,128]{1,0:T(8,128)(2,1)S(1)}, u32[]{:S(2)}, u32[]{:S(2)}) collective-permute-start(bf16[784,128]{1,0:T(8,128)(2,1)S(1)} %get-tuple-element.11), channel_id=1, source_target_pairs={{1,0},{2,1},{3,2},{4,3},{5,4},{6,5},{7,6},{8,7},{9,8},{10,9},{11,1... | collective-permute-start | bytes 602120 | tf_op jit(solution)/shard_map/ppermute | solution.py:340
  16.8 20.8 %collective-permute-start.6 = (bf16[1088,128]{1,0:T(8,128)(2,1)S(1)}, bf16[1088,128]{1,0:T(8,128)(2,1)S(1)}, u32[]{:S(2)}, u32[]{:S(2)}) collective-permute-start(bf16[1088,128]{1,0:T(8,128)(2,1)S(1)} %pad_maximum_fusion), channel_id=1, source_target_pairs={{0,2},{1,3},{2,0},{3,1},{4,6},{5,7},{6,4},{7,5},{8,10},{9,11},{10,... | collective-permute-start | bytes 835592 | tf_op jit(solution)/shard_map/ppermute | solution.py:290
  17.1 22.4 %collective-permute-start.7 = (bf16[1088,128]{1,0:T(8,128)(2,1)S(1)}, bf16[1088,128]{1,0:T(8,128)(2,1)S(1)}, u32[]{:S(2)}, u32[]{:S(2)}) collective-permute-start(bf16[1088,128]{1,0:T(8,128)(2,1)S(1)} %pad_maximum_fusion), channel_id=1, source_target_pairs={{0,4},{1,5},{2,6},{3,7},{4,0},{5,1},{6,2},{7,3},{8,12},{9,13},{10,... | collective-permute-start | bytes 835592 | tf_op jit(solution)/shard_map/ppermute | solution.py:290
  18.4 34.1 %collective-permute-start.8 = (bf16[1088,128]{1,0:T(8,128)(2,1)S(1)}, bf16[1088,128]{1,0:T(8,128)(2,1)S(1)}, u32[]{:S(2)}, u32[]{:S(2)}) collective-permute-start(bf16[1088,128]{1,0:T(8,128)(2,1)S(1)} %pad_maximum_fusion), channel_id=1, source_target_pairs={{0,6},{1,7},{2,4},{3,5},{4,2},{5,3},{6,0},{7,1},{8,14},{9,15},{10,... | collective-permute-start | bytes 835592 | tf_op jit(solution)/shard_map/ppermute | solution.py:290
  28.6 3.6 %collective-permute-start.10 = (bf16[128,128]{1,0:T(8,128)(2,1)S(1)}, bf16[128,128]{1,0:T(8,128)(2,1)S(1)}, u32[]{:S(2)}, u32[]{:S(2)}) collective-permute-start(bf16[128,128]{1,0:T(8,128)(2,1)S(1)} %get-tuple-element.15.refs_3_), channel_id=1, source_target_pairs={{0,8},{1,9},{2,10},{3,11},{4,12},{5,13},{6,14},{7,15},{8,0},{9,1},... | collective-permute-start | bytes 98312 | tf_op jit(solution)/shard_map/ppermute | solution.py:290
  28.9 6.1 %collective-permute-start.11 = (bf16[128,128]{1,0:T(8,128)(2,1)S(1)}, bf16[128,128]{1,0:T(8,128)(2,1)S(1)}, u32[]{:S(2)}, u32[]{:S(2)}) collective-permute-start(bf16[128,128]{1,0:T(8,128)(2,1)S(1)} %get-tuple-element.15.refs_3_), channel_id=1, source_target_pairs={{0,16},{1,17},{2,18},{3,19},{4,20},{5,21},{6,22},{7,23},{8,24},{9,... | collective-permute-start | bytes 98312 | tf_op jit(solution)/shard_map/ppermute | solution.py:290
  32.3 4.6 %collective-permute-start.12 = (bf16[128,128]{1,0:T(8,128)(2,1)S(1)}, bf16[128,128]{1,0:T(8,128)(2,1)S(1)}, u32[]{:S(2)}, u32[]{:S(2)}) collective-permute-start(bf16[128,128]{1,0:T(8,128)(2,1)S(1)} %get-tuple-element.15.refs_3_), channel_id=1, source_target_pairs={{0,24},{1,25},{2,26},{3,27},{4,28},{5,29},{6,30},{7,31},{8,16},{9,... | collective-permute-start | bytes 98312 | tf_op jit(solution)/shard_map/ppermute | solution.py:290
  36.8 40.4 %collective-permute-start.13 = (bf16[512,128]{1,0:T(8,128)(2,1)S(1)}, bf16[512,128]{1,0:T(8,128)(2,1)S(1)}, u32[]{:S(2)}, u32[]{:S(2)}) collective-permute-start(bf16[512,128]{1,0:T(8,128)(2,1)S(1)} %constant_dynamic-update-slice_fusion), channel_id=1, source_target_pairs={{0,2},{1,3},{2,0},{3,1},{4,6},{5,7},{6,4},{7,5},{8,10},{9,11},{10,... | collective-permute-start | bytes 393224 | tf_op jit(solution)/shard_map/ppermute | solution.py:290
  36.8 40.4 %collective-permute-start.14 = (bf16[512,128]{1,0:T(8,128)(2,1)S(1)}, bf16[512,128]{1,0:T(8,128)(2,1)S(1)}, u32[]{:S(2)}, u32[]{:S(2)}) collective-permute-start(bf16[512,128]{1,0:T(8,128)(2,1)S(1)} %constant_dynamic-update-slice_fusion), channel_id=1, source_target_pairs={{0,4},{1,5},{2,6},{3,7},{4,0},{5,1},{6,2},{7,3},{8,12},{9,13},{10,... | collective-permute-start | bytes 393224 | tf_op jit(solution)/shard_map/ppermute | solution.py:290
  37.6 39.7 %collective-permute-start.15 = (bf16[512,128]{1,0:T(8,128)(2,1)S(1)}, bf16[512,128]{1,0:T(8,128)(2,1)S(1)}, u32[]{:S(2)}, u32[]{:S(2)}) collective-permute-start(bf16[512,128]{1,0:T(8,128)(2,1)S(1)} %constant_dynamic-update-slice_fusion), channel_id=1, source_target_pairs={{0,6},{1,7},{2,4},{3,5},{4,2},{5,3},{6,0},{7,1},{8,14},{9,15},{10,... | collective-permute-start | bytes 393224 | tf_op jit(solution)/shard_map/ppermute | solution.py:290
  39.5 37.8 %collective-permute-start.9 = (s32[8,128]{1,0:T(8,128)S(1)}, s32[8,128]{1,0:T(8,128)S(1)}, u32[]{:S(2)}, u32[]{:S(2)}) collective-permute-start(s32[8,128]{1,0:T(8,128)S(1)} %bitcast.14), channel_id=1, source_target_pairs={{0,1},{1,0},{2,3},{3,2},{4,5},{5,4},{6,7},{7,6},{8,9},{9,8},{10,11... | collective-permute-start | bytes 12296 | tf_op jit(solution)/shard_map/ppermute | solution.py:290
  51.5 1.0 %copy-start = (f32[4,32,2048]{2,1,0:T(8,128)}, f32[4,32,2048]{2,1,0:T(8,128)S(1)}, u32[]{:S(2)}) copy-start(f32[4,32,2048]{2,1,0:T(8,128)S(1)} %near.1.refs_2_) | copy-start | bytes 3145732
  52.5 28.6 %copy-start.5 = (f32[32,1024]{1,0:T(8,128)S(1)}, f32[32,1024]{1,0:T(8,128)}, u32[]{:S(2)}) copy-start(f32[32,1024]{1,0:T(8,128)} %refs_0_.5) | copy-start | bytes 393220
  79.6 1.4 %collective-permute-start.16 = (f32[32,1024]{1,0:T(8,128)S(1)}, f32[32,1024]{1,0:T(8,128)S(1)}, u32[]{:S(2)}, u32[]{:S(2)}) collective-permute-start(f32[32,1024]{1,0:T(8,128)S(1)} %get-tuple-element.17), channel_id=1, source_target_pairs={{0,1},{1,0},{2,3},{3,2},{4,5},{5,4},{6,7},{7,6},{8,9},{9,8},{10,11... | collective-permute-start | bytes 393224 | tf_op jit(solution)/shard_map/ppermute | solution.py:290
  (5 other events, 3.6 us)

commit v2 on v1

--- a/solution.py
+++ b/solution.py
@@ -1,5 +1,3 @@
-import math
-
 import jax
 import jax.numpy as jnp
 from jax import lax
@@ -7,6 +5,7 @@
 from jax.experimental.pallas import tpu as pltpu
 from jax.sharding import PartitionSpec as P
 
+
 TILE = 2048
 
 softening = 0.0004
@@ -16,7 +15,7 @@
 
 FEATURES = 32
 PAIR_ROWS = 16
-VMEM_LIMIT = 52 << 20
+VMEM_LIMIT = 32 << 20
 
 F32 = jnp.float32
 BF16 = jnp.bfloat16
@@ -30,20 +29,43 @@
     return pl.BlockSpec(memory_space=pltpu.SMEM)
 
 
-def call(body, outs, ins, name, scratch=(), cost=None):
+def cost_of(count):
+    return pl.CostEstimate(flops=count * 2_500_000_000, bytes_accessed=count << 17, transcendentals=count << 21)
+
+
+def call(body, outs, ins, scratch=(), cost=None, out_specs=None, aliases=None):
     return pl.pallas_call(
         body,
         out_shape=outs,
         in_specs=ins,
-        out_specs=[vmem() for _ in outs],
+        out_specs=[vmem() for _ in outs] if out_specs is None else out_specs,
         scratch_shapes=list(scratch),
-        name=name,
         cost_estimate=cost,
+        input_output_aliases=aliases or {},
         compiler_params=pltpu.CompilerParams(vmem_limit_bytes=VMEM_LIMIT),
     )
 
 
-def halo_kernel(field, source, factor, up, down, *, rows, layers, width):
+def prepare_kernel(*refs, rows, layers, width):
+    count = 7
+    sources, results = refs[:count], refs[count:-2]
+    flux, sems = refs[-2:]
+    up, down, message, *held = results
+    field, source, factor, pairs, pos, area = held
+    places = [field, source, factor, flux, pairs, pos, area]
+    copies = [pltpu.make_async_copy(a, b, sems.at[i]) for i, (a, b) in enumerate(zip(sources, places))]
+    for copy in copies:
+        copy.start()
+    lanes = message.shape[1]
+    loads, pan = flux.shape
+    used = pan // lanes * loads
+    copies[3].wait()
+    for j in range(pan // lanes):
+        message[j * loads : (j + 1) * loads, :] = flux[:, j * lanes : (j + 1) * lanes].astype(BF16)
+    message[used:, :] = jnp.full((PAIR_ROWS, lanes), -2.0, BF16)
+    copies[0].wait()
+    copies[1].wait()
+    copies[2].wait()
     lines = field.shape[0] // width
 
     def line(ref, x, count):
@@ -58,6 +80,8 @@
         out[2 * lines : 3 * lines, :] = line(source, edge, lines)
         tail = factor[pl.ds(edge, layers, stride=width), :]
         out[3 * lines : rows, :] = jnp.concatenate([tail, tail], axis=0).astype(BF16)
+    for copy in copies[4:]:
+        copy.wait()
 
 
 def relax_kernel(material, scale, field, source, factor, above, below, out, top, *, layers, width):
@@ -128,7 +152,7 @@
     return [high, middle, high, middle, low, high]
 
 
-def feature_kernel(pos, area, rows_out, cols_out, *, pan, blocks):
+def feature_kernel(pos, area, rows_out, cols_out, strips, *, pan, blocks):
     me = lax.axis_index("dev")
     core = lax.rem(me, 2)
 
@@ -143,12 +167,17 @@
     scale = 1.0 / (weight * weight)
     terms = [(x * x + y * y + z * z + softening) * scale, scale, x * scale, y * scale, z * scale]
     flat = [piece for term in terms for piece in row_side(term)]
-    lanes = rows_out.shape[1]
+    lanes = strips.shape[1]
+    strip = FEATURES * blocks
     for j in range(pan // lanes):
         for f in range(FEATURES):
-            start = (j * FEATURES + f) * blocks
+            start = j * strip + f * blocks
             value = flat[f][:, j * lanes : (j + 1) * lanes] if f < len(flat) else jnp.zeros((blocks, lanes), F32)
-            rows_out[start : start + blocks, :] = value
+            strips[start : start + blocks, :] = value
+    for g in range(blocks):
+        for j in range(pan // lanes):
+            value = strips[pl.ds(j * strip + g, FEATURES, stride=blocks), :]
+            rows_out[g * FEATURES : (g + 1) * FEATURES, j * lanes : (j + 1) * lanes] = value.astype(BF16)
 
     constant = TILE / (kernel_gain * kernel_gain)
     for half, device in enumerate((me, me + 1 - 2 * core)):
@@ -160,24 +189,19 @@
         cols_out[:, half * pan : (half + 1) * pan] = jnp.concatenate(flat, axis=0).astype(BF16)
 
 
-def message_kernel(flux, pairs, partner, out, scratch, *, slots):
-    loads, pan = flux.shape
-    lanes = out.shape[1]
-    for j in range(pan // lanes):
-        out[j * loads : (j + 1) * loads, :] = flux[:, j * lanes : (j + 1) * lanes].astype(BF16)
+def message_kernel(message, pairs, partner, out, scratch):
+    slots = pairs.shape[1]
     scratch[...] = jnp.full(scratch.shape, -2.0, F32)
     scratch[0:2, 0:slots] = pairs[...].astype(F32)
-    scratch[2:4, 0:slots] = partner[...].astype(F32)
-    out[pan // lanes * loads :, :] = scratch[...].astype(BF16)
-
-
-def add_block(rows, cols, message, start, block, blocks, store, *, loads, pan, wide):
+    scratch[PAIR_ROWS // 2 : PAIR_ROWS // 2 + 2, 0:slots] = partner[...].astype(F32)
+    out[message.shape[0] - PAIR_ROWS :, :] = scratch[...].astype(BF16)
+
+
+def add_block(rows, cols, message, start, block, store, *, loads, pan, wide):
     lanes = message.shape[1]
     parts = [message[pl.ds(start + j * loads, loads), :] for j in range(pan // lanes)]
     flux = jnp.concatenate(parts, axis=1)
-    strip = FEATURES * blocks
-    parts = [rows[pl.ds(j * strip + block, FEATURES, stride=blocks), :] for j in range(pan // lanes)]
-    features = jnp.concatenate(parts, axis=1).astype(BF16)
+    features = rows[pl.ds(pl.multiple_of(block * FEATURES, FEATURES), FEATURES), :]
     for c in range(cols.shape[1] // wide):
         span = slice(c * wide, (c + 1) * wide)
         squared = lax.dot_general(
@@ -187,66 +211,81 @@
         store(span, jnp.dot(flux, kernel, preferred_element_type=F32))
 
 
-def near_kernel(rows, cols, *refs, masks, blocks, loads, pan):
-    messages, out = refs[:-1], refs[-1]
+def choose(values, i):
+    value = jnp.int32(values[0])
+    for k in range(1, len(values)):
+        value = jnp.where(i == k, values[k], value)
+    return value
+
+
+def near_kernel(rows, cols, stack, out, *, first, masks, loads, pan, size):
     me = lax.axis_index("dev")
-    for i, (message, mask) in enumerate(zip(messages, masks)):
-
-        def store(span, value, i=i):
+
+    @pl.loop(0, len(masks))
+    def _(i):
+        block = lax.shift_right_logical(me ^ choose(masks, i), 1)
+
+        def store(span, value):
             out[i, :, span] = value
 
-        block = lax.shift_right_logical(me ^ mask, 1)
-        add_block(rows, cols, message, 0, block, blocks, store, loads=loads, pan=pan, wide=512)
-
-
-def far_kernel(rows, cols, near, *refs, near_masks, stacks, blocks, loads, pan, size):
-    count = len(near_masks)
-    firsts, arrived, out = refs[:count], refs[count:-1], refs[-1]
+        start = pl.multiple_of((first + i) * size, 16)
+        add_block(rows, cols, stack, start, block, store, loads=loads, pan=pan, wide=512)
+
+
+def active(words, block):
+    word = words[0]
+    for w in range(1, words.shape[0]):
+        word = jnp.where(lax.shift_right_logical(block, 4) == w, words[w], word)
+    return (lax.shift_right_logical(word, block & 15) & 1) != 0
+
+
+def gate_kernel(*refs, near_masks, near_count, stacks, size):
+    nears, tables = refs[:near_count], refs[near_count:-2]
+    out, words = refs[-2:]
     me = lax.axis_index("dev")
     own = lax.shift_right_logical(me, 1)
     info = size - PAIR_ROWS
-    tables = [ref[info:size, :] for ref in firsts]
-    for ref, masks in zip(arrived, stacks):
-        tables += [ref[i * size + info : (i + 1) * size, :] for i in range(len(masks))]
-    first = jnp.concatenate(tables, axis=0).astype(F32)
+    first = []
+    for ref, masks in zip(tables, stacks):
+        first += [ref[i * size + info : (i + 1) * size, :] for i in range(len(masks))]
+    first = jnp.concatenate(first, axis=0).astype(F32)
     total = first.shape[0]
     second = pltpu.roll(first, total - 1, 0)
     index = lax.broadcasted_iota(jnp.int32, first.shape, 0)
-    paired = (index % PAIR_ROWS == 0) | (index % PAIR_ROWS == 2)
+    paired = index % (PAIR_ROWS // 2) == 0
     mine = own.astype(F32)
     linked = paired & ((first == mine) | (second == mine))
     other = jnp.where(first == mine, second, first).astype(jnp.int32)
-    words = []
-    for w in range((blocks + 15) // 16):
+    for w in range(words.shape[0]):
         inside = linked & (other >= 16 * w) & (other < 16 * (w + 1))
         bit = jnp.left_shift(1, jnp.clip(other - 16 * w, 0, 15)).astype(F32)
-        words.append(jnp.sum(jnp.where(inside, bit, 0.0)).astype(jnp.int32))
-
-    def active(block):
-        word = words[0]
-        for w in range(1, len(words)):
-            word = jnp.where(lax.shift_right_logical(block, 4) == w, words[w], word)
-        return (lax.shift_right_logical(word, block & 15) & 1) != 0
-
-    gate = [active(lax.shift_right_logical(me ^ mask, 1)).astype(F32) for mask in near_masks]
-    out[...] = sum(near[i] * gate[i] for i in range(count))
+        words[w] = jnp.sum(jnp.where(inside, bit, 0.0)).astype(jnp.int32)
+    total = None
+    i = 0
+    for ref in nears:
+        for k in range(ref.shape[0]):
+            gate = active(words, lax.shift_right_logical(me ^ near_masks[i], 1)).astype(F32)
+            value = ref[k] * gate
+            total = value if total is None else total + value
+            i += 1
+    out[...] = total
+
+
+def far_kernel(words, rows, cols, total, stack, out, *, masks, loads, pan, size):
+    me = lax.axis_index("dev")
+    out[...] = total[...]
 
     def store(span, value):
         out[:, span] += value
 
-    for ref, masks in zip(arrived, stacks):
-
-        @pl.loop(0, len(masks))
-        def _(i, ref=ref, masks=masks):
-            mask = jnp.int32(masks[0])
-            for k in range(1, len(masks)):
-                mask = jnp.where(i == k, masks[k], mask)
-            block = lax.shift_right_logical(me ^ mask, 1)
-
-            @pl.when(active(block))
-            def _():
-                start = pl.multiple_of(i * size, 16)
-                add_block(rows, cols, ref, start, block, blocks, store, loads=loads, pan=pan, wide=512)
+    @pl.loop(0, len(masks))
+    def _(i):
+        block = lax.shift_right_logical(me ^ choose(masks, i), 1)
+
+        @pl.when(active(words, block))
+        def _():
+            start = pl.multiple_of(i * size, 16)
+            add_block(rows, cols, stack, start, block, store, loads=loads, pan=pan, wide=512)
 
 
 def trace_kernel(potential, cells, partner, *refs, groups, loads, width, pan, ny):
@@ -295,11 +334,12 @@
     for masks in phases:
         stack = parts[0][0] if len(parts) == 1 else jnp.concatenate([a for a, _ in parts], axis=0)
         held = [m for _, group in parts for m in group]
-        parts = [*parts, *((swap(stack, mask, size), [mask ^ m for m in held]) for mask in masks)]
+        sent = [(swap(stack, mask, size), [mask ^ m for m in held]) for mask in masks]
+        parts = [*parts, *sent]
     return parts
 
 
-def body(
+def program(
     field_in,
     source,
     cell_factor,
@@ -314,7 +354,6 @@
     size = lax.axis_size("dev")
     loads, layers, width, ny = field_in.shape
     pan = flux_in.shape[1]
-    slots = pair_list.shape[0]
     blocks = size // 2
     lanes = 128
     lines = loads * layers
@@ -322,44 +361,52 @@
 
     cells = panel_cell.reshape(pan // lanes, lanes)
     pairs = pair_list.T
-    partner_cells = swap(cells, 1, size)
     partner_pairs = swap(pairs, 1, size)
 
-    field = field_in.reshape(lines * width, ny)
-    load = source.reshape(lines * width, ny)
-    factor = cell_factor.reshape(layers * width, ny)
     halo_rows = 3 * lines + 2 * layers
     halo = jax.ShapeDtypeStruct((halo_rows, ny), BF16)
-    up, down = call(
-        lambda *refs: halo_kernel(*refs, rows=halo_rows, layers=layers, width=width),
-        [halo, halo],
+    message_rows = pan // lanes * loads + PAIR_ROWS
+    wanted = (
+        field_in.reshape(lines * width, ny),
+        source.reshape(lines * width, ny),
+        cell_factor.reshape(layers * width, ny),
+        flux_in,
+        pairs,
+        panel_pos,
+        panel_area.reshape(1, -1),
+    )
+    shapes = [jax.ShapeDtypeStruct(a.shape, a.dtype) for a in wanted]
+    up, down, message, field, load, factor, pairs_here, pos, area = call(
+        lambda *refs: prepare_kernel(*refs, rows=halo_rows, layers=layers, width=width),
+        [halo, halo, jax.ShapeDtypeStruct((message_rows, lanes), BF16), *shapes[:3], *shapes[4:]],
+        [pl.BlockSpec(memory_space=pltpu.HBM)] * len(wanted),
+        scratch=[pltpu.VMEM(flux_in.shape, F32), pltpu.SemaphoreType.DMA((len(wanted),))],
+    )(*[pltpu.with_memory_space_constraint(a, pltpu.HBM) for a in wanted])
+    (message,) = call(
+        message_kernel,
+        [jax.ShapeDtypeStruct((message_rows, lanes), BF16)],
         [vmem()] * 3,
-        "halo",
-    )(field, load, factor)
+        scratch=[pltpu.VMEM((PAIR_ROWS, lanes), F32)],
+        aliases={0: 0},
+    )(message, pairs_here, partner_pairs)
+    flux_parts = spread(message, phases, size)
+    near_count = 1 + len(phases[0])
+    near_parts, far_parts = flux_parts[:near_count], flux_parts[near_count:]
+    near_stack = jnp.concatenate([a for a, _ in near_parts], axis=0)
+
     above = lax.ppermute(up, "dev", [(i, i + 1) for i in range(size - 1)])
     below = lax.ppermute(down, "dev", [(i + 1, i) for i in range(size - 1)])
+    partner_cells = swap(cells, 1, size)
 
     rows, cols = call(
         lambda *refs: feature_kernel(*refs, pan=pan, blocks=blocks),
         [
-            jax.ShapeDtypeStruct((pan // lanes * FEATURES * blocks, lanes), F32),
+            jax.ShapeDtypeStruct((FEATURES * blocks, pan), BF16),
             jax.ShapeDtypeStruct((FEATURES, 2 * pan), BF16),
         ],
         [vmem()] * 2,
-        "features",
-    )(panel_pos, panel_area.reshape(1, -1))
-
-    message_rows = pan // lanes * loads + PAIR_ROWS
-    (message,) = call(
-        lambda *refs: message_kernel(*refs, slots=slots),
-        [jax.ShapeDtypeStruct((message_rows, lanes), BF16)],
-        [vmem()] * 3,
-        "message",
-        scratch=[pltpu.VMEM((PAIR_ROWS, lanes), F32)],
-    )(flux_in, pairs, partner_pairs)
-    flux_parts = spread(message, phases, size)
-    near_count = 1 + len(phases[0])
-    near_parts, far_parts = flux_parts[:near_count], flux_parts[near_count:]
+        scratch=[pltpu.VMEM((pan // lanes * FEATURES * blocks, lanes), F32)],
+    )(pos, area)
 
     field_out, top = call(
         lambda *refs: relax_kernel(*refs, layers=layers, width=width),
@@ -368,31 +415,45 @@
             jax.ShapeDtypeStruct((width * loads, ny), BF16),
         ],
         [smem()] * 2 + [vmem()] * 5,
-        "relax",
     )(layer_material, material_scale, field, load, factor, above, below)
-    top_parts = spread(top, phases, size)
-
+    top_parts = spread(top, [[bit] for masks in phases for bit in masks[:2]], size)
+
+    wide = jax.ShapeDtypeStruct((loads, 2 * pan), F32)
     near_masks = [masks[0] for _, masks in near_parts]
-    (near,) = call(
-        lambda *refs: near_kernel(*refs, masks=near_masks, blocks=blocks, loads=loads, pan=pan),
-        [jax.ShapeDtypeStruct((near_count, loads, 2 * pan), F32)],
-        [vmem()] * (2 + near_count),
-        "near",
-    )(rows, cols, *[a for a, _ in near_parts])
-    (potential,) = call(
-        lambda *refs: far_kernel(
+    nears = []
+    first = 0
+    for count in (1, 1, near_count - 2):
+        masks = near_masks[first : first + count]
+        (near,) = call(
+            lambda *refs, first=first, masks=masks: near_kernel(
+                *refs, first=first, masks=masks, loads=loads, pan=pan, size=message_rows
+            ),
+            [jax.ShapeDtypeStruct((count, loads, 2 * pan), F32)],
+            [vmem()] * 3,
+            cost=cost_of(count),
+        )(rows, cols, near_stack)
+        nears.append(near)
+        first += count
+    potential, words = call(
+        lambda *refs: gate_kernel(
             *refs,
             near_masks=near_masks,
-            stacks=[masks for _, masks in far_parts],
-            blocks=blocks,
-            loads=loads,
-            pan=pan,
+            near_count=len(nears),
+            stacks=[masks for _, masks in flux_parts],
             size=message_rows,
         ),
-        [jax.ShapeDtypeStruct((loads, 2 * pan), F32)],
-        [vmem()] * (3 + near_count + len(far_parts)),
-        "far",
-    )(rows, cols, near, *[a for a, _ in near_parts], *[a for a, _ in far_parts])
+        [wide, jax.ShapeDtypeStruct(((blocks + 15) // 16,), jnp.int32)],
+        [vmem()] * (len(nears) + len(flux_parts)),
+        out_specs=[vmem(), smem()],
+    )(*nears, *[a for a, _ in flux_parts])
+    for stack, masks in far_parts:
+        (potential,) = call(
+            lambda *refs, masks=masks: far_kernel(*refs, masks=masks, loads=loads, pan=pan, size=message_rows),
+            [wide],
+            [smem()] + [vmem()] * 4,
+            cost=cost_of(len(masks)),
+            aliases={3: 0},
+        )(words, rows, cols, potential, stack)
 
     half = jax.ShapeDtypeStruct((loads, pan), F32)
     kept, given = call(
@@ -406,7 +467,6 @@
         ),
         [half, half],
         [vmem()] * (3 + len(top_parts)),
-        "traces",
         scratch=[pltpu.VMEM((blocks * width * loads, ny), F32)],
     )(potential, cells, partner_cells, *[a for a, _ in top_parts])
     flux_out = flux_in + kept + swap(given, 1, size)
@@ -427,4 +487,4 @@
         P("dev", None),
     )
     out_specs = (P(None, None, "dev", None), P(None, "dev"))
-    return jax.shard_map(body, mesh=mesh, in_specs=in_specs, out_specs=out_specs, check_vma=False)
+    return jax.shard_map(program, mesh=mesh, in_specs=in_specs, out_specs=out_specs, check_vma=False)

time: 80.8 us -> 75.5 us (0.934)
  the two profiles are of different devices: /device:TPU:3 before, /device:TPU:7 now
where the time goes in v2:
time: 75.5 us; the launch traced here: 75.2 us
  Pallas kernels  32.9 us (44%)
  starting transfers between devices  32.3 us (43%)
  waiting for transfers between devices  7.06 us (9%)
  local copies, waits for them, and re-layouts  1.34 us (2%)
  between operations  0.82 us (1%)
    ppermute x13, starting transfers between devices, swap(): return lax.ppermute(array, 'dev', [(i, i ^ mask) for i in range(size)])  27 us
    pallas_call x3, Pallas kernels, program(): call(lambda *refs, masks=masks: far_kernel(*refs, masks=masks, loads=load...  15.6 us
    pallas_call x3, Pallas kernels, program(): call(lambda *refs, first=first, masks=masks: near_kernel(*refs, first=fir...  8.9 us
    ppermute x13, waiting for transfers between devices, swap(): return lax.ppermute(array, 'dev', [(i, i ^ mask) for i in range(size)])  7.05 us
    ppermute x1, starting transfers between devices, program(): above = lax.ppermute(up, 'dev', [(i, i + 1) for i in range(size - 1)])  3.37 us
    pallas_call x1, Pallas kernels, program(): call(lambda *refs: trace_kernel(*refs, groups=[masks for _, masks in top_...  2.35 us
    pallas_call x1, Pallas kernels, program(): call(lambda *refs: relax_kernel(*refs, layers=layers, width=width), [jax....  2.34 us
    ppermute x1, starting transfers between devices, program(): below = lax.ppermute(down, 'dev', [(i + 1, i) for i in range(size - 1)])  1.92 us
  transfers between devices with their start and end apart: 15, of which 3 were waited for; matrix products, arithmetic and copies ran while one was open for 0% of the time, Pallas kernels for 41%

profile of v2, /device:TPU:7, one launch (start us, length us, event | category | flops | bytes accessed | tf_op | source)
XLA Modules:
  0.0 75.2 jit_solution(3616224606199910645)
XLA Ops:
  2.0 1.5 %shard_map.113 = (bf16[784,128]{1,0:T(8,128)(2,1)S(1)}, bf16[784,128]{1,0:T(8,128)(2,1)S(1)}, bf16[272,128]{1,0:T(8,128)(2,1)S(1)}, f32[1024,128]{1,0:T(8,128)S(...) custom-call(f32[1024,128]{1,0:T(8,128)} %bitcast.9, ...), custom_call_target="tpu_custom_call" | custom-call | tf_op jit(solution)/shard_map/pallas_call | solution.py:379
  3.5 3.4 %collective-permute-start.5 = (bf16[272,128]{1,0:T(8,128)(2,1)S(1)}, bf16[272,128]{1,0:T(8,128)(2,1)S(1)}, u32[]{:S(2)}, u32[]{:S(2)}) collective-permute-start(bf16[272,128]{1,0:T(8,128)(2,1)S(1)} %shard_map.116.refs_3_), channel_id=1, source_target_pairs={{0,24},{1,25},{2,26},{3,27},{4,28},{5,29},{6,30},{7,31},{8,16},{9,... | collective-permute-start | bytes 208904 | tf_op jit(solution)/shard_map/ppermute | solution.py:329
  7.3 3.4 %collective-permute-start = (bf16[784,128]{1,0:T(8,128)(2,1)S(1)}, bf16[784,128]{1,0:T(8,128)(2,1)S(1)}, u32[]{:S(2)}, u32[]{:S(2)}) collective-permute-start(bf16[784,128]{1,0:T(8,128)(2,1)S(1)} %get-tuple-element.22), channel_id=1, source_target_pairs={{0,1},{1,2},{2,3},{3,4},{4,5},{5,6},{6,7},{7,8},{8,9},{9,10},{10,1... | collective-permute-start | bytes 602120 | tf_op jit(solution)/shard_map/ppermute | solution.py:397
  10.7 1.9 %collective-permute-start.1 = (bf16[784,128]{1,0:T(8,128)(2,1)S(1)}, bf16[784,128]{1,0:T(8,128)(2,1)S(1)}, u32[]{:S(2)}, u32[]{:S(2)}) collective-permute-start(bf16[784,128]{1,0:T(8,128)(2,1)S(1)} %get-tuple-element.23), channel_id=1, source_target_pairs={{1,0},{2,1},{3,2},{4,3},{5,4},{6,5},{7,6},{8,7},{9,8},{10,9},{11,1... | collective-permute-start | bytes 602120 | tf_op jit(solution)/shard_map/ppermute | solution.py:398
  12.6 1.5 %shard_map.115 = (bf16[512,1024]{1,0:T(8,128)(2,1)S(1)}, bf16[32,2048]{1,0:T(8,128)(2,1)S(1)}) custom-call(f32[3,32768]{1,0:T(4,128)S(1)} %get-tuple-element.25.refs_0_, f32[1,32768]{1,0:T(1,128)S(1)} %get-tuple-element.26.refs_1_), custom_call_target="tpu_custom_call" | custom-call | tf_op jit(solution)/shard_map/pallas_call | solution.py:401
  14.1 1.0 %collective-permute-start.9 = (s32[8,128]{1,0:T(8,128)S(1)}, s32[8,128]{1,0:T(8,128)S(1)}, u32[]{:S(2)}, u32[]{:S(2)}) collective-permute-start(s32[8,128]{1,0:T(8,128)S(1)} %bitcast.7), channel_id=1, source_target_pairs={{0,1},{1,0},{2,3},{3,2},{4,5},{5,4},{6,7},{7,6},{8,9},{9,8},{10,11... | collective-permute-start | bytes 12296 | tf_op jit(solution)/shard_map/ppermute | solution.py:329
  15.2 4.5 %shard_map.119.refs_2_ = f32[2,32,2048]{2,1,0:T(8,128)S(1)} custom-call(bf16[512,1024]{1,0:T(8,128)(2,1)S(1)} %get-tuple-element.27.refs_0_.refs_1_, bf16[32,2048]{1,0:T(8,128)(2,1)S(1)} %get-tuple-element.28.refs_1_.refs_2_, bf16[1088,128]{1,0:T(8,128)(2,1)S(1)} %pad_maximum_fusion.refs_2_), custom_call_target="tpu_custom_call" | custom-call | flops 5000000000 | bytes 262144 | tf_op jit(solution)/shard_map/pallas_call | solution.py:427
  20.3 2.3 %shard_map.114 = (f32[1024,128]{1,0:T(8,128)}, bf16[128,128]{1,0:T(8,128)(2,1)S(1)}) custom-call(s32[8]{0:T(128)S(1)} %copy-done.1, f32[4]{0:T(128)S(1)} %copy-done.2, f32[1024,128]{1,0:T(8,128)S(1)} %get-tuple-element.19.refs_2_, f32[1024,128]{1,0:T(8,128)S(1)} %get-tuple-element.20.refs_3_, f32[32,128]{1,0:T(8,128)S(1)} %get-tuple-element.21.refs_4_, ...), custom_call_target="tpu_custom_call" | custom-call | tf_op jit(solution)/shard_map/pallas_call | solution.py:411
  22.7 1.0 %collective-permute-start.10 = (bf16[128,128]{1,0:T(8,128)(2,1)S(1)}, bf16[128,128]{1,0:T(8,128)(2,1)S(1)}, u32[]{:S(2)}, u32[]{:S(2)}) collective-permute-start(bf16[128,128]{1,0:T(8,128)(2,1)S(1)} %get-tuple-element.33.refs_3_), channel_id=1, source_target_pairs={{0,8},{1,9},{2,10},{3,11},{4,12},{5,13},{6,14},{7,15},{8,0},{9,1},... | collective-permute-start | bytes 98312 | tf_op jit(solution)/shard_map/ppermute | solution.py:329
  23.7 2.2 %shard_map.117.refs_0_ = f32[1,32,2048]{2,1,0:T(8,128)S(1)} custom-call(bf16[512,1024]{1,0:T(8,128)(2,1)S(1)} %get-tuple-element.27.refs_0_.refs_1_, bf16[32,2048]{1,0:T(8,128)(2,1)S(1)} %get-tuple-element.28.refs_1_.refs_2_, bf16[1088,128]{1,0:T(8,128)(2,1)S(1)} %pad_maximum_fusion.refs_2_), custom_call_target="tpu_custom_call" | custom-call | flops 2500000000 | bytes 131072 | tf_op jit(solution)/shard_map/pallas_call | solution.py:427
  25.9 1.1 %collective-permute-start.6 = (bf16[1088,128]{1,0:T(8,128)(2,1)S(1)}, bf16[1088,128]{1,0:T(8,128)(2,1)S(1)}, u32[]{:S(2)}, u32[]{:S(2)}) collective-permute-start(bf16[1088,128]{1,0:T(8,128)(2,1)S(1)} %pad_maximum_fusion.refs_2_), channel_id=1, source_target_pairs={{0,2},{1,3},{2,0},{3,1},{4,6},{5,7},{6,4},{7,5},{8,10},{9,11},{10,... | collective-permute-start | bytes 835592 | tf_op jit(solution)/shard_map/ppermute | solution.py:329
  27.0 1.1 %collective-permute-start.7 = (bf16[1088,128]{1,0:T(8,128)(2,1)S(1)}, bf16[1088,128]{1,0:T(8,128)(2,1)S(1)}, u32[]{:S(2)}, u32[]{:S(2)}) collective-permute-start(bf16[1088,128]{1,0:T(8,128)(2,1)S(1)} %pad_maximum_fusion.refs_2_), channel_id=1, source_target_pairs={{0,4},{1,5},{2,6},{3,7},{4,0},{5,1},{6,2},{7,3},{8,12},{9,13},{10,... | collective-permute-start | bytes 835592 | tf_op jit(solution)/shard_map/ppermute | solution.py:329
  28.6 2.6 %collective-permute-start.11 = (bf16[256,128]{1,0:T(8,128)(2,1)S(1)}, bf16[256,128]{1,0:T(8,128)(2,1)S(1)}, u32[]{:S(2)}, u32[]{:S(2)}) collective-permute-start(bf16[256,128]{1,0:T(8,128)(2,1)S(1)} %pad_maximum_fusion.3), channel_id=1, source_target_pairs={{0,16},{1,17},{2,18},{3,19},{4,20},{5,21},{6,22},{7,23},{8,24},{9,... | collective-permute-start | bytes 196616 | tf_op jit(solution)/shard_map/ppermute | solution.py:329
  31.2 2.2 %shard_map.118.refs_1_ = f32[1,32,2048]{2,1,0:T(8,128)S(1)} custom-call(bf16[512,1024]{1,0:T(8,128)(2,1)S(1)} %get-tuple-element.27.refs_0_.refs_1_, bf16[32,2048]{1,0:T(8,128)(2,1)S(1)} %get-tuple-element.28.refs_1_.refs_2_, bf16[1088,128]{1,0:T(8,128)(2,1)S(1)} %pad_maximum_fusion.refs_2_), custom_call_target="tpu_custom_call" | custom-call | flops 2500000000 | bytes 131072 | tf_op jit(solution)/shard_map/pallas_call | solution.py:427
  34.0 1.1 %collective-permute-start.12 = (bf16[512,128]{1,0:T(8,128)(2,1)S(1)}, bf16[512,128]{1,0:T(8,128)(2,1)S(1)}, u32[]{:S(2)}, u32[]{:S(2)}) collective-permute-start(bf16[512,128]{1,0:T(8,128)(2,1)S(1)} %pad_maximum_fusion.2), channel_id=1, source_target_pairs={{0,2},{1,3},{2,0},{3,1},{4,6},{5,7},{6,4},{7,5},{8,10},{9,11},{10,... | collective-permute-start | bytes 393224 | tf_op jit(solution)/shard_map/ppermute | solution.py:329
  35.1 5.5 %collective-permute-done.8.refs_9_.refs_4_ = bf16[1088,128]{1,0:T(8,128)(2,1)S(1)} collective-permute-done((bf16[1088,128]{1,0:T(8,128)(2,1)S(1)}, bf16[1088,128]{1,0:T(8,128)(2,1)S(1)}, u32[]{:S(2)}, u32[]{:S(2)}) %collective-permute-start.8) | collective-permute-done | bytes 278560 | tf_op jit(solution)/shard_map/ppermute | solution.py:329
  40.6 0.7 shard_map.120
  41.3 2.9 %shard_map.121.refs_3_ = f32[32,2048]{1,0:T(8,128)S(1)} custom-call(s32[1]{0:T(128)} %get-tuple-element.31.refs_0_, bf16[512,1024]{1,0:T(8,128)(2,1)S(1)} %get-tuple-element.27.refs_0_.refs_1_, bf16[32,2048]{1,0:T(8,128)(2,1)S(1)} %get-tuple-element.28.refs_1_.refs_2_, f32[32,2048]{1,0:T(8,128)S(1)} %get-tuple-element.32.refs_3_, ...), custom_call_target="tpu_custom_call", output_to_operand_aliasing={{}: (3, {})} | custom-call | flops 10000000000 | bytes 524288 | tf_op jit(solution)/shard_map/pallas_call | solution.py:450
  44.3 5.2 %shard_map.122.refs_3_ = f32[32,2048]{1,0:T(8,128)S(1)} custom-call(s32[1]{0:T(128)} %get-tuple-element.31.refs_0_, bf16[512,1024]{1,0:T(8,128)(2,1)S(1)} %get-tuple-element.27.refs_0_.refs_1_, bf16[32,2048]{1,0:T(8,128)(2,1)S(1)} %get-tuple-element.28.refs_1_.refs_2_, f32[32,2048]{1,0:T(8,128)S(1)} %shard_map.121.refs_3_, ...), custom_call_target="tpu_custom_call", output_to_operand_aliasing={{}: (3, {})} | custom-call | flops 10000000000 | bytes 524288 | tf_op jit(solution)/shard_map/pallas_call | solution.py:450
  49.5 11.7 %collective-permute-start.13 = (bf16[1024,128]{1,0:T(8,128)(2,1)S(1)}, bf16[1024,128]{1,0:T(8,128)(2,1)S(1)}, u32[]{:S(2)}, u32[]{:S(2)}) collective-permute-start(bf16[1024,128]{1,0:T(8,128)(2,1)S(1)} %pad_maximum_fusion.1), channel_id=1, source_target_pairs={{0,4},{1,5},{2,6},{3,7},{4,0},{5,1},{6,2},{7,3},{8,12},{9,13},{10,... | collective-permute-start | bytes 786440 | tf_op jit(solution)/shard_map/ppermute | solution.py:329
  61.2 7.6 %shard_map.123.refs_0_ = f32[32,2048]{1,0:T(8,128)S(1)} custom-call(s32[1]{0:T(128)} %get-tuple-element.31.refs_0_, bf16[512,1024]{1,0:T(8,128)(2,1)S(1)} %get-tuple-element.27.refs_0_.refs_1_, bf16[32,2048]{1,0:T(8,128)(2,1)S(1)} %get-tuple-element.28.refs_1_.refs_2_, f32[32,2048]{1,0:T(8,128)S(1)} %shard_map.122.refs_3_, ...), custom_call_target="tpu_custom_call", output_to_operand_aliasing={{}: (3, {})} | custom-call | flops 10000000000 | bytes 524288 | tf_op jit(solution)/shard_map/pallas_call | solution.py:450
  68.8 2.3 %shard_map.124 = (f32[32,1024]{1,0:T(8,128)S(1)}, f32[32,1024]{1,0:T(8,128)S(1)}) custom-call(f32[32,2048]{1,0:T(8,128)S(1)} %shard_map.123.refs_0_, s32[8,128]{1,0:T(8,128)S(1)} %bitcast.8, s32[8,128]{1,0:T(8,128)S(1)} %collective-permute-done.9.refs_2_, bf16[128,128]{1,0:T(8,128)(2,1)S(1)} %get-tuple-element.33.refs_3_, ...), custom_call_target="tpu_custom_call" | custom-call | tf_op jit(solution)/shard_map/pallas_call | solution.py:459
  71.1 2.4 %collective-permute-start.14 = (f32[32,1024]{1,0:T(8,128)S(1)}, f32[32,1024]{1,0:T(8,128)S(1)}, u32[]{:S(2)}, u32[]{:S(2)}) collective-permute-start(f32[32,1024]{1,0:T(8,128)S(1)} %get-tuple-element.35), channel_id=1, source_target_pairs={{0,1},{1,0},{2,3},{3,2},{4,5},{5,4},{6,7},{7,6},{8,9},{9,8},{10,11... | collective-permute-start | bytes 393224 | tf_op jit(solution)/shard_map/ppermute | solution.py:329
  73.6 1.0 %collective-permute-done.14 = f32[32,1024]{1,0:T(8,128)S(1)} collective-permute-done((f32[32,1024]{1,0:T(8,128)S(1)}, f32[32,1024]{1,0:T(8,128)S(1)}, u32[]{:S(2)}, u32[]{:S(2)}) %collective-permute-start.14) | collective-permute-done | bytes 131104 | tf_op jit(solution)/shard_map/ppermute | solution.py:329
  (33 shorter events, 4.1 us)
Async XLA Ops:
  0.6 0.7 copy-start.4
  1.3 2.2 %collective-permute-start.2 = (s32[2,4]{1,0:T(2,128)S(1)}, s32[2,4]{1,0:T(2,128)S(1)}, u32[]{:S(2)}, u32[]{:S(2)}) collective-permute-start(s32[2,4]{1,0:T(2,128)S(1)} %bitcast.14), channel_id=1, source_target_pairs={{0,1},{1,0},{2,3},{3,2},{4,5},{5,4},{6,7},{7,6},{8,9},{9,8},{10,11... | collective-permute-start | bytes 104 | tf_op jit(solution)/shard_map/ppermute | solution.py:329
  3.5 10.5 %collective-permute-start.5 = (bf16[272,128]{1,0:T(8,128)(2,1)S(1)}, bf16[272,128]{1,0:T(8,128)(2,1)S(1)}, u32[]{:S(2)}, u32[]{:S(2)}) collective-permute-start(bf16[272,128]{1,0:T(8,128)(2,1)S(1)} %shard_map.116.refs_3_), channel_id=1, source_target_pairs={{0,24},{1,25},{2,26},{3,27},{4,28},{5,29},{6,30},{7,31},{8,16},{9,... | collective-permute-start | bytes 208904 | tf_op jit(solution)/shard_map/ppermute | solution.py:329
  6.9 8.2 %collective-permute-start.4 = (bf16[272,128]{1,0:T(8,128)(2,1)S(1)}, bf16[272,128]{1,0:T(8,128)(2,1)S(1)}, u32[]{:S(2)}, u32[]{:S(2)}) collective-permute-start(bf16[272,128]{1,0:T(8,128)(2,1)S(1)} %shard_map.116.refs_3_), channel_id=1, source_target_pairs={{0,16},{1,17},{2,18},{3,19},{4,20},{5,21},{6,22},{7,23},{8,24},{9,... | collective-permute-start | bytes 208904 | tf_op jit(solution)/shard_map/ppermute | solution.py:329
  6.9 8.2 %collective-permute-start.3 = (bf16[272,128]{1,0:T(8,128)(2,1)S(1)}, bf16[272,128]{1,0:T(8,128)(2,1)S(1)}, u32[]{:S(2)}, u32[]{:S(2)}) collective-permute-start(bf16[272,128]{1,0:T(8,128)(2,1)S(1)} %shard_map.116.refs_3_), channel_id=1, source_target_pairs={{0,8},{1,9},{2,10},{3,11},{4,12},{5,13},{6,14},{7,15},{8,0},{9,1},... | collective-permute-start | bytes 208904 | tf_op jit(solution)/shard_map/ppermute | solution.py:329
  7.3 12.3 %collective-permute-start = (bf16[784,128]{1,0:T(8,128)(2,1)S(1)}, bf16[784,128]{1,0:T(8,128)(2,1)S(1)}, u32[]{:S(2)}, u32[]{:S(2)}) collective-permute-start(bf16[784,128]{1,0:T(8,128)(2,1)S(1)} %get-tuple-element.22), channel_id=1, source_target_pairs={{0,1},{1,2},{2,3},{3,4},{4,5},{5,6},{6,7},{7,8},{8,9},{9,10},{10,1... | collective-permute-start | bytes 602120 | tf_op jit(solution)/shard_map/ppermute | solution.py:397
  10.7 9.0 %collective-permute-start.1 = (bf16[784,128]{1,0:T(8,128)(2,1)S(1)}, bf16[784,128]{1,0:T(8,128)(2,1)S(1)}, u32[]{:S(2)}, u32[]{:S(2)}) collective-permute-start(bf16[784,128]{1,0:T(8,128)(2,1)S(1)} %get-tuple-element.23), channel_id=1, source_target_pairs={{1,0},{2,1},{3,2},{4,3},{5,4},{6,5},{7,6},{8,7},{9,8},{10,9},{11,1... | collective-permute-start | bytes 602120 | tf_op jit(solution)/shard_map/ppermute | solution.py:398
  12.6 1.5 %copy-start = (s32[1024]{0:T(1024)S(1)}, s32[1024]{0:T(1024)}, u32[]{:S(2)}) copy-start(s32[1024]{0:T(1024)} %param.15) | copy-start | bytes 12292
  14.1 54.7 %collective-permute-start.9 = (s32[8,128]{1,0:T(8,128)S(1)}, s32[8,128]{1,0:T(8,128)S(1)}, u32[]{:S(2)}, u32[]{:S(2)}) collective-permute-start(s32[8,128]{1,0:T(8,128)S(1)} %bitcast.7), channel_id=1, source_target_pairs={{0,1},{1,0},{2,3},{3,2},{4,5},{5,4},{6,7},{7,6},{8,9},{9,8},{10,11... | collective-permute-start | bytes 12296 | tf_op jit(solution)/shard_map/ppermute | solution.py:329
  19.6 0.7 copy-start.1
  19.7 0.7 copy-start.2
  22.7 5.9 %collective-permute-start.10 = (bf16[128,128]{1,0:T(8,128)(2,1)S(1)}, bf16[128,128]{1,0:T(8,128)(2,1)S(1)}, u32[]{:S(2)}, u32[]{:S(2)}) collective-permute-start(bf16[128,128]{1,0:T(8,128)(2,1)S(1)} %get-tuple-element.33.refs_3_), channel_id=1, source_target_pairs={{0,8},{1,9},{2,10},{3,11},{4,12},{5,13},{6,14},{7,15},{8,0},{9,1},... | collective-permute-start | bytes 98312 | tf_op jit(solution)/shard_map/ppermute | solution.py:329
  25.9 9.2 %collective-permute-start.6 = (bf16[1088,128]{1,0:T(8,128)(2,1)S(1)}, bf16[1088,128]{1,0:T(8,128)(2,1)S(1)}, u32[]{:S(2)}, u32[]{:S(2)}) collective-permute-start(bf16[1088,128]{1,0:T(8,128)(2,1)S(1)} %pad_maximum_fusion.refs_2_), channel_id=1, source_target_pairs={{0,2},{1,3},{2,0},{3,1},{4,6},{5,7},{6,4},{7,5},{8,10},{9,11},{10,... | collective-permute-start | bytes 835592 | tf_op jit(solution)/shard_map/ppermute | solution.py:329
  27.0 8.1 %collective-permute-start.7 = (bf16[1088,128]{1,0:T(8,128)(2,1)S(1)}, bf16[1088,128]{1,0:T(8,128)(2,1)S(1)}, u32[]{:S(2)}, u32[]{:S(2)}) collective-permute-start(bf16[1088,128]{1,0:T(8,128)(2,1)S(1)} %pad_maximum_fusion.refs_2_), channel_id=1, source_target_pairs={{0,4},{1,5},{2,6},{3,7},{4,0},{5,1},{6,2},{7,3},{8,12},{9,13},{10,... | collective-permute-start | bytes 835592 | tf_op jit(solution)/shard_map/ppermute | solution.py:329
  28.1 12.5 %collective-permute-start.8 = (bf16[1088,128]{1,0:T(8,128)(2,1)S(1)}, bf16[1088,128]{1,0:T(8,128)(2,1)S(1)}, u32[]{:S(2)}, u32[]{:S(2)}) collective-permute-start(bf16[1088,128]{1,0:T(8,128)(2,1)S(1)} %pad_maximum_fusion.refs_2_), channel_id=1, source_target_pairs={{0,6},{1,7},{2,4},{3,5},{4,2},{5,3},{6,0},{7,1},{8,14},{9,15},{10,... | collective-permute-start | bytes 835592 | tf_op jit(solution)/shard_map/ppermute | solution.py:329
  28.6 5.4 %collective-permute-start.11 = (bf16[256,128]{1,0:T(8,128)(2,1)S(1)}, bf16[256,128]{1,0:T(8,128)(2,1)S(1)}, u32[]{:S(2)}, u32[]{:S(2)}) collective-permute-start(bf16[256,128]{1,0:T(8,128)(2,1)S(1)} %pad_maximum_fusion.3), channel_id=1, source_target_pairs={{0,16},{1,17},{2,18},{3,19},{4,20},{5,21},{6,22},{7,23},{8,24},{9,... | collective-permute-start | bytes 196616 | tf_op jit(solution)/shard_map/ppermute | solution.py:329
  34.0 15.5 %collective-permute-start.12 = (bf16[512,128]{1,0:T(8,128)(2,1)S(1)}, bf16[512,128]{1,0:T(8,128)(2,1)S(1)}, u32[]{:S(2)}, u32[]{:S(2)}) collective-permute-start(bf16[512,128]{1,0:T(8,128)(2,1)S(1)} %pad_maximum_fusion.2), channel_id=1, source_target_pairs={{0,2},{1,3},{2,0},{3,1},{4,6},{5,7},{6,4},{7,5},{8,10},{9,11},{10,... | collective-permute-start | bytes 393224 | tf_op jit(solution)/shard_map/ppermute | solution.py:329
  49.5 19.3 %collective-permute-start.13 = (bf16[1024,128]{1,0:T(8,128)(2,1)S(1)}, bf16[1024,128]{1,0:T(8,128)(2,1)S(1)}, u32[]{:S(2)}, u32[]{:S(2)}) collective-permute-start(bf16[1024,128]{1,0:T(8,128)(2,1)S(1)} %pad_maximum_fusion.1), channel_id=1, source_target_pairs={{0,4},{1,5},{2,6},{3,7},{4,0},{5,1},{6,2},{7,3},{8,12},{9,13},{10,... | collective-permute-start | bytes 786440 | tf_op jit(solution)/shard_map/ppermute | solution.py:329
  68.7 5.8 %copy-start.3 = (f32[32,1024]{1,0:T(8,128)S(1)}, f32[32,1024]{1,0:T(8,128)}, u32[]{:S(2)}) copy-start(f32[32,1024]{1,0:T(8,128)} %refs_3_.1) | copy-start | bytes 393220
  71.1 3.4 %collective-permute-start.14 = (f32[32,1024]{1,0:T(8,128)S(1)}, f32[32,1024]{1,0:T(8,128)S(1)}, u32[]{:S(2)}, u32[]{:S(2)}) collective-permute-start(f32[32,1024]{1,0:T(8,128)S(1)} %get-tuple-element.35), channel_id=1, source_target_pairs={{0,1},{1,0},{2,3},{3,2},{4,5},{5,4},{6,7},{7,6},{8,9},{9,8},{10,11... | collective-permute-start | bytes 393224 | tf_op jit(solution)/shard_map/ppermute | solution.py:329

commit v3 on v2

v3 whole, which is shorter than its diff:
```python
import math

import jax
import jax.numpy as jnp
from jax import lax
from jax.experimental import pallas as pl
from jax.experimental.pallas import tpu as pltpu
from jax.sharding import PartitionSpec as P


TILE = 2048

softening = 0.0004
relax_rate = 0.8
update_rate = 0.5
kernel_gain = 0.25

FEATURES = 32
VALUES = 8
PAIR_ROWS = 16
VMEM_LIMIT = 32 << 20

F32 = jnp.float32
BF16 = jnp.bfloat16


def vmem():
    return pl.BlockSpec(memory_space=pltpu.VMEM)


def smem():
    return pl.BlockSpec(memory_space=pltpu.SMEM)


def cost_of(count):
    return pl.CostEstimate(flops=count * 2_500_000_000, bytes_accessed=count << 17, transcendentals=count << 21)


def call(body, outs, ins, scratch=(), cost=None, out_specs=None, aliases=None):
    return pl.pallas_call(
        body,
        out_shape=outs,
        in_specs=ins,
        out_specs=[vmem() for _ in outs] if out_specs is None else out_specs,
        scratch_shapes=list(scratch),
        cost_estimate=cost,
        input_output_aliases=aliases or {},
        compiler_params=pltpu.CompilerParams(vmem_limit_bytes=VMEM_LIMIT),
    )


def prepare_kernel(*refs, rows, layers, width):
    count = 8
    sources, results = refs[:count], refs[count:-5]
    flux, pairs, cells, tile, sems = refs[-5:]
    inner, outer, message, *held = results
    field, source, factor, pos, area = held
    places = [field, source, factor, flux, pairs, cells, pos, area]
    copies = [pltpu.make_async_copy(a, b, sems.at[i]) for i, (a, b) in enumerate(zip(sources, places))]
    for copy in copies:
        copy.start()
    lanes = message.shape[1]
    loads, pan = flux.shape
    slots = pairs.shape[1]
    used = pan // lanes * loads
    for copy in copies[:3]:
        copy.wait()
    lines = field.shape[0] // width
    core = lax.rem(lax.axis_index("dev"), 2)

    def line(ref, x, count):
        return ref[pl.ds(x, count, stride=width), :].astype(BF16)

    for out, upward in ((inner, 1 - core), (outer, core)):
        near = upward * (width - 2)
        edge = upward * (width - 1)
        out[0:lines, :] = line(field, near, lines)
        out[lines : 2 * lines, :] = line(field, near + 1, lines)
        out[2 * lines : 3 * lines, :] = line(source, edge, lines)
        tail = factor[pl.ds(edge, layers, stride=width), :]
        out[3 * lines : rows, :] = jnp.concatenate([tail, tail], axis=0).astype(BF16)
    for copy in copies[3:]:
        copy.wait()
    tile[...] = jnp.full(tile.shape, -2.0, F32)
    tile[0:2, 0:slots] = pairs[...].astype(F32)
    slot_rows = tile[...].astype(BF16)
    inner[rows : rows + PAIR_ROWS, :] = slot_rows
    high = lax.shift_right_logical(cells[...], 8)
    both = jnp.concatenate([high, cells[...] - high * 256], axis=0)
    inner[rows + PAIR_ROWS :, :] = both.astype(F32).astype(BF16)
    weight = area[:, pl.ds(pl.multiple_of(lax.axis_index("dev") * pan, pan), pan)]
    for j in range(pan // lanes):
        span = slice(j * lanes, (j + 1) * lanes)
        half = flux[:, span].astype(BF16).astype(F32)
        message[j * loads : (j + 1) * loads, :] = (half * weight[:, span]).astype(BF16)
    message[used:, :] = slot_rows


def relax_kernel(material, scale, field, source, factor, inner, outer, out, top, *, layers, width):
    lines = field.shape[0] // width
    loads = lines // layers
    ny = field.shape[1]
    depth = lax.broadcasted_iota(jnp.int32, (layers, ny), 0)
    lane = lax.broadcasted_iota(jnp.int32, (1, layers, ny), 2)
    level = lax.broadcasted_iota(jnp.int32, (1, layers, ny), 1)
    layer_scale = jnp.zeros((layers, ny), F32)
    for k in range(layers):
        layer_scale = jnp.where(depth == k, scale[material[k]], layer_scale)

    def cube(value):
        return value.reshape(loads, layers, ny)

    def own(ref, x):
        return cube(ref[pl.ds(x, lines, stride=width), :])

    odd = lax.rem(lax.axis_index("dev"), 2) == 1

    def sent(start, count, above):
        first = inner[start : start + count, :].astype(F32)
        second = outer[start : start + count, :].astype(F32)
        return jnp.where(odd, first, second) if above else jnp.where(odd, second, first)

    def part(i, above):
        return cube(sent(i * lines, lines, above))

    def tail(above):
        return sent(3 * lines, 2 * layers, above)[0:layers]

    fields = {-2: part(0, True), -1: part(1, True), width: part(0, False), width + 1: part(1, False)}
    sources = {-1: part(2, True), width: part(2, False)}
    factors = {-1: tail(True), width: tail(False)}
    for x in range(width):
        fields[x] = own(field, x)
        sources[x] = own(source, x)
        factors[x] = factor[pl.ds(x, layers, stride=width), :]
    conducts = {x: (layer_scale * value)[None] for x, value in factors.items()}
    gains = {x: relax_rate / (6.0 * value + 1.0) for x, value in conducts.items()}

    def sweep(values, x):
        centre = values[x]
        over = jnp.where(level == layers - 1, 0.0, pltpu.roll(centre, layers - 1, 1))
        under = jnp.where(level == 0, 0.0, pltpu.roll(centre, 1, 1))
        right = jnp.where(lane == ny - 1, 0.0, pltpu.roll(centre, ny - 1, 2))
        left = jnp.where(lane == 0, 0.0, pltpu.roll(centre, 1, 2))
        beside = over + under + (values[x + 1] + values[x - 1]) + (right + left)
        applied = conducts[x] * (6.0 * centre - beside) + centre
        return centre + (sources[x] - applied) * gains[x]

    first = {x: sweep(fields, x) for x in range(-1, width + 1)}
    for x in range(width):
        out[pl.ds(x, lines, stride=width), :] = sweep(first, x).reshape(lines, ny)
    for x in range(width):
        rows = pl.ds((layers - 1) * width + x, loads, stride=layers * width)
        top[x * loads : (x + 1) * loads, :] = out[rows, :].astype(BF16)


def pieces(value):
    high = value.astype(BF16).astype(F32)
    rest = value - high
    middle = rest.astype(BF16).astype(F32)
    return high, middle, (rest - middle).astype(BF16).astype(F32)


def row_side(value):
    high, middle, low = pieces(value)
    return [high, high, middle, middle, high, low]


def col_side(value):
    high, middle, low = pieces(value)
    return [high, middle, high, middle, low, high]


def feature_kernel(pos, area, rows_out, row_values, cols_out, col_values, gains, strips, *, pan, blocks):
    me = lax.axis_index("dev")
    core = lax.rem(me, 2)

    def pick(ref, k, device):
        return ref[k : k + 1, pl.ds(pl.multiple_of(device * pan, pan), pan)]

    def gather(devices):
        lines = [jnp.concatenate([pick(pos, k, d) for d in devices], axis=0) - 0.5 for k in range(3)]
        x, y, z = lines
        return lines, x * x + y * y + z * z

    def filled(flat, like, count):
        return flat + [jnp.zeros_like(like)] * (count - len(flat))

    lines, norm = gather([2 * g + core for g in range(blocks)])
    ones = jnp.ones_like(norm)
    norm = norm + softening
    flat = [piece for line in lines for piece in row_side(line)] + [*pieces(norm), ones, ones, ones]
    flat = filled(flat, norm, FEATURES) + filled([*lines, norm], norm, VALUES)
    count = len(flat)
    lanes = strips.shape[1]
    strip = count * blocks
    for j in range(pan // lanes):
        for f in range(count):
            start = j * strip + f * blocks
            strips[start : start + blocks, :] = flat[f][:, j * lanes : (j + 1) * lanes]
    for g in range(blocks):
        for j in range(pan // lanes):
            span = slice(j * lanes, (j + 1) * lanes)
            value = strips[pl.ds(j * strip + g, FEATURES, stride=blocks), :]
            rows_out[g * FEATURES : (g + 1) * FEATURES, span] = value.astype(BF16)
            value = strips[pl.ds(j * strip + FEATURES * blocks + g, VALUES, stride=blocks), :]
            row_values[g * VALUES : (g + 1) * VALUES, span] = value

    for half, device in enumerate((me, me + 1 - 2 * core)):
        span = slice(half * pan, (half + 1) * pan)
        lines, norm = gather([device])
        lines = [-2.0 * line for line in lines]
        ones = jnp.ones_like(norm)
        flat = [piece for line in lines for piece in col_side(line)] + [ones, ones, ones, *pieces(norm)]
        cols_out[:, span] = jnp.concatenate(filled(flat, norm, FEATURES), axis=0).astype(BF16)
        col_values[:, span] = jnp.concatenate(filled([*lines, norm], norm, VALUES), axis=0)
        gains[:, span] = pick(area, 0, device) * (kernel_gain / math.sqrt(TILE))


def message_kernel(message, arrived, out, *, rows):
    half = PAIR_ROWS // 2
    used = message.shape[0] - PAIR_ROWS
    mine = message[used:, :].astype(F32)[0:half]
    other = arrived[rows : rows + PAIR_ROWS, :].astype(F32)[0:half]
    out[used:, :] = jnp.concatenate([mine, other], axis=0).astype(BF16)


def add_block(tables, message, start, block, kernel, store, *, loads, pan, wide=512, step=64):
    rows, row_values, cols, col_values = tables
    lanes = message.shape[1]
    parts = [message[pl.ds(start + j * loads, loads), :] for j in range(pan // lanes)]
    flux = jnp.concatenate(parts, axis=1)
    features = rows[pl.ds(pl.multiple_of(block * FEATURES, FEATURES), FEATURES), :]
    split = pan * 5 // 8
    values = row_values[pl.ds(pl.multiple_of(block * VALUES, VALUES), VALUES), :]
    values = jnp.transpose(values[:, split:])

    def make(span):
        squared = lax.dot_general(
            features[:, :split], cols[:, span], (((0,), (0,)), ((), ())), preferred_element_type=F32
        )
        kernel[:split, span] = lax.rsqrt(squared.astype(BF16))
        col = col_values[:, span]
        for at in range(0, pan - split, step):
            row = values[at : at + step]
            squared = row[:, 0:1] * col[0:1] + row[:, 1:2] * col[1:2] + row[:, 2:3] * col[2:3]
            squared = squared + (row[:, 3:4] + col[3:4])
            kernel[split + at : split + at + step, span] = lax.rsqrt(squared.astype(BF16))

    def apply(span):
        store(span, jnp.dot(flux, kernel[:, span], preferred_element_type=F32))

    spans = [slice(c, c + wide) for c in range(0, cols.shape[1], wide)]
    make(spans[0])
    for before, span in zip(spans, spans[1:]):
        make(span)
        apply(before)
    apply(spans[-1])


def choose(values, i):
    value = jnp.int32(values[0])
    for k in range(1, len(values)):
        value = jnp.where(i == k, values[k], value)
    return value


def near_kernel(*refs, first, masks, loads, pan, size):
    tables, (stack, out, kernel) = refs[:4], refs[4:]
    me = lax.axis_index("dev")

    @pl.loop(0, len(masks))
    def _(i):
        block = lax.shift_right_logical(me ^ choose(masks, i), 1)

        def store(span, value):
            out[i, :, span] = value

        start = pl.multiple_of((first + i) * size, 16)
        add_block(tables, stack, start, block, kernel, store, loads=loads, pan=pan)


def active(words, block):
    word = words[0]
    for w in range(1, words.shape[0]):
        word = jnp.where(lax.shift_right_logical(block, 4) == w, words[w], word)
    return (lax.shift_right_logical(word, block & 15) & 1) != 0


def far_kernel(*refs, near_masks, near_count, stacks, far_count, loads, pan, size):
    tables, nears, stacked = refs[:4], refs[4 : 4 + near_count], refs[4 + near_count : -3]
    out, words, kernel = refs[-3:]
    me = lax.axis_index("dev")
    own = lax.shift_right_logical(me, 1)
    info = size - PAIR_ROWS
    first = []
    for ref, masks in zip(stacked, stacks):
        first += [ref[i * size + info : (i + 1) * size, :] for i in range(len(masks))]
    first = jnp.concatenate(first, axis=0).astype(F32)
    total = first.shape[0]
    second = pltpu.roll(first, total - 1, 0)
    index = lax.broadcasted_iota(jnp.int32, first.shape, 0)
    paired = index % (PAIR_ROWS // 2) == 0
    mine = own.astype(F32)
    linked = paired & ((first == mine) | (second == mine))
    other = jnp.where(first == mine, second, first).astype(jnp.int32)
    for w in range(words.shape[0]):
        inside = linked & (other >= 16 * w) & (other < 16 * (w + 1))
        bit = jnp.left_shift(1, jnp.clip(other - 16 * w, 0, 15)).astype(F32)
        words[w] = jnp.sum(jnp.where(inside, bit, 0.0)).astype(jnp.int32)
    total = None
    i = 0
    for ref in nears:
        for k in range(ref.shape[0]):
            gate = active(words, lax.shift_right_logical(me ^ near_masks[i], 1)).astype(F32)
            value = ref[k] * gate
            total = value if total is None else total + value
            i += 1
    out[...] = total

    def store(span, value):
        out[:, span] += value

    for stack, masks in list(zip(stacked, stacks))[len(stacked) - far_count :]:

        @pl.loop(0, len(masks))
        def _(i, stack=stack, masks=masks):
            block = lax.shift_right_logical(me ^ choose(masks, i), 1)

            @pl.when(active(words, block))
            def _():
                start = pl.multiple_of(i * size, 16)
                add_block(tables, stack, start, block, kernel, store, loads=loads, pan=pan)


def trace_kernel(potential, gains, cells, partner, *refs, groups, loads, width, pan, ny):
    arrived, outs, table = refs[: len(groups)], refs[len(groups) : -1], refs[-1]
    me = lax.axis_index("dev")
    base = 0
    owners = []
    for ref, masks in zip(arrived, groups):
        count = len(masks) * width * loads
        table[pl.ds(base, count), :] = ref[...].astype(F32)
        base += count
        owners += [me ^ mask for mask in masks]
    lanes = cells.shape[1]
    count = pan // lanes
    both = partner[partner.shape[0] - 2 * count :, :].astype(F32)
    theirs = (both[:count] * 256.0 + both[count:]).astype(jnp.int32)
    for half, (mine, out) in enumerate(zip((cells[...], theirs), outs)):
        for pb in range(count):
            cell = jnp.broadcast_to(mine[pb : pb + 1, :], (loads, lanes))
            line = lax.div(cell, ny)
            lane = cell - line * ny
            acc = jnp.zeros((loads, lanes), F32)
            for b, owner in enumerate(owners):
                for x in range(width):
                    start = (b * width + x) * loads
                    seen = jnp.take_along_axis(table[start : start + loads, :], lane, axis=1)
                    acc = jnp.where(line == owner * width + x, seen, acc)
            here = half * pan + pb * lanes
            span = slice(here, here + lanes)
            change = acc - potential[:, span] * gains[:, span]
            out[:, pb * lanes : (pb + 1) * lanes] = update_rate * change


def groups_of(size):
    bits = [1 << b for b in range(1, size.bit_length() - 1)]
    low = len(bits) % 2
    split = [bits[i : i + 2] for i in range(low, len(bits), 2)]
    split = ([bits[:low]] if low else []) + split
    phases = []
    for pair in reversed(split):
        phases.append([pair[0]] if len(pair) == 1 else [pair[0], pair[1], pair[0] | pair[1]])
    return phases


def swap(array, mask, size):
    return lax.ppermute(array, "dev", [(i, i ^ mask) for i in range(size)])


def spread(array, phases, size):
    parts = [(array, [0])]
    for masks in phases:
        stack = parts[0][0] if len(parts) == 1 else jnp.concatenate([a for a, _ in parts], axis=0)
        held = [m for _, group in parts for m in group]
        sent = [(swap(stack, mask, size), [mask ^ m for m in held]) for mask in masks]
        parts = [*parts, *sent]
    return parts


def program(
    field_in,
    source,
    cell_factor,
    layer_material,
    material_scale,
    panel_cell,
    panel_pos,
    panel_area,
    flux_in,
    pair_list,
):
    size = lax.axis_size("dev")
    loads, layers, width, ny = field_in.shape
    pan = flux_in.shape[1]
    blocks = size // 2
    lanes = 128
    lines = loads * layers
    phases = groups_of(size)

    cells = panel_cell.reshape(pan // lanes, lanes)
    halo_rows = 3 * lines + 2 * layers
    inner_rows = halo_rows + PAIR_ROWS + 2 * (pan // lanes)
    message_rows = pan // lanes * loads + PAIR_ROWS
    wanted = (
        field_in.reshape(lines * width, ny),
        source.reshape(lines * width, ny),
        cell_factor.reshape(layers * width, ny),
        flux_in,
        pair_list.T,
        cells,
        panel_pos,
        panel_area.reshape(1, -1),
    )
    shapes = [jax.ShapeDtypeStruct(a.shape, a.dtype) for a in wanted]
    inner, outer, message, field, load, factor, pos, area = call(
        lambda *refs: prepare_kernel(*refs, rows=halo_rows, layers=layers, width=width),
        [
            jax.ShapeDtypeStruct((inner_rows, ny), BF16),
            jax.ShapeDtypeStruct((halo_rows, ny), BF16),
            jax.ShapeDtypeStruct((message_rows, lanes), BF16),
            *shapes[:3],
            *shapes[6:],
        ],
        [pl.BlockSpec(memory_space=pltpu.HBM)] * len(wanted),
        scratch=[
            pltpu.VMEM(flux_in.shape, F32),
            pltpu.VMEM(shapes[4].shape, jnp.int32),
            pltpu.VMEM(cells.shape, jnp.int32),
            pltpu.VMEM((PAIR_ROWS, lanes), F32),
            pltpu.SemaphoreType.DMA((len(wanted),)),
        ],
    )(*[pltpu.with_memory_space_constraint(a, pltpu.HBM) for a in wanted])
    inner = swap(inner, 1, size)
    sides = [(i, i + 1) for i in range(1, size - 1, 2)]
    outer = lax.ppermute(outer, "dev", sides + [(j, i) for i, j in sides])
    (message,) = call(
        lambda *refs: message_kernel(*refs, rows=halo_rows),
        [jax.ShapeDtypeStruct((message_rows, lanes), BF16)],
        [vmem()] * 2,
        aliases={0: 0},
    )(message, inner)
    flux_parts = spread(message, phases, size)
    near_count = 1 + len(phases[0])
    near_parts, far_parts = flux_parts[:near_count], flux_parts[near_count:]
    near_stack = jnp.concatenate([a for a, _ in near_parts], axis=0)

    *tables, gains = call(
        lambda *refs: feature_kernel(*refs, pan=pan, blocks=blocks),
        [
            jax.ShapeDtypeStruct((FEATURES * blocks, pan), BF16),
            jax.ShapeDtypeStruct((VALUES * blocks, pan), F32),
            jax.ShapeDtypeStruct((FEATURES, 2 * pan), BF16),
            jax.ShapeDtypeStruct((VALUES, 2 * pan), F32),
            jax.ShapeDtypeStruct((1, 2 * pan), F32),
        ],
        [vmem()] * 2,
        scratch=[pltpu.VMEM((pan // lanes * (FEATURES + VALUES) * blocks, lanes), F32)],
    )(pos, area)

    field_out, top = call(
        lambda *refs: relax_kernel(*refs, layers=layers, width=width),
        [
            jax.ShapeDtypeStruct((lines * width, ny), F32),
            jax.ShapeDtypeStruct((width * loads, ny), BF16),
        ],
        [smem()] * 2 + [vmem()] * 5,
    )(layer_material, material_scale, field, load, factor, inner, outer)
    top_parts = spread(top, phases, size)

    wide = jax.ShapeDtypeStruct((loads, 2 * pan), F32)
    strip = pltpu.VMEM((pan, 2 * pan), BF16)
    near_masks = [masks[0] for _, masks in near_parts]
    nears = []
    for first, masks, stack in ((0, near_masks[:1], message), (1, near_masks[1:], near_stack)):
        (near,) = call(
            lambda *refs, first=first, masks=masks: near_kernel(
                *refs, first=first, masks=masks, loads=loads, pan=pan, size=message_rows
            ),
            [jax.ShapeDtypeStruct((len(masks), loads, 2 * pan), F32)],
            [vmem()] * 5,
            scratch=[strip],
            cost=cost_of(len(masks)),
        )(*tables, stack)
        nears.append(near)
    (potential,) = call(
        lambda *refs: far_kernel(
            *refs,
            near_masks=near_masks,
            near_count=len(nears),
            stacks=[masks for _, masks in flux_parts],
            far_count=len(far_parts),
            loads=loads,
            pan=pan,
            size=message_rows,
        ),
        [wide],
        [vmem()] * (4 + len(nears) + len(flux_parts)),
        scratch=[pltpu.SMEM(((blocks + 15) // 16,), jnp.int32), strip],
        cost=cost_of(blocks - near_count),
    )(*tables, *nears, *[a for a, _ in flux_parts])

    half = jax.ShapeDtypeStruct((loads, pan), F32)
    kept, given = call(
        lambda *refs: trace_kernel(
            *refs,
            groups=[masks for _, masks in top_parts],
            loads=loads,
            width=width,
            pan=pan,
            ny=ny,
        ),
        [half, half],
        [vmem()] * (4 + len(top_parts)),
        scratch=[pltpu.VMEM((blocks * width * loads, ny), F32)],
    )(potential, gains, cells, inner, *[a for a, _ in top_parts])
    flux_out = flux_in + kept + swap(given, 1, size)
    return (field_out.reshape(field_in.shape), flux_out)


def solution(mesh):
    in_specs = (
        P(None, None, "dev", None),
        P(None, None, "dev", None),
        P(None, "dev", None),
        P(),
        P(),
        P("dev"),
        P(),
        P(),
        P(None, "dev"),
        P("dev", None),
    )
    out_specs = (P(None, None, "dev", None), P(None, "dev"))
    return jax.shard_map(program, mesh=mesh, in_specs=in_specs, out_specs=out_specs, check_vma=False)
```

time: 75.5 us -> 72.8 us (0.964)
  the two profiles are of different devices: /device:TPU:7 before, /device:TPU:3 now
where the time goes in v3:
time: 72.8 us; the launch traced here: 72.6 us
  Pallas kernels  35.8 us (49%)
  starting transfers between devices  21.3 us (29%)
  waiting for transfers between devices  13.4 us (18%)
  between operations  0.78 us (1%)
    pallas_call x1, Pallas kernels, program(): call(lambda *refs: far_kernel(*refs, near_masks=near_masks, near_count=le...  20.2 us
    ppermute x14, starting transfers between devices, swap(): return lax.ppermute(array, 'dev', [(i, i ^ mask) for i in range(size)])  18.3 us
    ppermute x14, waiting for transfers between devices, swap(): return lax.ppermute(array, 'dev', [(i, i ^ mask) for i in range(size)])  12 us
    pallas_call x2, Pallas kernels, program(): call(lambda *refs, first=first, masks=masks: near_kernel(*refs, first=fir...  7.65 us
    ppermute x1, starting transfers between devices, program(): outer = lax.ppermute(outer, 'dev', sides + [(j, i) for i, j in sides])  3.02 us
    pallas_call x1, Pallas kernels, program(): call(lambda *refs: relax_kernel(*refs, layers=layers, width=width), [jax....  2.38 us
    pallas_call x1, Pallas kernels, program(): call(lambda *refs: trace_kernel(*refs, groups=[masks for _, masks in top_...  2.33 us
    pallas_call x1, Pallas kernels, program(): call(lambda *refs: feature_kernel(*refs, pan=pan, blocks=blocks), [jax.Sh...  1.64 us
  transfers between devices with their start and end apart: 15, of which 5 were waited for; matrix products, arithmetic and copies ran while one was open for 0% of the time, Pallas kernels for 44%

profile of v3, /device:TPU:3, one launch (start us, length us, event | category | flops | bytes accessed | tf_op | source)
XLA Modules:
  0.0 72.6 jit_solution(11709556470543507831)
XLA Ops:
  0.6 1.6 %shard_map.113 = (bf16[816,128]{1,0:T(8,128)(2,1)S(1)}, bf16[784,128]{1,0:T(8,128)(2,1)S(1)}, bf16[272,128]{1,0:T(8,128)(2,1)S(1)}, f32[1024,128]{1,0:T(8,128)S(...) custom-call(f32[1024,128]{1,0:T(8,128)} %bitcast.9, ...), custom_call_target="tpu_custom_call" | custom-call | tf_op jit(solution)/shard_map/pallas_call | solution.py:427
  2.2 0.7 %collective-permute-start = (bf16[816,128]{1,0:T(8,128)(2,1)S(1)}, bf16[816,128]{1,0:T(8,128)(2,1)S(1)}, u32[]{:S(2)}, u32[]{:S(2)}) collective-permute-start(bf16[816,128]{1,0:T(8,128)(2,1)S(1)} %get-tuple-element.22), channel_id=1, source_target_pairs={{0,1},{1,0},{2,3},{3,2},{4,5},{5,4},{6,7},{7,6},{8,9},{9,8},{10,11... | collective-permute-start | bytes 626696 | tf_op jit(solution)/shard_map/ppermute | solution.py:379
  2.9 3.0 %collective-permute-start.1 = (bf16[784,128]{1,0:T(8,128)(2,1)S(1)}, bf16[784,128]{1,0:T(8,128)(2,1)S(1)}, u32[]{:S(2)}, u32[]{:S(2)}) collective-permute-start(bf16[784,128]{1,0:T(8,128)(2,1)S(1)} %get-tuple-element.23), channel_id=1, source_target_pairs={{1,2},{3,4},{5,6},{7,8},{9,10},{11,12},{13,14},{15,16},{17,18},{19... | collective-permute-start | bytes 602120 | tf_op jit(solution)/shard_map/ppermute | solution.py:447
  6.0 1.6 %shard_map.115 = (bf16[512,1024]{1,0:T(8,128)(2,1)S(1)}, f32[128,1024]{1,0:T(8,128)S(1)}, bf16[32,2048]{1,0:T(8,128)(2,1)S(1)}, f32[8,2048]{1,0:T(8,128)S(1)}, f32[1,2048]{1,0:T(1,128)S(1)}) custom-call(f32[3,32768]{1,0:T(4,128)S(1)} %get-tuple-element.25.refs_0_, f32[1,32768]{1,0:T(1,128)S(1)} %get-tuple-element.26.refs_1_), custom_call_target="tpu_custom_call" | custom-call | tf_op jit(solution)/shard_map/pallas_call | solution.py:459
  7.6 3.4 %collective-permute-start.4 = (bf16[272,128]{1,0:T(8,128)(2,1)S(1)}, bf16[272,128]{1,0:T(8,128)(2,1)S(1)}, u32[]{:S(2)}, u32[]{:S(2)}) collective-permute-start(bf16[272,128]{1,0:T(8,128)(2,1)S(1)} %shard_map.116.refs_4_.refs_6_), channel_id=1, source_target_pairs={{0,24},{1,25},{2,26},{3,27},{4,28},{5,29},{6,30},{7,31},{8,16},{9,... | collective-permute-start | bytes 208904 | tf_op jit(solution)/shard_map/ppermute | solution.py:379
  11.4 1.3 %collective-permute-done.1.refs_6_ = bf16[784,128]{1,0:T(8,128)(2,1)S(1)} collective-permute-done((bf16[784,128]{1,0:T(8,128)(2,1)S(1)}, bf16[784,128]{1,0:T(8,128)(2,1)S(1)}, u32[]{:S(2)}, u32[]{:S(2)}) %collective-permute-start.1) | collective-permute-done | bytes 200736 | tf_op jit(solution)/shard_map/ppermute | solution.py:447
  13.4 2.4 %shard_map.114 = (f32[1024,128]{1,0:T(8,128)}, bf16[128,128]{1,0:T(8,128)(2,1)S(1)}) custom-call(s32[8]{0:T(128)S(1)} %copy-done.1, f32[4]{0:T(128)S(1)} %copy-done.2, f32[1024,128]{1,0:T(8,128)S(1)} %get-tuple-element.19.refs_2_, f32[1024,128]{1,0:T(8,128)S(1)} %get-tuple-element.20.refs_3_, f32[32,128]{1,0:T(8,128)S(1)} %get-tuple-element.21.refs_4_, ...), custom_call_target="tpu_custom_call" | custom-call | tf_op jit(solution)/shard_map/pallas_call | solution.py:472
  15.7 1.0 %collective-permute-start.8 = (bf16[128,128]{1,0:T(8,128)(2,1)S(1)}, bf16[128,128]{1,0:T(8,128)(2,1)S(1)}, u32[]{:S(2)}, u32[]{:S(2)}) collective-permute-start(bf16[128,128]{1,0:T(8,128)(2,1)S(1)} %get-tuple-element.33.refs_4_), channel_id=1, source_target_pairs={{0,8},{1,9},{2,10},{3,11},{4,12},{5,13},{6,14},{7,15},{8,0},{9,1},... | collective-permute-start | bytes 98312 | tf_op jit(solution)/shard_map/ppermute | solution.py:379
  16.7 2.6 %collective-permute-start.9 = (bf16[128,128]{1,0:T(8,128)(2,1)S(1)}, bf16[128,128]{1,0:T(8,128)(2,1)S(1)}, u32[]{:S(2)}, u32[]{:S(2)}) collective-permute-start(bf16[128,128]{1,0:T(8,128)(2,1)S(1)} %get-tuple-element.33.refs_4_), channel_id=1, source_target_pairs={{0,16},{1,17},{2,18},{3,19},{4,20},{5,21},{6,22},{7,23},{8,24},{9,... | collective-permute-start | bytes 98312 | tf_op jit(solution)/shard_map/ppermute | solution.py:379
  19.3 1.9 %shard_map.117.refs_4_ = f32[1,32,2048]{2,1,0:T(8,128)S(1)} custom-call(bf16[512,1024]{1,0:T(8,128)(2,1)S(1)} %get-tuple-element.27.refs_0_, f32[128,1024]{1,0:T(8,128)S(1)} %get-tuple-element.28.refs_1_, bf16[32,2048]{1,0:T(8,128)(2,1)S(1)} %get-tuple-element.29.refs_2_, f32[8,2048]{1,0:T(8,128)S(1)} %get-tuple-element.30.refs_3_, ...), custom_call_target="tpu_custom_call" | custom-call | flops 2500000000 | bytes 131072 | tf_op jit(solution)/shard_map/pallas_call | solution.py:487
  21.3 0.9 %collective-permute-start.10 = (bf16[128,128]{1,0:T(8,128)(2,1)S(1)}, bf16[128,128]{1,0:T(8,128)(2,1)S(1)}, u32[]{:S(2)}, u32[]{:S(2)}) collective-permute-start(bf16[128,128]{1,0:T(8,128)(2,1)S(1)} %get-tuple-element.33.refs_4_), channel_id=1, source_target_pairs={{0,24},{1,25},{2,26},{3,27},{4,28},{5,29},{6,30},{7,31},{8,16},{9,... | collective-permute-start | bytes 98312 | tf_op jit(solution)/shard_map/ppermute | solution.py:379
  22.2 4.3 %collective-permute-done.10.refs_7_ = bf16[128,128]{1,0:T(8,128)(2,1)S(1)} collective-permute-done((bf16[128,128]{1,0:T(8,128)(2,1)S(1)}, bf16[128,128]{1,0:T(8,128)(2,1)S(1)}, u32[]{:S(2)}, u32[]{:S(2)}) %collective-permute-start.10) | collective-permute-done | bytes 32800 | tf_op jit(solution)/shard_map/ppermute | solution.py:379
  26.4 1.0 %collective-permute-start.12 = (bf16[512,128]{1,0:T(8,128)(2,1)S(1)}, bf16[512,128]{1,0:T(8,128)(2,1)S(1)}, u32[]{:S(2)}, u32[]{:S(2)}) collective-permute-start(bf16[512,128]{1,0:T(8,128)(2,1)S(1)} %constant_dynamic-update-slice_fusion), channel_id=1, source_target_pairs={{0,4},{1,5},{2,6},{3,7},{4,0},{5,1},{6,2},{7,3},{8,12},{9,13},{10,... | collective-permute-start | bytes 393224 | tf_op jit(solution)/shard_map/ppermute | solution.py:379
  27.5 1.5 %collective-permute-start.5 = (bf16[1088,128]{1,0:T(8,128)(2,1)S(1)}, bf16[1088,128]{1,0:T(8,128)(2,1)S(1)}, u32[]{:S(2)}, u32[]{:S(2)}) collective-permute-start(bf16[1088,128]{1,0:T(8,128)(2,1)S(1)} %pad_maximum_fusion.refs_4_), channel_id=1, source_target_pairs={{0,2},{1,3},{2,0},{3,1},{4,6},{5,7},{6,4},{7,5},{8,10},{9,11},{10,... | collective-permute-start | bytes 835592 | tf_op jit(solution)/shard_map/ppermute | solution.py:379
  29.5 0.7 %collective-permute-start.7 = (bf16[1088,128]{1,0:T(8,128)(2,1)S(1)}, bf16[1088,128]{1,0:T(8,128)(2,1)S(1)}, u32[]{:S(2)}, u32[]{:S(2)}) collective-permute-start(bf16[1088,128]{1,0:T(8,128)(2,1)S(1)} %pad_maximum_fusion.refs_4_), channel_id=1, source_target_pairs={{0,6},{1,7},{2,4},{3,5},{4,2},{5,3},{6,0},{7,1},{8,14},{9,15},{10,... | collective-permute-start | bytes 835592 | tf_op jit(solution)/shard_map/ppermute | solution.py:379
  30.2 5.7 %shard_map.118.refs_5_ = f32[3,32,2048]{2,1,0:T(8,128)S(1)} custom-call(bf16[512,1024]{1,0:T(8,128)(2,1)S(1)} %get-tuple-element.27.refs_0_, f32[128,1024]{1,0:T(8,128)S(1)} %get-tuple-element.28.refs_1_, bf16[32,2048]{1,0:T(8,128)(2,1)S(1)} %get-tuple-element.29.refs_2_, f32[8,2048]{1,0:T(8,128)S(1)} %get-tuple-element.30.refs_3_, ...), custom_call_target="tpu_custom_call" | custom-call | flops 7500000256 | bytes 393216 | tf_op jit(solution)/shard_map/pallas_call | solution.py:487
  36.0 0.9 %collective-permute-done.5.refs_10_ = bf16[1088,128]{1,0:T(8,128)(2,1)S(1)} collective-permute-done((bf16[1088,128]{1,0:T(8,128)(2,1)S(1)}, bf16[1088,128]{1,0:T(8,128)(2,1)S(1)}, u32[]{:S(2)}, u32[]{:S(2)}) %collective-permute-start.5) | collective-permute-done | bytes 278560 | tf_op jit(solution)/shard_map/ppermute | solution.py:379
  36.9 0.8 %collective-permute-start.13 = (bf16[512,128]{1,0:T(8,128)(2,1)S(1)}, bf16[512,128]{1,0:T(8,128)(2,1)S(1)}, u32[]{:S(2)}, u32[]{:S(2)}) collective-permute-start(bf16[512,128]{1,0:T(8,128)(2,1)S(1)} %constant_dynamic-update-slice_fusion), channel_id=1, source_target_pairs={{0,6},{1,7},{2,4},{3,5},{4,2},{5,3},{6,0},{7,1},{8,14},{9,15},{10,... | collective-permute-start | bytes 393224 | tf_op jit(solution)/shard_map/ppermute | solution.py:379
  37.7 5.8 %collective-permute-done.7.refs_12_ = bf16[1088,128]{1,0:T(8,128)(2,1)S(1)} collective-permute-done((bf16[1088,128]{1,0:T(8,128)(2,1)S(1)}, bf16[1088,128]{1,0:T(8,128)(2,1)S(1)}, u32[]{:S(2)}, u32[]{:S(2)}) %collective-permute-start.7) | collective-permute-done | bytes 278560 | tf_op jit(solution)/shard_map/ppermute | solution.py:379
  43.6 20.2 %shard_map.119.refs_0_ = f32[32,2048]{1,0:T(8,128)S(1)} custom-call(bf16[512,1024]{1,0:T(8,128)(2,1)S(1)} %get-tuple-element.27.refs_0_, f32[128,1024]{1,0:T(8,128)S(1)} %get-tuple-element.28.refs_1_, bf16[32,2048]{1,0:T(8,128)(2,1)S(1)} %get-tuple-element.29.refs_2_, f32[8,2048]{1,0:T(8,128)S(1)} %get-tuple-element.30.refs_3_, ...), custom_call_target="tpu_custom_call" | custom-call | flops 30000001024 | bytes 1572864 | tf_op jit(solution)/shard_map/pallas_call | solution.py:497
  63.9 2.3 %shard_map.120 = (f32[32,1024]{1,0:T(8,128)S(1)}, f32[32,1024]{1,0:T(8,128)S(1)}) custom-call(f32[32,2048]{1,0:T(8,128)S(1)} %shard_map.119.refs_0_, f32[1,2048]{1,0:T(1,128)S(1)} %get-tuple-element.32.refs_1_, s32[8,128]{1,0:T(8,128)S(1)} %bitcast.8, bf16[816,128]{1,0:T(8,128)(2,1)S(1)} %collective-permute-done.refs_5_.refs_1_.refs_3_, ...), custom_call_target="tpu_custom_call" | custom-call | tf_op jit(solution)/shard_map/pallas_call | solution.py:515
  66.2 4.7 %collective-permute-start.14 = (f32[32,1024]{1,0:T(8,128)S(1)}, f32[32,1024]{1,0:T(8,128)S(1)}, u32[]{:S(2)}, u32[]{:S(2)}) collective-permute-start(f32[32,1024]{1,0:T(8,128)S(1)} %get-tuple-element.35), channel_id=1, source_target_pairs={{0,1},{1,0},{2,3},{3,2},{4,5},{5,4},{6,7},{7,6},{8,9},{9,8},{10,11... | collective-permute-start | bytes 393224 | tf_op jit(solution)/shard_map/ppermute | solution.py:379
  70.9 1.0 %collective-permute-done.14 = f32[32,1024]{1,0:T(8,128)S(1)} collective-permute-done((f32[32,1024]{1,0:T(8,128)S(1)}, f32[32,1024]{1,0:T(8,128)S(1)}, u32[]{:S(2)}, u32[]{:S(2)}) %collective-permute-start.14) | collective-permute-done | bytes 131104 | tf_op jit(solution)/shard_map/ppermute | solution.py:379
  71.9 0.7 add_add_fusion
  (28 shorter events, 1.7 us)
Async XLA Ops:
  2.2 5.4 %collective-permute-start = (bf16[816,128]{1,0:T(8,128)(2,1)S(1)}, bf16[816,128]{1,0:T(8,128)(2,1)S(1)}, u32[]{:S(2)}, u32[]{:S(2)}) collective-permute-start(bf16[816,128]{1,0:T(8,128)(2,1)S(1)} %get-tuple-element.22), channel_id=1, source_target_pairs={{0,1},{1,0},{2,3},{3,2},{4,5},{5,4},{6,7},{7,6},{8,9},{9,8},{10,11... | collective-permute-start | bytes 626696 | tf_op jit(solution)/shard_map/ppermute | solution.py:379
  2.9 9.8 %collective-permute-start.1 = (bf16[784,128]{1,0:T(8,128)(2,1)S(1)}, bf16[784,128]{1,0:T(8,128)(2,1)S(1)}, u32[]{:S(2)}, u32[]{:S(2)}) collective-permute-start(bf16[784,128]{1,0:T(8,128)(2,1)S(1)} %get-tuple-element.23), channel_id=1, source_target_pairs={{1,2},{3,4},{5,6},{7,8},{9,10},{11,12},{13,14},{15,16},{17,18},{19... | collective-permute-start | bytes 602120 | tf_op jit(solution)/shard_map/ppermute | solution.py:447
  7.6 19.8 %collective-permute-start.4 = (bf16[272,128]{1,0:T(8,128)(2,1)S(1)}, bf16[272,128]{1,0:T(8,128)(2,1)S(1)}, u32[]{:S(2)}, u32[]{:S(2)}) collective-permute-start(bf16[272,128]{1,0:T(8,128)(2,1)S(1)} %shard_map.116.refs_4_.refs_6_), channel_id=1, source_target_pairs={{0,24},{1,25},{2,26},{3,27},{4,28},{5,29},{6,30},{7,31},{8,16},{9,... | collective-permute-start | bytes 208904 | tf_op jit(solution)/shard_map/ppermute | solution.py:379
  11.0 16.4 %collective-permute-start.3 = (bf16[272,128]{1,0:T(8,128)(2,1)S(1)}, bf16[272,128]{1,0:T(8,128)(2,1)S(1)}, u32[]{:S(2)}, u32[]{:S(2)}) collective-permute-start(bf16[272,128]{1,0:T(8,128)(2,1)S(1)} %shard_map.116.refs_4_.refs_6_), channel_id=1, source_target_pairs={{0,16},{1,17},{2,18},{3,19},{4,20},{5,21},{6,22},{7,23},{8,24},{9,... | collective-permute-start | bytes 208904 | tf_op jit(solution)/shard_map/ppermute | solution.py:379
  11.0 16.4 %collective-permute-start.2 = (bf16[272,128]{1,0:T(8,128)(2,1)S(1)}, bf16[272,128]{1,0:T(8,128)(2,1)S(1)}, u32[]{:S(2)}, u32[]{:S(2)}) collective-permute-start(bf16[272,128]{1,0:T(8,128)(2,1)S(1)} %shard_map.116.refs_4_.refs_6_), channel_id=1, source_target_pairs={{0,8},{1,9},{2,10},{3,11},{4,12},{5,13},{6,14},{7,15},{8,0},{9,1},... | collective-permute-start | bytes 208904 | tf_op jit(solution)/shard_map/ppermute | solution.py:379
  12.7 0.7 copy-start.1
  12.7 0.7 copy-start.2
  15.7 5.5 %collective-permute-start.8 = (bf16[128,128]{1,0:T(8,128)(2,1)S(1)}, bf16[128,128]{1,0:T(8,128)(2,1)S(1)}, u32[]{:S(2)}, u32[]{:S(2)}) collective-permute-start(bf16[128,128]{1,0:T(8,128)(2,1)S(1)} %get-tuple-element.33.refs_4_), channel_id=1, source_target_pairs={{0,8},{1,9},{2,10},{3,11},{4,12},{5,13},{6,14},{7,15},{8,0},{9,1},... | collective-permute-start | bytes 98312 | tf_op jit(solution)/shard_map/ppermute | solution.py:379
  16.7 5.4 %collective-permute-start.9 = (bf16[128,128]{1,0:T(8,128)(2,1)S(1)}, bf16[128,128]{1,0:T(8,128)(2,1)S(1)}, u32[]{:S(2)}, u32[]{:S(2)}) collective-permute-start(bf16[128,128]{1,0:T(8,128)(2,1)S(1)} %get-tuple-element.33.refs_4_), channel_id=1, source_target_pairs={{0,16},{1,17},{2,18},{3,19},{4,20},{5,21},{6,22},{7,23},{8,24},{9,... | collective-permute-start | bytes 98312 | tf_op jit(solution)/shard_map/ppermute | solution.py:379
  21.3 5.1 %collective-permute-start.10 = (bf16[128,128]{1,0:T(8,128)(2,1)S(1)}, bf16[128,128]{1,0:T(8,128)(2,1)S(1)}, u32[]{:S(2)}, u32[]{:S(2)}) collective-permute-start(bf16[128,128]{1,0:T(8,128)(2,1)S(1)} %get-tuple-element.33.refs_4_), channel_id=1, source_target_pairs={{0,24},{1,25},{2,26},{3,27},{4,28},{5,29},{6,30},{7,31},{8,16},{9,... | collective-permute-start | bytes 98312 | tf_op jit(solution)/shard_map/ppermute | solution.py:379
  26.4 37.4 %collective-permute-start.11 = (bf16[512,128]{1,0:T(8,128)(2,1)S(1)}, bf16[512,128]{1,0:T(8,128)(2,1)S(1)}, u32[]{:S(2)}, u32[]{:S(2)}) collective-permute-start(bf16[512,128]{1,0:T(8,128)(2,1)S(1)} %constant_dynamic-update-slice_fusion), channel_id=1, source_target_pairs={{0,2},{1,3},{2,0},{3,1},{4,6},{5,7},{6,4},{7,5},{8,10},{9,11},{10,... | collective-permute-start | bytes 393224 | tf_op jit(solution)/shard_map/ppermute | solution.py:379
  26.4 37.4 %collective-permute-start.12 = (bf16[512,128]{1,0:T(8,128)(2,1)S(1)}, bf16[512,128]{1,0:T(8,128)(2,1)S(1)}, u32[]{:S(2)}, u32[]{:S(2)}) collective-permute-start(bf16[512,128]{1,0:T(8,128)(2,1)S(1)} %constant_dynamic-update-slice_fusion), channel_id=1, source_target_pairs={{0,4},{1,5},{2,6},{3,7},{4,0},{5,1},{6,2},{7,3},{8,12},{9,13},{10,... | collective-permute-start | bytes 393224 | tf_op jit(solution)/shard_map/ppermute | solution.py:379
  27.5 9.4 %collective-permute-start.5 = (bf16[1088,128]{1,0:T(8,128)(2,1)S(1)}, bf16[1088,128]{1,0:T(8,128)(2,1)S(1)}, u32[]{:S(2)}, u32[]{:S(2)}) collective-permute-start(bf16[1088,128]{1,0:T(8,128)(2,1)S(1)} %pad_maximum_fusion.refs_4_), channel_id=1, source_target_pairs={{0,2},{1,3},{2,0},{3,1},{4,6},{5,7},{6,4},{7,5},{8,10},{9,11},{10,... | collective-permute-start | bytes 835592 | tf_op jit(solution)/shard_map/ppermute | solution.py:379
  29.0 8.8 %collective-permute-start.6 = (bf16[1088,128]{1,0:T(8,128)(2,1)S(1)}, bf16[1088,128]{1,0:T(8,128)(2,1)S(1)}, u32[]{:S(2)}, u32[]{:S(2)}) collective-permute-start(bf16[1088,128]{1,0:T(8,128)(2,1)S(1)} %pad_maximum_fusion.refs_4_), channel_id=1, source_target_pairs={{0,4},{1,5},{2,6},{3,7},{4,0},{5,1},{6,2},{7,3},{8,12},{9,13},{10,... | collective-permute-start | bytes 835592 | tf_op jit(solution)/shard_map/ppermute | solution.py:379
  29.5 14.1 %collective-permute-start.7 = (bf16[1088,128]{1,0:T(8,128)(2,1)S(1)}, bf16[1088,128]{1,0:T(8,128)(2,1)S(1)}, u32[]{:S(2)}, u32[]{:S(2)}) collective-permute-start(bf16[1088,128]{1,0:T(8,128)(2,1)S(1)} %pad_maximum_fusion.refs_4_), channel_id=1, source_target_pairs={{0,6},{1,7},{2,4},{3,5},{4,2},{5,3},{6,0},{7,1},{8,14},{9,15},{10,... | collective-permute-start | bytes 835592 | tf_op jit(solution)/shard_map/ppermute | solution.py:379
  36.9 27.0 %collective-permute-start.13 = (bf16[512,128]{1,0:T(8,128)(2,1)S(1)}, bf16[512,128]{1,0:T(8,128)(2,1)S(1)}, u32[]{:S(2)}, u32[]{:S(2)}) collective-permute-start(bf16[512,128]{1,0:T(8,128)(2,1)S(1)} %constant_dynamic-update-slice_fusion), channel_id=1, source_target_pairs={{0,6},{1,7},{2,4},{3,5},{4,2},{5,3},{6,0},{7,1},{8,14},{9,15},{10,... | collective-permute-start | bytes 393224 | tf_op jit(solution)/shard_map/ppermute | solution.py:379
  43.6 20.3 %copy-start = (s32[1024]{0:T(1024)S(1)}, s32[1024]{0:T(1024)}, u32[]{:S(2)}) copy-start(s32[1024]{0:T(1024)} %param.15) | copy-start | bytes 12292
  63.9 8.1 %copy-start.3 = (f32[32,1024]{1,0:T(8,128)S(1)}, f32[32,1024]{1,0:T(8,128)}, u32[]{:S(2)}) copy-start(f32[32,1024]{1,0:T(8,128)} %refs_3_.1) | copy-start | bytes 393220
  66.2 5.7 %collective-permute-start.14 = (f32[32,1024]{1,0:T(8,128)S(1)}, f32[32,1024]{1,0:T(8,128)S(1)}, u32[]{:S(2)}, u32[]{:S(2)}) collective-permute-start(f32[32,1024]{1,0:T(8,128)S(1)} %get-tuple-element.35), channel_id=1, source_target_pairs={{0,1},{1,0},{2,3},{3,2},{4,5},{5,4},{6,7},{7,6},{8,9},{9,8},{10,11... | collective-permute-start | bytes 393224 | tf_op jit(solution)/shard_map/ppermute | solution.py:379

commit v4 on v3

--- a/solution.py
+++ b/solution.py
@@ -26,10 +26,6 @@
 
 def vmem():
     return pl.BlockSpec(memory_space=pltpu.VMEM)
-
-
-def smem():
-    return pl.BlockSpec(memory_space=pltpu.SMEM)
 
 
 def cost_of(count):
@@ -50,12 +46,12 @@
 
 
 def prepare_kernel(*refs, rows, layers, width):
-    count = 8
-    sources, results = refs[:count], refs[count:-5]
-    flux, pairs, cells, tile, sems = refs[-5:]
+    count = 10
+    sources, results = refs[:count], refs[count:-8]
+    raw, material, scale, flux, pairs, cells, tile, sems = refs[-8:]
     inner, outer, message, *held = results
     field, source, factor, pos, area = held
-    places = [field, source, factor, flux, pairs, cells, pos, area]
+    places = [field, source, raw, material, scale, flux, pairs, cells, pos, area]
     copies = [pltpu.make_async_copy(a, b, sems.at[i]) for i, (a, b) in enumerate(zip(sources, places))]
     for copy in copies:
         copy.start()
@@ -63,9 +59,16 @@
     loads, pan = flux.shape
     slots = pairs.shape[1]
     used = pan // lanes * loads
-    for copy in copies[:3]:
+    for copy in copies[:5]:
         copy.wait()
     lines = field.shape[0] // width
+    depth = lax.broadcasted_iota(jnp.int32, (layers, lanes), 0)
+    layer_scale = jnp.zeros((layers, lanes), F32)
+    for k in range(layers):
+        layer_scale = jnp.where(depth == k, scale[material[k]], layer_scale)
+    for x in range(width):
+        own = pl.ds(x, layers, stride=width)
+        factor[own, :] = layer_scale * raw[own, :]
     core = lax.rem(lax.axis_index("dev"), 2)
 
     def line(ref, x, count):
@@ -79,7 +82,7 @@
         out[2 * lines : 3 * lines, :] = line(source, edge, lines)
         tail = factor[pl.ds(edge, layers, stride=width), :]
         out[3 * lines : rows, :] = jnp.concatenate([tail, tail], axis=0).astype(BF16)
-    for copy in copies[3:]:
+    for copy in copies[5:]:
         copy.wait()
     tile[...] = jnp.full(tile.shape, -2.0, F32)
     tile[0:2, 0:slots] = pairs[...].astype(F32)
@@ -96,16 +99,12 @@
     message[used:, :] = slot_rows
 
 
-def relax_kernel(material, scale, field, source, factor, inner, outer, out, top, *, layers, width):
+def relax_kernel(field, source, conduct, inner, outer, out, top, *, layers, width):
     lines = field.shape[0] // width
     loads = lines // layers
     ny = field.shape[1]
-    depth = lax.broadcasted_iota(jnp.int32, (layers, ny), 0)
     lane = lax.broadcasted_iota(jnp.int32, (1, layers, ny), 2)
     level = lax.broadcasted_iota(jnp.int32, (1, layers, ny), 1)
-    layer_scale = jnp.zeros((layers, ny), F32)
-    for k in range(layers):
-        layer_scale = jnp.where(depth == k, scale[material[k]], layer_scale)
 
     def cube(value):
         return value.reshape(loads, layers, ny)
@@ -128,12 +127,11 @@
 
     fields = {-2: part(0, True), -1: part(1, True), width: part(0, False), width + 1: part(1, False)}
     sources = {-1: part(2, True), width: part(2, False)}
-    factors = {-1: tail(True), width: tail(False)}
+    conducts = {-1: tail(True)[None], width: tail(False)[None]}
     for x in range(width):
         fields[x] = own(field, x)
         sources[x] = own(source, x)
-        factors[x] = factor[pl.ds(x, layers, stride=width), :]
-    conducts = {x: (layer_scale * value)[None] for x, value in factors.items()}
+        conducts[x] = conduct[pl.ds(x, layers, stride=width), :][None]
     gains = {x: relax_rate / (6.0 * value + 1.0) for x, value in conducts.items()}
 
     def sweep(values, x):
@@ -265,7 +263,7 @@
     return value
 
 
-def near_kernel(*refs, first, masks, loads, pan, size):
+def near_kernel(*refs, masks, loads, pan, size):
     tables, (stack, out, kernel) = refs[:4], refs[4:]
     me = lax.axis_index("dev")
 
@@ -276,7 +274,7 @@
         def store(span, value):
             out[i, :, span] = value
 
-        start = pl.multiple_of((first + i) * size, 16)
+        start = pl.multiple_of(i * size, 16)
         add_block(tables, stack, start, block, kernel, store, loads=loads, pan=pan)
 
 
@@ -375,6 +373,11 @@
     return phases
 
 
+def phases_of(size):
+    first, *others = groups_of(size)
+    return [[mask] for mask in first[:2]] + others
+
+
 def swap(array, mask, size):
     return lax.ppermute(array, "dev", [(i, i ^ mask) for i in range(size)])
 
@@ -407,7 +410,7 @@
     blocks = size // 2
     lanes = 128
     lines = loads * layers
-    phases = groups_of(size)
+    phases = phases_of(size)
 
     cells = panel_cell.reshape(pan // lanes, lanes)
     halo_rows = 3 * lines + 2 * layers
@@ -417,6 +420,8 @@
         field_in.reshape(lines * width, ny),
         source.reshape(lines * width, ny),
         cell_factor.reshape(layers * width, ny),
+        layer_material,
+        material_scale,
         flux_in,
         pair_list.T,
         cells,
@@ -424,19 +429,22 @@
         panel_area.reshape(1, -1),
     )
     shapes = [jax.ShapeDtypeStruct(a.shape, a.dtype) for a in wanted]
-    inner, outer, message, field, load, factor, pos, area = call(
+    inner, outer, message, field, load, conduct, pos, area = call(
         lambda *refs: prepare_kernel(*refs, rows=halo_rows, layers=layers, width=width),
         [
             jax.ShapeDtypeStruct((inner_rows, ny), BF16),
             jax.ShapeDtypeStruct((halo_rows, ny), BF16),
             jax.ShapeDtypeStruct((message_rows, lanes), BF16),
             *shapes[:3],
-            *shapes[6:],
+            *shapes[8:],
         ],
         [pl.BlockSpec(memory_space=pltpu.HBM)] * len(wanted),
         scratch=[
+            pltpu.VMEM(shapes[2].shape, F32),
+            pltpu.SMEM(layer_material.shape, jnp.int32),
+            pltpu.SMEM(material_scale.shape, F32),
             pltpu.VMEM(flux_in.shape, F32),
-            pltpu.VMEM(shapes[4].shape, jnp.int32),
+            pltpu.VMEM(pair_list.shape[::-1], jnp.int32),
             pltpu.VMEM(cells.shape, jnp.int32),
             pltpu.VMEM((PAIR_ROWS, lanes), F32),
             pltpu.SemaphoreType.DMA((len(wanted),)),
@@ -452,9 +460,8 @@
         aliases={0: 0},
     )(message, inner)
     flux_parts = spread(message, phases, size)
-    near_count = 1 + len(phases[0])
+    near_count = 3
     near_parts, far_parts = flux_parts[:near_count], flux_parts[near_count:]
-    near_stack = jnp.concatenate([a for a, _ in near_parts], axis=0)
 
     *tables, gains = call(
         lambda *refs: feature_kernel(*refs, pan=pan, blocks=blocks),
@@ -475,18 +482,22 @@
             jax.ShapeDtypeStruct((lines * width, ny), F32),
             jax.ShapeDtypeStruct((width * loads, ny), BF16),
         ],
-        [smem()] * 2 + [vmem()] * 5,
-    )(layer_material, material_scale, field, load, factor, inner, outer)
+        [vmem()] * 5,
+    )(field, load, conduct, inner, outer)
     top_parts = spread(top, phases, size)
 
     wide = jax.ShapeDtypeStruct((loads, 2 * pan), F32)
     strip = pltpu.VMEM((pan, 2 * pan), BF16)
-    near_masks = [masks[0] for _, masks in near_parts]
+    near_masks = [mask for _, masks in near_parts for mask in masks]
     nears = []
-    for first, masks, stack in ((0, near_masks[:1], message), (1, near_masks[1:], near_stack)):
+    for masks, stack in (
+        (near_masks[:1], message),
+        (near_masks[1:2], near_parts[1][0]),
+        (near_masks[2:], near_parts[2][0]),
+    ):
         (near,) = call(
-            lambda *refs, first=first, masks=masks: near_kernel(
-                *refs, first=first, masks=masks, loads=loads, pan=pan, size=message_rows
+            lambda *refs, masks=masks: near_kernel(
+                *refs, masks=masks, loads=loads, pan=pan, size=message_rows
             ),
             [jax.ShapeDtypeStruct((len(masks), loads, 2 * pan), F32)],
             [vmem()] * 5,
@@ -508,7 +519,7 @@
         [wide],
         [vmem()] * (4 + len(nears) + len(flux_parts)),
         scratch=[pltpu.SMEM(((blocks + 15) // 16,), jnp.int32), strip],
-        cost=cost_of(blocks - near_count),
+        cost=cost_of(blocks - len(near_masks)),
     )(*tables, *nears, *[a for a, _ in flux_parts])
 
     half = jax.ShapeDtypeStruct((loads, pan), F32)

time: 72.8 us -> 71.8 us (0.986)
  waiting for transfers between devices: 13.4 us -> 16.8 us
  starting transfers between devices: 21.3 us -> 18.1 us
    ppermute x14 -> x12, starting transfers between devices: 18.3 us -> 15.1 us  [swap(): return lax.ppermute(array, 'dev', [(i, i ^ mask) for i in range(size)])]
    ppermute x1, waiting for transfers between devices: 1.31 us -> 3.41 us  [program(): outer = lax.ppermute(outer, 'dev', sides + [(j, i) for i, j in sides])]
    ppermute x14 -> x12, waiting for transfers between devices: 12 us -> 13.4 us  [swap(): return lax.ppermute(array, 'dev', [(i, i ^ mask) for i in range(size)])]
    pallas_call x2 -> x3, Pallas kernels: 7.65 us -> 7.6 us  [program(): call(lambda *refs, masks=masks: near_kernel(*refs, masks=masks, loads=loa...]
  transfers between devices with their start and end apart: 15 -> 13, of which waited for: 5 -> 6; matrix products, arithmetic and copies ran while one was open for 0% -> 0% of each run, Pallas kernels for 44% -> 44%
where the time goes in v4:
time: 71.8 us; the launch traced here: 71.7 us
  Pallas kernels  35.3 us (49%)
  starting transfers between devices  18.1 us (25%)
  waiting for transfers between devices  16.8 us (23%)
  between operations  0.78 us (1%)
  other arithmetic  0.72 us (1%)
    pallas_call x1, Pallas kernels, program(): call(lambda *refs: far_kernel(*refs, near_masks=near_masks, near_count=le...  20.3 us
    ppermute x12, starting transfers between devices, swap(): return lax.ppermute(array, 'dev', [(i, i ^ mask) for i in range(size)])  15.1 us
    ppermute x12, waiting for transfers between devices, swap(): return lax.ppermute(array, 'dev', [(i, i ^ mask) for i in range(size)])  13.4 us
    pallas_call x3, Pallas kernels, program(): call(lambda *refs, masks=masks: near_kernel(*refs, masks=masks, loads=loa...  7.6 us
    ppermute x1, waiting for transfers between devices, program(): outer = lax.ppermute(outer, 'dev', sides + [(j, i) for i, j in sides])  3.41 us
    ppermute x1, starting transfers between devices, program(): outer = lax.ppermute(outer, 'dev', sides + [(j, i) for i, j in sides])  3.02 us
    pallas_call x1, Pallas kernels, program(): call(lambda *refs: trace_kernel(*refs, groups=[masks for _, masks in top_...  2.33 us
    pallas_call x1, Pallas kernels, program(): call(lambda *refs: relax_kernel(*refs, layers=layers, width=width), [jax....  1.83 us
  transfers between devices with their start and end apart: 13, of which 6 were waited for; matrix products, arithmetic and copies ran while one was open for 0% of the time, Pallas kernels for 44%

profile of v4, /device:TPU:3, one launch (start us, length us, event | category | flops | bytes accessed | tf_op | source)
XLA Modules:
  0.0 71.7 jit_solution(13463388556239571427)
XLA Ops:
  0.6 1.6 %shard_map.113 = (bf16[816,128]{1,0:T(8,128)(2,1)S(1)}, bf16[784,128]{1,0:T(8,128)(2,1)S(1)}, bf16[272,128]{1,0:T(8,128)(2,1)S(1)}, f32[1024,128]{1,0:T(8,128)S(...) custom-call(f32[1024,128]{1,0:T(8,128)} %bitcast.9, ...), custom_call_target="tpu_custom_call" | custom-call | tf_op jit(solution)/shard_map/pallas_call | solution.py:432
  2.2 0.7 %collective-permute-start = (bf16[816,128]{1,0:T(8,128)(2,1)S(1)}, bf16[816,128]{1,0:T(8,128)(2,1)S(1)}, u32[]{:S(2)}, u32[]{:S(2)}) collective-permute-start(bf16[816,128]{1,0:T(8,128)(2,1)S(1)} %get-tuple-element.22), channel_id=1, source_target_pairs={{0,1},{1,0},{2,3},{3,2},{4,5},{5,4},{6,7},{7,6},{8,9},{9,8},{10,11... | collective-permute-start | bytes 626696 | tf_op jit(solution)/shard_map/ppermute | solution.py:382
  3.0 3.0 %collective-permute-start.1 = (bf16[784,128]{1,0:T(8,128)(2,1)S(1)}, bf16[784,128]{1,0:T(8,128)(2,1)S(1)}, u32[]{:S(2)}, u32[]{:S(2)}) collective-permute-start(bf16[784,128]{1,0:T(8,128)(2,1)S(1)} %get-tuple-element.23), channel_id=1, source_target_pairs={{1,2},{3,4},{5,6},{7,8},{9,10},{11,12},{13,14},{15,16},{17,18},{19... | collective-permute-start | bytes 602120 | tf_op jit(solution)/shard_map/ppermute | solution.py:455
  6.0 1.6 %shard_map.115 = (bf16[512,1024]{1,0:T(8,128)(2,1)S(1)}, f32[128,1024]{1,0:T(8,128)S(1)}, bf16[32,2048]{1,0:T(8,128)(2,1)S(1)}, f32[8,2048]{1,0:T(8,128)S(1)}, f32[1,2048]{1,0:T(1,128)S(1)}) custom-call(f32[3,32768]{1,0:T(4,128)S(1)} %get-tuple-element.25.refs_0_, f32[1,32768]{1,0:T(1,128)S(1)} %get-tuple-element.26.refs_1_), custom_call_target="tpu_custom_call" | custom-call | tf_op jit(solution)/shard_map/pallas_call | solution.py:466
  7.7 1.4 %collective-permute-start.2 = (bf16[272,128]{1,0:T(8,128)(2,1)S(1)}, bf16[272,128]{1,0:T(8,128)(2,1)S(1)}, u32[]{:S(2)}, u32[]{:S(2)}) collective-permute-start(bf16[272,128]{1,0:T(8,128)(2,1)S(1)} %shard_map.116.refs_4_.refs_7_), channel_id=1, source_target_pairs={{0,8},{1,9},{2,10},{3,11},{4,12},{5,13},{6,14},{7,15},{8,0},{9,1},... | collective-permute-start | bytes 208904 | tf_op jit(solution)/shard_map/ppermute | solution.py:382
  9.0 3.4 %collective-permute-done.1.refs_4_ = bf16[784,128]{1,0:T(8,128)(2,1)S(1)} collective-permute-done((bf16[784,128]{1,0:T(8,128)(2,1)S(1)}, bf16[784,128]{1,0:T(8,128)(2,1)S(1)}, u32[]{:S(2)}, u32[]{:S(2)}) %collective-permute-start.1) | collective-permute-done | bytes 200736 | tf_op jit(solution)/shard_map/ppermute | solution.py:455
  12.4 1.8 %shard_map.114 = (f32[1024,128]{1,0:T(8,128)}, bf16[128,128]{1,0:T(8,128)(2,1)S(1)}) custom-call(f32[1024,128]{1,0:T(8,128)S(1)} %get-tuple-element.19.refs_0_, f32[1024,128]{1,0:T(8,128)S(1)} %get-tuple-element.20.refs_1_, f32[32,128]{1,0:T(8,128)S(1)} %get-tuple-element.21.refs_2_, bf16[816,128]{1,0:T(8,128)(2,1)S(1)} %collective-permute-done.refs_3_.refs_1_, ...), custom_call_target="tpu_custom_call" | custom-call | tf_op jit(solution)/shard_map/pallas_call | solution.py:479
  14.2 1.3 %collective-permute-start.7 = (bf16[128,128]{1,0:T(8,128)(2,1)S(1)}, bf16[128,128]{1,0:T(8,128)(2,1)S(1)}, u32[]{:S(2)}, u32[]{:S(2)}) collective-permute-start(bf16[128,128]{1,0:T(8,128)(2,1)S(1)} %get-tuple-element.33.refs_4_), channel_id=1, source_target_pairs={{0,8},{1,9},{2,10},{3,11},{4,12},{5,13},{6,14},{7,15},{8,0},{9,1},... | collective-permute-start | bytes 98312 | tf_op jit(solution)/shard_map/ppermute | solution.py:382
  15.5 1.9 %shard_map.117.refs_4_ = f32[1,32,2048]{2,1,0:T(8,128)S(1)} custom-call(bf16[512,1024]{1,0:T(8,128)(2,1)S(1)} %get-tuple-element.27.refs_0_, f32[128,1024]{1,0:T(8,128)S(1)} %get-tuple-element.28.refs_1_, bf16[32,2048]{1,0:T(8,128)(2,1)S(1)} %get-tuple-element.29.refs_2_, f32[8,2048]{1,0:T(8,128)S(1)} %get-tuple-element.30.refs_3_, ...), custom_call_target="tpu_custom_call" | custom-call | flops 2500000000 | bytes 131072 | tf_op jit(solution)/shard_map/pallas_call | solution.py:498
  17.5 2.4 %collective-permute-start.8 = (bf16[256,128]{1,0:T(8,128)(2,1)S(1)}, bf16[256,128]{1,0:T(8,128)(2,1)S(1)}, u32[]{:S(2)}, u32[]{:S(2)}) collective-permute-start(bf16[256,128]{1,0:T(8,128)(2,1)S(1)} %pad_maximum_fusion.2), channel_id=1, source_target_pairs={{0,16},{1,17},{2,18},{3,19},{4,20},{5,21},{6,22},{7,23},{8,24},{9,... | collective-permute-start | bytes 196616 | tf_op jit(solution)/shard_map/ppermute | solution.py:382
  20.0 1.9 %shard_map.118.refs_5_ = f32[1,32,2048]{2,1,0:T(8,128)S(1)} custom-call(bf16[512,1024]{1,0:T(8,128)(2,1)S(1)} %get-tuple-element.27.refs_0_, f32[128,1024]{1,0:T(8,128)S(1)} %get-tuple-element.28.refs_1_, bf16[32,2048]{1,0:T(8,128)(2,1)S(1)} %get-tuple-element.29.refs_2_, f32[8,2048]{1,0:T(8,128)S(1)} %get-tuple-element.30.refs_3_, ...), custom_call_target="tpu_custom_call" | custom-call | flops 2500000000 | bytes 131072 | tf_op jit(solution)/shard_map/pallas_call | solution.py:498
  21.9 1.5 %collective-permute-done.8.refs_6_ = bf16[256,128]{1,0:T(8,128)(2,1)S(1)} collective-permute-done((bf16[256,128]{1,0:T(8,128)(2,1)S(1)}, bf16[256,128]{1,0:T(8,128)(2,1)S(1)}, u32[]{:S(2)}, u32[]{:S(2)}) %collective-permute-start.8) | collective-permute-done | bytes 65568 | tf_op jit(solution)/shard_map/ppermute | solution.py:382
  24.2 4.7 %collective-permute-done.3.refs_4_.refs_9_ = bf16[544,128]{1,0:T(8,128)(2,1)S(1)} collective-permute-done((bf16[544,128]{1,0:T(8,128)(2,1)S(1)}, bf16[544,128]{1,0:T(8,128)(2,1)S(1)}, u32[]{:S(2)}, u32[]{:S(2)}) %collective-permute-start.3) | collective-permute-done | bytes 139296 | tf_op jit(solution)/shard_map/ppermute | solution.py:382
  29.0 0.7 collective-permute-start.4
  29.6 1.9 %collective-permute-start.5 = (bf16[1088,128]{1,0:T(8,128)(2,1)S(1)}, bf16[1088,128]{1,0:T(8,128)(2,1)S(1)}, u32[]{:S(2)}, u32[]{:S(2)}) collective-permute-start(bf16[1088,128]{1,0:T(8,128)(2,1)S(1)} %pad_maximum_fusion), channel_id=1, source_target_pairs={{0,4},{1,5},{2,6},{3,7},{4,0},{5,1},{6,2},{7,3},{8,12},{9,13},{10,... | collective-permute-start | bytes 835592 | tf_op jit(solution)/shard_map/ppermute | solution.py:382
  31.7 3.8 %shard_map.119.refs_6_ = f32[2,32,2048]{2,1,0:T(8,128)S(1)} custom-call(bf16[512,1024]{1,0:T(8,128)(2,1)S(1)} %get-tuple-element.27.refs_0_, f32[128,1024]{1,0:T(8,128)S(1)} %get-tuple-element.28.refs_1_, bf16[32,2048]{1,0:T(8,128)(2,1)S(1)} %get-tuple-element.29.refs_2_, f32[8,2048]{1,0:T(8,128)S(1)} %get-tuple-element.30.refs_3_, ...), custom_call_target="tpu_custom_call" | custom-call | flops 5000000000 | bytes 262144 | tf_op jit(solution)/shard_map/pallas_call | solution.py:498
  35.5 1.4 %collective-permute-done.4.refs_10_ = bf16[1088,128]{1,0:T(8,128)(2,1)S(1)} collective-permute-done((bf16[1088,128]{1,0:T(8,128)(2,1)S(1)}, bf16[1088,128]{1,0:T(8,128)(2,1)S(1)}, u32[]{:S(2)}, u32[]{:S(2)}) %collective-permute-start.4) | collective-permute-done | bytes 278560 | tf_op jit(solution)/shard_map/ppermute | solution.py:382
  36.9 2.1 %collective-permute-start.11 = (bf16[512,128]{1,0:T(8,128)(2,1)S(1)}, bf16[512,128]{1,0:T(8,128)(2,1)S(1)}, u32[]{:S(2)}, u32[]{:S(2)}) collective-permute-start(bf16[512,128]{1,0:T(8,128)(2,1)S(1)} %constant_dynamic-update-slice_fusion), channel_id=1, source_target_pairs={{0,6},{1,7},{2,4},{3,5},{4,2},{5,3},{6,0},{7,1},{8,14},{9,15},{10,... | collective-permute-start | bytes 393224 | tf_op jit(solution)/shard_map/ppermute | solution.py:382
  39.0 4.7 %collective-permute-done.6.refs_12_ = bf16[1088,128]{1,0:T(8,128)(2,1)S(1)} collective-permute-done((bf16[1088,128]{1,0:T(8,128)(2,1)S(1)}, bf16[1088,128]{1,0:T(8,128)(2,1)S(1)}, u32[]{:S(2)}, u32[]{:S(2)}) %collective-permute-start.6) | collective-permute-done | bytes 278560 | tf_op jit(solution)/shard_map/ppermute | solution.py:382
  43.7 20.3 %shard_map.120.refs_0_ = f32[32,2048]{1,0:T(8,128)S(1)} custom-call(bf16[512,1024]{1,0:T(8,128)(2,1)S(1)} %get-tuple-element.27.refs_0_, f32[128,1024]{1,0:T(8,128)S(1)} %get-tuple-element.28.refs_1_, bf16[32,2048]{1,0:T(8,128)(2,1)S(1)} %get-tuple-element.29.refs_2_, f32[8,2048]{1,0:T(8,128)S(1)} %get-tuple-element.30.refs_3_, ...), custom_call_target="tpu_custom_call" | custom-call | flops 30000001024 | bytes 1572864 | tf_op jit(solution)/shard_map/pallas_call | solution.py:508
  64.0 2.3 %shard_map.121 = (f32[32,1024]{1,0:T(8,128)S(1)}, f32[32,1024]{1,0:T(8,128)S(1)}) custom-call(f32[32,2048]{1,0:T(8,128)S(1)} %shard_map.120.refs_0_, f32[1,2048]{1,0:T(1,128)S(1)} %get-tuple-element.32.refs_1_, s32[8,128]{1,0:T(8,128)S(1)} %bitcast.8, bf16[816,128]{1,0:T(8,128)(2,1)S(1)} %collective-permute-done.refs_3_.refs_1_, ...), custom_call_target="tpu_custom_call" | custom-call | tf_op jit(solution)/shard_map/pallas_call | solution.py:526
  66.4 3.7 %collective-permute-start.12 = (f32[32,1024]{1,0:T(8,128)S(1)}, f32[32,1024]{1,0:T(8,128)S(1)}, u32[]{:S(2)}, u32[]{:S(2)}) collective-permute-start(f32[32,1024]{1,0:T(8,128)S(1)} %get-tuple-element.35), channel_id=1, source_target_pairs={{0,1},{1,0},{2,3},{3,2},{4,5},{5,4},{6,7},{7,6},{8,9},{9,8},{10,11... | collective-permute-start | bytes 393224 | tf_op jit(solution)/shard_map/ppermute | solution.py:382
  70.0 1.0 %collective-permute-done.12 = f32[32,1024]{1,0:T(8,128)S(1)} collective-permute-done((f32[32,1024]{1,0:T(8,128)S(1)}, f32[32,1024]{1,0:T(8,128)S(1)}, u32[]{:S(2)}, u32[]{:S(2)}) %collective-permute-start.12) | collective-permute-done | bytes 131104 | tf_op jit(solution)/shard_map/ppermute | solution.py:382
  71.0 0.7 add_add_fusion
  (22 shorter events, 1.1 us)
Async XLA Ops:
  2.2 5.4 %collective-permute-start = (bf16[816,128]{1,0:T(8,128)(2,1)S(1)}, bf16[816,128]{1,0:T(8,128)(2,1)S(1)}, u32[]{:S(2)}, u32[]{:S(2)}) collective-permute-start(bf16[816,128]{1,0:T(8,128)(2,1)S(1)} %get-tuple-element.22), channel_id=1, source_target_pairs={{0,1},{1,0},{2,3},{3,2},{4,5},{5,4},{6,7},{7,6},{8,9},{9,8},{10,11... | collective-permute-start | bytes 626696 | tf_op jit(solution)/shard_map/ppermute | solution.py:382
  3.0 9.5 %collective-permute-start.1 = (bf16[784,128]{1,0:T(8,128)(2,1)S(1)}, bf16[784,128]{1,0:T(8,128)(2,1)S(1)}, u32[]{:S(2)}, u32[]{:S(2)}) collective-permute-start(bf16[784,128]{1,0:T(8,128)(2,1)S(1)} %get-tuple-element.23), channel_id=1, source_target_pairs={{1,2},{3,4},{5,6},{7,8},{9,10},{11,12},{13,14},{15,16},{17,18},{19... | collective-permute-start | bytes 602120 | tf_op jit(solution)/shard_map/ppermute | solution.py:455
  7.7 12.2 %collective-permute-start.2 = (bf16[272,128]{1,0:T(8,128)(2,1)S(1)}, bf16[272,128]{1,0:T(8,128)(2,1)S(1)}, u32[]{:S(2)}, u32[]{:S(2)}) collective-permute-start(bf16[272,128]{1,0:T(8,128)(2,1)S(1)} %shard_map.116.refs_4_.refs_7_), channel_id=1, source_target_pairs={{0,8},{1,9},{2,10},{3,11},{4,12},{5,13},{6,14},{7,15},{8,0},{9,1},... | collective-permute-start | bytes 208904 | tf_op jit(solution)/shard_map/ppermute | solution.py:382
  14.2 3.2 %collective-permute-start.7 = (bf16[128,128]{1,0:T(8,128)(2,1)S(1)}, bf16[128,128]{1,0:T(8,128)(2,1)S(1)}, u32[]{:S(2)}, u32[]{:S(2)}) collective-permute-start(bf16[128,128]{1,0:T(8,128)(2,1)S(1)} %get-tuple-element.33.refs_4_), channel_id=1, source_target_pairs={{0,8},{1,9},{2,10},{3,11},{4,12},{5,13},{6,14},{7,15},{8,0},{9,1},... | collective-permute-start | bytes 98312 | tf_op jit(solution)/shard_map/ppermute | solution.py:382
  17.5 6.0 %collective-permute-start.8 = (bf16[256,128]{1,0:T(8,128)(2,1)S(1)}, bf16[256,128]{1,0:T(8,128)(2,1)S(1)}, u32[]{:S(2)}, u32[]{:S(2)}) collective-permute-start(bf16[256,128]{1,0:T(8,128)(2,1)S(1)} %pad_maximum_fusion.2), channel_id=1, source_target_pairs={{0,16},{1,17},{2,18},{3,19},{4,20},{5,21},{6,22},{7,23},{8,24},{9,... | collective-permute-start | bytes 196616 | tf_op jit(solution)/shard_map/ppermute | solution.py:382
  19.9 9.0 %collective-permute-start.3 = (bf16[544,128]{1,0:T(8,128)(2,1)S(1)}, bf16[544,128]{1,0:T(8,128)(2,1)S(1)}, u32[]{:S(2)}, u32[]{:S(2)}) collective-permute-start(bf16[544,128]{1,0:T(8,128)(2,1)S(1)} %pad_maximum_fusion.1), channel_id=1, source_target_pairs={{0,16},{1,17},{2,18},{3,19},{4,20},{5,21},{6,22},{7,23},{8,24},{9,... | collective-permute-start | bytes 417800 | tf_op jit(solution)/shard_map/ppermute | solution.py:382
  23.5 40.5 %collective-permute-start.9 = (bf16[512,128]{1,0:T(8,128)(2,1)S(1)}, bf16[512,128]{1,0:T(8,128)(2,1)S(1)}, u32[]{:S(2)}, u32[]{:S(2)}) collective-permute-start(bf16[512,128]{1,0:T(8,128)(2,1)S(1)} %constant_dynamic-update-slice_fusion), channel_id=1, source_target_pairs={{0,2},{1,3},{2,0},{3,1},{4,6},{5,7},{6,4},{7,5},{8,10},{9,11},{10,... | collective-permute-start | bytes 393224 | tf_op jit(solution)/shard_map/ppermute | solution.py:382
  23.6 40.4 %collective-permute-start.10 = (bf16[512,128]{1,0:T(8,128)(2,1)S(1)}, bf16[512,128]{1,0:T(8,128)(2,1)S(1)}, u32[]{:S(2)}, u32[]{:S(2)}) collective-permute-start(bf16[512,128]{1,0:T(8,128)(2,1)S(1)} %constant_dynamic-update-slice_fusion), channel_id=1, source_target_pairs={{0,4},{1,5},{2,6},{3,7},{4,0},{5,1},{6,2},{7,3},{8,12},{9,13},{10,... | collective-permute-start | bytes 393224 | tf_op jit(solution)/shard_map/ppermute | solution.py:382
  29.0 7.9 %collective-permute-start.4 = (bf16[1088,128]{1,0:T(8,128)(2,1)S(1)}, bf16[1088,128]{1,0:T(8,128)(2,1)S(1)}, u32[]{:S(2)}, u32[]{:S(2)}) collective-permute-start(bf16[1088,128]{1,0:T(8,128)(2,1)S(1)} %pad_maximum_fusion), channel_id=1, source_target_pairs={{0,2},{1,3},{2,0},{3,1},{4,6},{5,7},{6,4},{7,5},{8,10},{9,11},{10,... | collective-permute-start | bytes 835592 | tf_op jit(solution)/shard_map/ppermute | solution.py:382
  29.6 9.3 %collective-permute-start.5 = (bf16[1088,128]{1,0:T(8,128)(2,1)S(1)}, bf16[1088,128]{1,0:T(8,128)(2,1)S(1)}, u32[]{:S(2)}, u32[]{:S(2)}) collective-permute-start(bf16[1088,128]{1,0:T(8,128)(2,1)S(1)} %pad_maximum_fusion), channel_id=1, source_target_pairs={{0,4},{1,5},{2,6},{3,7},{4,0},{5,1},{6,2},{7,3},{8,12},{9,13},{10,... | collective-permute-start | bytes 835592 | tf_op jit(solution)/shard_map/ppermute | solution.py:382
  31.6 12.1 %collective-permute-start.6 = (bf16[1088,128]{1,0:T(8,128)(2,1)S(1)}, bf16[1088,128]{1,0:T(8,128)(2,1)S(1)}, u32[]{:S(2)}, u32[]{:S(2)}) collective-permute-start(bf16[1088,128]{1,0:T(8,128)(2,1)S(1)} %pad_maximum_fusion), channel_id=1, source_target_pairs={{0,6},{1,7},{2,4},{3,5},{4,2},{5,3},{6,0},{7,1},{8,14},{9,15},{10,... | collective-permute-start | bytes 835592 | tf_op jit(solution)/shard_map/ppermute | solution.py:382
  36.9 27.1 %collective-permute-start.11 = (bf16[512,128]{1,0:T(8,128)(2,1)S(1)}, bf16[512,128]{1,0:T(8,128)(2,1)S(1)}, u32[]{:S(2)}, u32[]{:S(2)}) collective-permute-start(bf16[512,128]{1,0:T(8,128)(2,1)S(1)} %constant_dynamic-update-slice_fusion), channel_id=1, source_target_pairs={{0,6},{1,7},{2,4},{3,5},{4,2},{5,3},{6,0},{7,1},{8,14},{9,15},{10,... | collective-permute-start | bytes 393224 | tf_op jit(solution)/shard_map/ppermute | solution.py:382
  43.7 20.3 %copy-start = (s32[1024]{0:T(1024)S(1)}, s32[1024]{0:T(1024)}, u32[]{:S(2)}) copy-start(s32[1024]{0:T(1024)} %param.15) | copy-start | bytes 12292
  64.0 7.0 %copy-start.1 = (f32[32,1024]{1,0:T(8,128)S(1)}, f32[32,1024]{1,0:T(8,128)}, u32[]{:S(2)}) copy-start(f32[32,1024]{1,0:T(8,128)} %refs_5_.1) | copy-start | bytes 393220
  66.4 4.6 %collective-permute-start.12 = (f32[32,1024]{1,0:T(8,128)S(1)}, f32[32,1024]{1,0:T(8,128)S(1)}, u32[]{:S(2)}, u32[]{:S(2)}) collective-permute-start(f32[32,1024]{1,0:T(8,128)S(1)} %get-tuple-element.35), channel_id=1, source_target_pairs={{0,1},{1,0},{2,3},{3,2},{4,5},{5,4},{6,7},{7,6},{8,9},{9,8},{10,11... | collective-permute-start | bytes 393224 | tf_op jit(solution)/shard_map/ppermute | solution.py:382
